TPU v7x, 256 devices: a whole 4x4x8 slice. The times are simulated.
256 devices in a mesh: gx: 16 (over z, x_hi), gy: 16 (over x_lo, y, core).
Axes of the slice: x: 4 (x_hi: 2, x_lo: 2; x = x_hi * 2 + x_lo), y: 4, z: 8, core: 2. Of those that a mesh axis runs over, the one named last changes fastest.
Arguments:
- fine_e: float32 [3, 16, 96, 6144], P(None, None, 'gx', 'gy'), may hold values from -6 to 6
- fine_h: float32 [3, 16, 96, 6144], P(None, None, 'gx', 'gy'), may hold values from -6 to 6
- drude_current: float32 [3, 16, 96, 6144], P(None, None, 'gx', 'gy'), may hold values from -4 to 4
- lorentz_pol: float32 [3, 16, 96, 6144], P(None, None, 'gx', 'gy'), may hold values from -4 to 4
- lorentz_rate: float32 [3, 16, 96, 6144], P(None, None, 'gx', 'gy'), may hold values from -4 to 4
- material: int32 [16, 96, 6144], P(None, 'gx', 'gy'), may hold values from 0 to 7
- permittivity: float32 [8], replicated, may hold values from 1 to 4
- plasma: float32 [8], replicated, may hold values from 0.2 to 1.5
- damping: float32 [8], replicated, may hold values from 0.05 to 1
- strength: float32 [8], replicated, may hold values from 0.5 to 4
- resonance: float32 [8], replicated, may hold values from 0.3 to 1.2
- linewidth: float32 [8], replicated, may hold values from 0.05 to 0.5
- coarse_e: float32 [3, 16, 32, 2048], P(None, None, 'gx', 'gy'), may hold values from -6 to 6
- coarse_h: float32 [3, 16, 32, 2048], P(None, None, 'gx', 'gy'), may hold values from -6 to 6
- coarse_material: int32 [16, 32, 2048], P(None, 'gx', 'gy'), may hold values from 0 to 7
- coarse_prior: float32 [2, 32, 2048], P(None, 'gx', 'gy'), may hold values from -6 to 6
Outputs:
- fine_e_out: float32 [3, 16, 96, 6144], P(None, None, 'gx', 'gy')
- fine_h_out: float32 [3, 16, 96, 6144], P(None, None, 'gx', 'gy')
- current_out: float32 [3, 16, 96, 6144], P(None, None, 'gx', 'gy')
- pol_out: float32 [3, 16, 96, 6144], P(None, None, 'gx', 'gy')
- rate_out: float32 [3, 16, 96, 6144], P(None, None, 'gx', 'gy')
- coarse_e_out: float32 [3, 16, 32, 2048], P(None, None, 'gx', 'gy')
- coarse_h_out: float32 [3, 16, 32, 2048], P(None, None, 'gx', 'gy')
All inputs are finite; a program needn't handle non-finite values.
Results may differ from a plain program's by a relative error of at most 0.0001.
Values sent between devices are 32-bit elements; how exact they have to be, the bound alone decides.
No kernel may reach another device: no remote copies, remote signals or barrier semaphores. Data moves between devices by JAX's collectives and lax.ppermute only.
A program may use at most 128 MiB of HBM per device.

v0:
```python
import functools

import jax
import jax.numpy as jnp
from jax import lax
from jax.experimental import pallas as pl
from jax.experimental.pallas import tpu as pltpu
from jax.sharding import PartitionSpec as P

RATIO = 3
STEPS = 3
COURANT = 0.5
TIMESTEP = 0.5

Z = 16
ROWS = 6
OWN = 384
W = 256
CROWS = 2
CW = 128
GHOST = 9
CGHOST = 3
TILES = ((0, 1), (1, 2))
F32 = jnp.float32


def rolled(value, shift, axis):
    shift %= value.shape[axis]
    return value if shift == 0 else pltpu.roll(value, shift, axis)


def lanes(shape):
    return lax.broadcasted_iota(jnp.int32, shape, len(shape) - 1)


def right(value):
    return rolled(value, -1, 1)


def left(value):
    return rolled(value, 1, 1)


def above(value, top):
    sublane = lax.broadcasted_iota(jnp.int32, value.shape, 0)
    return jnp.where(sublane == Z - 1, top, rolled(value, -1, 0))


def below(value, bottom):
    sublane = lax.broadcasted_iota(jnp.int32, value.shape, 0)
    return jnp.where(sublane == 0, bottom, rolled(value, 1, 0))


def minus(first, second):
    if first is None:
        return None if second is None else -second
    return first if second is None else first - second


def h_row(h, e, following, top, wanted=(0, 1, 2)):
    ex, ey, ez = e
    next_y, next_z = following
    out = [None, None, None]
    if 0 in wanted:
        out[0] = h[0] - COURANT * ((right(ez) - ez) - (above(ey, top[1]) - ey))
    if 1 in wanted:
        out[1] = h[1] - COURANT * ((above(ex, top[0]) - ex) - minus(next_z, ez))
    if 2 in wanted:
        out[2] = h[2] - COURANT * (minus(next_y, ey) - (right(ex) - ex))
    return out


def curl_h(h, preceding, bottom, wanted=(0, 1, 2)):
    hx, hy, hz = h
    prev_y, prev_z = preceding
    out = [None, None, None]
    if 0 in wanted:
        out[0] = (hz - left(hz)) - (hy - below(hy, bottom[1]))
    if 1 in wanted:
        out[1] = (hx - below(hx, bottom[0])) - minus(hz, prev_z)
    if 2 in wanted:
        out[2] = minus(hy, prev_y) - (hx - left(hx))
    return out


def e_row(e, h, preceding, j, p, v, c, wanted=(0, 1, 2)):
    curl = curl_h(h, preceding, (0.0, 0.0), wanted)
    e2, j2, p2, v2 = [None] * 3, [None] * 3, [None] * 3, [None] * 3
    for k in wanted:
        v2[k] = c[3] * v[k] + c[4] * (c[5] * e[k] - p[k])
        j2[k] = c[1] * j[k] + c[2] * e[k]
        p2[k] = p[k] + TIMESTEP * v2[k]
        e2[k] = e[k] + c[0] * (curl[k] - j2[k] - v2[k])
    return e2, j2, p2, v2


def y_slots():
    entries = [("f", a, k, x, GHOST) for a in range(5) for k in range(3) for x in range(ROWS)]
    entries += [("m", 0, 0, x, GHOST) for x in range(ROWS)]
    entries += [("c", a, k, r, CGHOST) for a in range(2) for k in range(3) for r in range(CROWS)]
    entries += [("cm", 0, 0, r, CGHOST) for r in range(CROWS)]
    entries += [("prior", 0, 0, 0, CGHOST)]
    slots, plane, offset = {}, 0, 0
    for *key, width in entries:
        if offset + width > 128:
            plane, offset = plane + 1, 0
        slots[tuple(key)] = (plane, offset, width)
        offset += width
    return slots, plane + 1


Y_SLOTS, Y_PLANES = y_slots()


def coarse_row(ref, k, r):
    return ref[k, pl.ds(r, Z, stride=CROWS), :]


def pack_y_kernel(*refs):
    fields, (material, ce_in, ch_in, cmat_in, prior_in) = refs[0:5], refs[5:10]
    to_left, to_right, ce, ch, cmat, prior = refs[10:16]
    firsts, lasts, mats, sems = refs[16:20]
    pairs = []
    for a in range(5):
        pairs.append((fields[a].at[:, :, :, 0:128], firsts.at[a]))
        pairs.append((fields[a].at[:, :, :, OWN - 128 : OWN], lasts.at[a]))
    pairs.append((material.at[:, :, 0:128], mats.at[0]))
    pairs.append((material.at[:, :, OWN - 128 : OWN], mats.at[1]))
    pairs += [(ce_in, ce), (ch_in, ch), (cmat_in, cmat), (prior_in, prior)]
    copies = [pltpu.make_async_copy(src, dst, sems.at[i]) for i, (src, dst) in enumerate(pairs)]
    for copy in copies:
        copy.start()
    for copy in copies:
        copy.wait()
    lane = lanes((Z, 128))
    built = {}
    for key, (plane, offset, width) in Y_SLOTS.items():
        kind, a, k, x = key
        if kind == "f":
            first, last = firsts[a, k, x], lasts[a, k, x]
        elif kind == "m":
            first, last = mats[0, x].astype(F32), mats[1, x].astype(F32)
        elif kind == "c":
            first = last = coarse_row((ce, ch)[a], k, x)
        elif kind == "cm":
            first = last = cmat[pl.ds(x, Z, stride=CROWS), :].astype(F32)
        else:
            first = last = jnp.concatenate([prior[...]] * (Z // 4), 0)
        pair = (rolled(first, offset, 1), rolled(last, offset + width, 1))
        if plane in built:
            keep = lane < offset
            pair = tuple(jnp.where(keep, old, new) for old, new in zip(built[plane], pair))
        built[plane] = pair
    for plane, (one, other) in built.items():
        to_left[plane] = one
        to_right[plane] = other


def with_ghosts(half, message, key, tile):
    plane, offset, width = Y_SLOTS[key]
    lane = lanes((Z, 128))
    if half == 0:
        return jnp.where(lane < 96, tile, rolled(message[plane], -offset - width, 1))
    return jnp.where(lane < 32, rolled(message[plane], -offset, 1), tile)


def load_kernel(*refs):
    own, material_in, tab = refs[0:5], refs[5], refs[6]
    states = (refs[7:12], refs[12:17])
    c_halves, mat_halves = refs[17:19], refs[19:21]
    material, sems = refs[21:23]
    first = pltpu.make_async_copy(material_in, material, sems.at[10])
    first.start()
    copies = []
    for half in range(2):
        for a in range(5):
            source = own[a].at[:, :, :, 128 * half : 128 * half + W]
            copies.append(pltpu.make_async_copy(source, states[half][a], sems.at[5 * half + a]))
            copies[-1].start()
    first.wait()
    for x in range(ROWS):
        for half in range(2):
            mat_halves[half][x] = material[x, :, 128 * half : 128 * half + W].astype(F32)
        for tile in range(3):
            index = material[x, :, 128 * tile : 128 * (tile + 1)]
            for k in range(6):
                value = lookup(tab, k, index)
                for half in range(2):
                    if tile in TILES[half]:
                        local_tile = TILES[half].index(tile)
                        c_halves[half][k, x, :, 128 * local_tile : 128 * (local_tile + 1)] = value
    for copy in copies:
        copy.wait()


E_ITEMS = [(("e", t, k), 9 - t, 8 - t, True) for t in range(RATIO) for k in (1, 2)]
H_ITEMS = [(("h", t, k), 8 - t, 8 - t, True) for t in range(RATIO) for k in (1, 2)]
COARSE_ITEMS = [(("c", 0, k), CGHOST, CGHOST, False) for k in (1, 2)]
MATERIAL_ITEM = [(("m", 0, 0), 8, 8, True)]


def x_places(half, items):
    places, half_slots, plane, offset = {}, [], 1, 0
    for name, lefts, rights, fine in items:
        mixed = (1 - half) if fine else 0
        segments = []
        if fine:
            segments.append((half, 0, plane, 0, 128))
            plane += 1
        if not half_slots:
            half_slots = [(plane, 0), (plane, 64)]
            plane += 1
        own_lane = 64 * half
        segments.append((mixed, own_lane, *half_slots.pop(0), 64))
        left_lane = 64 - lefts if half else 128 - lefts
        right_lane = 0 if half else 64
        for lane, length in ((left_lane, lefts), (right_lane, rights)):
            segments.append((mixed, lane, 0, offset, length))
            offset += length
        places[name] = segments
    assert offset <= 128
    return places, plane


def write_x(half, items, values):
    places, planes = x_places(half, items)
    lane = lanes((Z, 128))
    built_planes = []
    for plane in range(planes):
        parts = sorted(
            (there, name, tile, start)
            for name, segments in places.items()
            for tile, start, where, there, _ in segments
            if where == plane
        )
        built = None
        for there, name, tile, start in parts:
            value = rolled(values[name][:, 128 * tile : 128 * (tile + 1)], there - start, 1)
            built = value if built is None else jnp.where(lane < there, built, value)
        built_planes.append(built)
    return built_planes


def read_x(ref, half, items, name):
    lane = lanes((Z, 128))
    built = {}
    for tile, start, plane, there, _ in sorted(x_places(half, items)[0][name]):
        value = rolled(ref[plane], start - there, 1)
        built[tile] = value if tile not in built else jnp.where(lane < start, built[tile], value)
    return jnp.concatenate([built[tile] for tile in sorted(built)], 1)


def x_items(first):
    extra = MATERIAL_ITEM if first else []
    return E_ITEMS + COARSE_ITEMS + extra, H_ITEMS + COARSE_ITEMS + extra


def gather(value, index):
    return jnp.take_along_axis(value, index, axis=1, mode="promise_in_bounds")


def prolong_lanes(half, value):
    lane = lanes((8, 128))
    third = lambda number: (number * 21846) >> 16
    if half == 0:
        indices = [third(lane), jnp.where(lane < 96, third(lane + 128), 128 - third(130 - lane))]
    else:
        indices = [jnp.where(lane < 32, third(lane), third(lane + 128)), third(lane + 256)]
    return jnp.concatenate([gather(value, index) for index in indices], 1)


def restrict_lanes(half, value):
    three = value + rolled(value, -1, 1) + rolled(value, -2, 1)
    lane = lanes((8, 128))
    index = (lane * RATIO) & 127
    tiles = [gather(three[:, 128 * tile : 128 * (tile + 1)], index) for tile in range(2)]
    in_first = lane * RATIO < (128 if half == 0 else 256)
    return jnp.where(in_first, tiles[0], tiles[1]) * (1.0 / RATIO**3)


def sort_messages(received, sorted_refs):
    even = lax.rem(lax.axis_index("gx"), 2) == 0
    first, second = received
    from_left, from_right = sorted_refs
    for plane in range(first.shape[0]):
        from_left[plane] = jnp.where(even, second[plane], first[plane])
        from_right[plane] = jnp.where(even, first[plane], second[plane])
    return from_left, from_right


def interface_rows(ce):
    return jnp.concatenate([ce[k, r][0:1] for k in range(2) for r in range(CROWS)], 0)


def top_plane(pl_ref, x, t):
    r = x // RATIO
    out = []
    for k in range(2):
        row = 2 * k + r
        value = pl_ref[row : row + 1, :]
        if t:
            value = value + float(t) * pl_ref[4 + row : 5 + row, :]
        out.append(value)
    return out


def lookup(tab, row, index):
    entry = jnp.broadcast_to(tab[row : row + 1, :], (8, 128))
    rows = []
    for z in range(0, Z, 8):
        rows.append(
            jnp.concatenate(
                [
                    gather(entry, index[z : z + 8, lane : lane + 128])
                    for lane in range(0, index.shape[1], 128)
                ],
                1,
            )
        )
    return jnp.concatenate(rows, 0)


def row_of(ref, x):
    return [ref[k, x] for k in range(3)]


def send_edges(half, first, fields, c, ce, ch, pl_ref, mat, to_first, to_second):
    fe, fh, fj, fp, fv = fields
    none = (None, None)
    e_items, h_items = x_items(first)
    coef = lambda x: [c[k, x] for k in range(6)]
    states = lambda x: (row_of(fj, x), row_of(fp, x), row_of(fv, x))
    e0 = {x: row_of(fe, x) for x in range(ROWS)}
    low, high = {}, {}

    for k in (1, 2):
        low["e", 0, k] = e0[0][k]
    h1 = {x: h_row(row_of(fh, x), e0[x], e0[x + 1][1:], top_plane(pl_ref, x, 0)) for x in (0, 1)}
    e1, s1 = {}, {}
    e1[0], *s1[0] = e_row(e0[0], h1[0], none, *states(0), coef(0))
    e1[1], *s1[1] = e_row(e0[1], h1[1], h1[0][1:], *states(1), coef(1), (1, 2))
    h2 = h_row(h1[0], e1[0], e1[1][1:], top_plane(pl_ref, 0, 1))
    e2 = e_row(e1[0], h2, none, *s1[0], coef(0), (1, 2))[0]
    for k in (1, 2):
        low["e", 1, k] = e1[0][k]
        low["e", 2, k] = e2[k]
        low["c", 0, k] = ce[k, 0]

    a, b, d = ROWS - 3, ROWS - 2, ROWS - 1
    h1 = {
        a: h_row(row_of(fh, a), e0[a], e0[b][1:], top_plane(pl_ref, a, 0), (1, 2)),
        b: h_row(row_of(fh, b), e0[b], e0[d][1:], top_plane(pl_ref, b, 0)),
        d: h_row(row_of(fh, d), e0[d], none, top_plane(pl_ref, d, 0)),
    }
    e1, s1 = {}, {}
    e1[b], *s1[b] = e_row(e0[b], h1[b], h1[a][1:], *states(b), coef(b))
    e1[d], *s1[d] = e_row(e0[d], h1[d], h1[b][1:], *states(d), coef(d))
    h2 = {
        b: h_row(h1[b], e1[b], e1[d][1:], top_plane(pl_ref, b, 1), (1, 2)),
        d: h_row(h1[d], e1[d], none, top_plane(pl_ref, d, 1)),
    }
    e2 = e_row(e1[d], h2[d], h2[b][1:], *s1[d], coef(d))[0]
    h3 = h_row(h2[d], e2, none, top_plane(pl_ref, d, 2), (1, 2))
    ch_last = h_row(row_of(ch, CROWS - 1), row_of(ce, CROWS - 1), none, (0.0, 0.0), (1, 2))
    for k in (1, 2):
        high["h", 0, k] = h1[d][k]
        high["h", 1, k] = h2[d][k]
        high["h", 2, k] = h3[k]
        high["c", 0, k] = ch_last[k]
    if first:
        low["m", 0, 0] = mat[0]
        high["m", 0, 0] = mat[ROWS - 1]
    even = lax.rem(lax.axis_index("gx"), 2) == 0
    for first_part, second_part, plane in zip(write_x(half, h_items, high), write_x(half, e_items, low), range(99)):
        to_first[plane] = jnp.where(even, first_part, second_part)
        to_second[plane] = jnp.where(even, second_part, first_part)


def start_kernel(half, *refs):
    fields_in, (c_in, mat_in, ce_in, ch_in, cmat, prior, tab, message) = refs[0:5], refs[5:13]
    fields, (c, ce, ch, inv, pl_ref, to_first, to_second, mat) = refs[13:18], refs[18:26]
    outer = slice(128, 256) if half == 0 else slice(0, 128)
    inner = slice(0, 128) if half == 0 else slice(128, 256)
    for x in range(ROWS):
        value = with_ghosts(half, message, ("m", 0, 0, x), mat_in[x, :, outer])
        index = jnp.clip(value.astype(jnp.int32), 0, 127)
        if x in (0, ROWS - 1):
            mat[x, :, outer] = value
            mat[x, :, inner] = mat_in[x, :, inner]
        for k in range(6):
            c[k, x, :, outer] = lookup(tab, k, index)
    for a in range(5):
        for k in range(3):
            for x in range(ROWS):
                fields[a][k, x, :, outer] = with_ghosts(
                    half, message, ("f", a, k, x), fields_in[a][k, x, :, outer]
                )
    for a, (source, target) in enumerate(((ce_in, ce), (ch_in, ch))):
        for k in range(3):
            for r in range(CROWS):
                target[k, r] = with_ghosts(half, message, ("c", a, k, r), coarse_row(source, k, r))
    for r in range(CROWS):
        value = cmat[pl.ds(r, Z, stride=CROWS), :].astype(F32)
        index = with_ghosts(half, message, ("cm", 0, 0, r), value).astype(jnp.int32)
        inv[r] = lookup(tab, 7, jnp.clip(index, 0, 127))
    before = jnp.concatenate([prior[...]] * (Z // 4), 0)
    before = with_ghosts(half, message, ("prior", 0, 0, 0), before)[0:4]
    interface = interface_rows(ce)
    increment = (interface - before) * (1.0 / RATIO)
    pl_ref[...] = prolong_lanes(half, jnp.concatenate([interface, increment], 0))
    send_edges(half, True, fields, c, ce, ch, pl_ref, mat, to_first, to_second)


def coarse_step(half, first, olds, news, c, ghost, olds_c, news_c, inv, pl_ref, from_left, from_right):
    e_items, h_items = x_items(first)
    zero = jnp.zeros((Z, W), F32)
    flat = (0.0, 0.0)
    (ce0, ch0), (ce, ch) = olds_c, news_c
    coarse_e0 = [row_of(ce0, r) for r in range(CROWS)]
    up = [read_x(from_right, half, e_items, ("c", 0, k)) for k in (1, 2)]
    down = [read_x(from_left, half, h_items, ("c", 0, k)) for k in (1, 2)]
    down = [down[0] + COURANT * coarse_e0[0][2], down[1] - COURANT * coarse_e0[0][1]]
    coarse_h = []
    for r in range(CROWS):
        following = coarse_e0[r + 1][1:] if r + 1 < CROWS else up
        coarse_h.append(h_row(row_of(ch0, r), coarse_e0[r], following, flat))
        for k in range(3):
            ch[k, r] = coarse_h[r][k]

    ge = gh = he = hh = None
    summed = [[None] * CROWS for _ in range(2)]
    for t in range(RATIO):
        fe, fh, fj, fp, fv = olds if t == 0 else news
        e_first = row_of(fe, 0)
        following = [read_x(from_right, half, e_items, ("e", t, k)) for k in (1, 2)]
        if t:
            following = [base + more for base, more in zip(following, he[1:])]
        far = [None, None]
        if t == 0:
            gh = [None, COURANT * e_first[2], -COURANT * e_first[1]]
        else:
            far = [COURANT * ge[2], -COURANT * ge[1]]
            old = [zero if value is None else value for value in gh]
            gh = h_row(old, ge, e_first[1:], flat, (0, 1, 2) if t < RATIO - 1 else (1, 2))
        preceding = [read_x(from_left, half, h_items, ("h", t, k)) + gh[k] for k in (1, 2)]
        current = e_first
        for x in range(ROWS):
            upper = row_of(fe, x + 1) if x + 1 < ROWS else None
            h = h_row(
                row_of(fh, x), current, upper[1:] if upper else following, top_plane(pl_ref, x, t)
            )
            e2, j2, p2, v2 = e_row(
                current, h, preceding, row_of(fj, x), row_of(fp, x), row_of(fv, x), [c[k, x] for k in range(6)]
            )
            for k in range(3):
                news[0][k, x] = e2[k]
                news[1][k, x] = h[k]
                news[2][k, x] = j2[k]
                news[3][k, x] = p2[k]
                news[4][k, x] = v2[k]
            for k in range(2):
                part = h[k][8:Z]
                have = summed[k][x // RATIO]
                summed[k][x // RATIO] = part if have is None else have + part
            preceding = h[1:]
            current = upper
        if t == 0:
            (a, b), (a2, b2) = [[ghost[k, side] for k in range(2)] for side in range(2)]
            ge = [
                a * ((gh[2] - left(gh[2])) - (gh[1] - below(gh[1], 0.0))),
                -a * gh[2],
                a * gh[1],
            ]
            he = [zero, a2 * preceding[1], -a2 * preceding[0]]
        elif t == 1:
            curl = curl_h(gh, far, flat)
            ge = [ge[k] + a * (curl[k] - b * ge[k]) for k in range(3)]
            hh = h_row([zero] * 3, he, (None, None), flat)
            curl = curl_h(hh, preceding, flat, (1, 2))
            he = [None] + [he[k] + a2 * (curl[k] - b2 * he[k]) for k in (1, 2)]

    rows = [summed[k][r][7:8] for k in range(2) for r in range(CROWS)]
    bottoms = restrict_lanes(half, jnp.concatenate(rows + rows, 0))
    preceding = down
    for r in range(CROWS):
        bottom = [bottoms[2 * k + r : 2 * k + r + 1, :] for k in range(2)]
        curl = curl_h(coarse_h[r], preceding, bottom)
        for k in range(3):
            ce[k, r] = coarse_e0[r][k] + inv[r] * curl[k]
        preceding = coarse_h[r][1:]


def ghost_coefficients(half, ghost, tab, from_left, from_right):
    e_items, h_items = x_items(True)
    for side, (ref, items) in enumerate(((from_left, h_items), (from_right, e_items))):
        index = jnp.clip(read_x(ref, half, items, ("m", 0, 0)).astype(jnp.int32), 0, 127)
        ghost[0, side] = lookup(tab, 0, index)
        ghost[1, side] = lookup(tab, 6, index)


def step_kernel(half, first, *refs):
    olds, rest = refs[0:5], refs[5:]
    c, ce0, ch0, inv, pl0, ghost_in = rest[0:6]
    from_left, from_right = sort_messages(rest[6:8], rest[-2:])
    news, rest = rest[8:13], rest[13:-2]
    if first:
        ce, ch, pl_ref, to_first, to_second, ghost = rest
        ghost_coefficients(half, ghost, ghost_in, from_left, from_right)
    else:
        ce, ch, pl_ref, to_first, to_second = rest
        ghost = ghost_in
    coarse_step(half, first, olds, news, c, ghost, (ce0, ch0), (ce, ch), inv, pl0, from_left, from_right)
    interface = interface_rows(ce)
    increment = (interface - interface_rows(ce0)) * (1.0 / RATIO)
    pl_ref[...] = prolong_lanes(half, jnp.concatenate([interface, increment], 0))
    send_edges(half, False, news, c, ce, ch, pl_ref, None, to_first, to_second)


def final_kernel(half, *refs):
    olds, rest = refs[0:5], refs[5:]
    c, ce0, ch0, inv, pl0, ghost = rest[0:6]
    from_left, from_right = sort_messages(rest[6:8], rest[-2:])
    if half == 0:
        news, (ce, ch) = rest[8:13], rest[13:15]
    else:
        others, others_c = rest[8:13], rest[13:15]
        outs, outs_c = rest[15:20], rest[20:22]
        news, (ce, ch) = rest[22:27], rest[27:29]
    coarse_step(half, False, olds, news, c, ghost, (ce0, ch0), (ce, ch), inv, pl0, from_left, from_right)
    if half == 0:
        return
    first = lanes((Z, 128)) < 64
    for a in range(5):
        for k in range(3):
            for x in range(ROWS):
                outs[a][k, x, :, 0:128] = others[a][k, x, :, 0:128]
                outs[a][k, x, :, 128:256] = jnp.where(
                    first, others[a][k, x, :, 128:256], news[a][k, x, :, 0:128]
                )
                outs[a][k, x, :, 256:384] = news[a][k, x, :, 128:256]
    for other, source, target in zip(others_c, (ce, ch), outs_c):
        for k in range(3):
            for r in range(CROWS):
                target[k, pl.ds(r, Z, stride=CROWS), :] = jnp.where(first, other[k, r], source[k, r])


def shifted(value, axis, steps):
    count = lax.axis_size(axis)
    return lax.ppermute(value, axis, [(source, (source + steps) % count) for source in range(count)])


FULL = pl.BlockSpec(memory_space=pltpu.VMEM)
RAW = pl.BlockSpec(memory_space=pltpu.HBM)
COST = pl.CostEstimate(flops=4_000_000, transcendentals=0, bytes_accessed=8_000_000)
FIELD = (3, ROWS, Z, W)
COEF = (6, ROWS, Z, W)
COARSE = (3, CROWS, Z, CW)
PLANES = (8, W)


def call(kernel, outs, args, specs=None, scratch=(), aliases=None, vmem=16):
    outs = [dims if isinstance(dims, jax.ShapeDtypeStruct) else jax.ShapeDtypeStruct(dims, F32) for dims in outs]
    return pl.pallas_call(
        kernel,
        out_shape=outs,
        in_specs=specs or [FULL] * len(args),
        out_specs=[FULL] * len(outs),
        scratch_shapes=list(scratch),
        input_output_aliases=aliases or {},
        compiler_params=pltpu.CompilerParams(vmem_limit_bytes=vmem * 1024 * 1024),
        cost_estimate=COST,
    )(*args)


def table(permittivity, plasma, damping, strength, resonance, linewidth):
    half_step = 0.5 * TIMESTEP
    c2 = plasma * plasma * TIMESTEP / (1.0 + damping * half_step)
    c4 = TIMESTEP * resonance * resonance / (1.0 + linewidth * half_step)
    rows = jnp.stack(
        [
            TIMESTEP / permittivity,
            (1.0 - damping * half_step) / (1.0 + damping * half_step),
            c2,
            (1.0 - linewidth * half_step) / (1.0 + linewidth * half_step),
            c4,
            strength,
            c2 + c4 * strength,
            COURANT / permittivity,
        ]
    )
    return jnp.pad(rows, ((0, 0), (0, 120)))


def message_shapes(half, first):
    return [(x_places(half, items)[1], Z, 128) for items in x_items(first)]


def exchanged(messages):
    count = lax.axis_size("gx")
    swapped = []
    for message, first in zip(messages, (0, 1)):
        pairs = [((first + i) % count, (first + (i ^ 1)) % count) for i in range(count)]
        swapped.append(lax.ppermute(message, "gx", pairs))
    return swapped


def local(
    fine_e,
    fine_h,
    drude_current,
    lorentz_pol,
    lorentz_rate,
    material,
    permittivity,
    plasma,
    damping,
    strength,
    resonance,
    linewidth,
    coarse_e,
    coarse_h,
    coarse_material,
    coarse_prior,
):
    fields = [
        jnp.transpose(value, (0, 2, 1, 3))
        for value in (fine_e, fine_h, drude_current, lorentz_pol, lorentz_rate)
    ]
    mat = jnp.transpose(material, (1, 0, 2))
    ce = coarse_e.reshape(3, Z * CROWS, 128)
    ch = coarse_h.reshape(3, Z * CROWS, 128)
    cmat = coarse_material.reshape(Z * CROWS, 128)
    prior = coarse_prior.reshape(2 * CROWS, 128)
    tab = table(permittivity, plasma, damping, strength, resonance, linewidth)

    vmem = lambda *dims: pltpu.VMEM(dims, F32)
    ints = lambda *dims: jax.ShapeDtypeStruct(dims, jnp.int32)
    to_left, to_right, ce, ch, cmat, prior = call(
        pack_y_kernel,
        [(Y_PLANES, Z, 128)] * 2 + [ce.shape, ch.shape, ints(*cmat.shape), prior.shape],
        [*fields, mat, ce, ch, cmat, prior],
        [RAW] * 10,
        [
            vmem(5, 3, ROWS, Z, 128),
            vmem(5, 3, ROWS, Z, 128),
            pltpu.VMEM((2, ROWS, Z, 128), jnp.int32),
            pltpu.SemaphoreType.DMA((16,)),
        ],
        vmem=61,
    )
    from_right = shifted(to_left, "gy", -1)
    from_left = shifted(to_right, "gy", 1)
    loaded = call(
        load_kernel,
        [FIELD] * 10 + [COEF] * 2 + [(ROWS, Z, W)] * 2,
        [*fields, mat, tab],
        [RAW] * 6 + [FULL],
        [pltpu.VMEM((ROWS, Z, OWN), jnp.int32), pltpu.SemaphoreType.DMA((11,))],
    )
    parts, waiting = [None, None], [None, None]
    for half in range(2):
        state = loaded[5 * half : 5 * half + 5]
        out = call(
            functools.partial(start_kernel, half),
            [FIELD] * 5 + [COEF, COARSE, COARSE, (CROWS, Z, CW), PLANES] + message_shapes(half, True),
            [*state, loaded[10 + half], loaded[12 + half], ce, ch, cmat, prior, tab, (from_left, from_right)[half]],
            scratch=[vmem(ROWS, Z, W)],
            aliases={index: index for index in range(6)},
        )
        parts[half] = (out[0:5], out[5:10], tab)
        waiting[half] = exchanged(out[10:12])
    for step in range(STEPS - 1):
        for half in range(2):
            state, (c, ce, ch, inv, planes), ghost = parts[half]
            out = call(
                functools.partial(step_kernel, half, step == 0),
                [FIELD] * 5
                + [COARSE, COARSE, PLANES]
                + message_shapes(half, False)
                + ([(2, 2, Z, W)] if step == 0 else []),
                [*state, c, ce, ch, inv, planes, ghost, *waiting[half]],
                scratch=[vmem(*message.shape) for message in waiting[half]],
            )
            if step == 0:
                ghost = out[10]
            parts[half] = (out[0:5], (c, out[5], out[6], inv, out[7]), ghost)
            waiting[half] = exchanged(out[8:10])
    done = []
    for half in range(2):
        state, coarse, ghost = parts[half]
        done = call(
            functools.partial(final_kernel, half),
            [FIELD] * 5 + [COARSE] * 2 if half == 0 else [(3, ROWS, Z, OWN)] * 5 + [(3, Z * CROWS, 128)] * 2,
            [*state, *coarse, ghost, *waiting[half], *done],
            scratch=([vmem(*FIELD)] * 5 + [vmem(*COARSE)] * 2 if half else [])
            + [vmem(*message.shape) for message in waiting[half]],
        )
    fine = [jnp.transpose(value, (0, 2, 1, 3)) for value in done[0:5]]
    coarse = [value.reshape(3, Z, CROWS, 128) for value in done[5:7]]
    return (*fine, *coarse)


def solution(mesh):
    field = P(None, None, "gx", "gy")
    plane = P(None, "gx", "gy")
    in_specs = (field,) * 5 + (plane,) + (P(),) * 6 + (field, field, plane, plane)
    return jax.shard_map(local, mesh=mesh, in_specs=in_specs, out_specs=(field,) * 7, check_vma=False)
```

profile of v0, /device:TPU:2, one launch (start us, length us, event | category | flops | bytes accessed | tf_op | source)
XLA Modules:
  0.0 61.2 jit_solution(5442033184356194425)
XLA Ops:
  0.7 2.9 %shard_map.208 = (f32[8,16,128]{2,1,0:T(8,128)}, f32[8,16,128]{2,1,0:T(8,128)}, f32[3,32,128]{2,1,0:T(8,128)}, f32[3,32,128]{2,1,0:T(8,128)}, s32[32,128]{1,0:T(8,128)}, /*index=5*/f32[4,128]{1,0:T(4,128)}) custom-call(f32[3,6,16,384]{3,2,1,0:T(8,128)} %bitcast.28, f32[3,6,16,384]{3,2,1,0:T(8,128)} %bitcast.30, f32[3,6,16,384]{3,2,1,0:T(8,128)} %bitcast.32, ...), custom_call_target="tpu_custom_call" | custom-call | flops 4000000 | bytes 8000000 | tf_op jit(solution)/shard_map/pallas_call | solution.py:563
  3.6 0.0 copy-start.13
  3.7 0.0 copy-start.10
  3.7 0.0 copy-start.11
  3.7 0.1 collective-permute-start.7
  3.8 0.0 copy-start.15
  3.8 3.8 %collective-permute-start = (f32[8,16,128]{2,1,0:T(8,128)}, f32[8,16,128]{2,1,0:T(8,128)S(1)}, u32[]{:S(2)}, u32[]{:S(2)}) collective-permute-start(f32[8,16,128]{2,1,0:T(8,128)} %get-tuple-element.118), channel_id=1, source_target_pairs={{0,15},{1,0},{2,1},{3,2},{4,3},{5,4},{6,5},{7,6},{8,7},{9,8},{10,9... | collective-permute-start | bytes 196616 | tf_op jit(solution)/shard_map/ppermute | solution.py:549
  7.8 1.1 %shard_map.207 = (f32[3,6,16,256]{3,2,1,0:T(8,128)S(1)}, f32[3,6,16,256]{3,2,1,0:T(8,128)S(1)}, f32[3,6,16,256]{3,2,1,0:T(8,128)S(1)}, f32[3,6,16,256]{3,2,1,0:T...) custom-call(f32[3,6,16,384]{3,2,1,0:T(8,128)S(1)} %bitcast.29, ...), custom_call_target="tpu_custom_call" | custom-call | flops 4000000 | bytes 8000000 | tf_op jit(solution)/shard_map/pallas_call | solution.py:563
  8.9 0.0 copy-start.8
  8.9 0.9 %collective-permute-done.7.refs_12_ = f32[8,16,128]{2,1,0:T(8,128)S(1)} collective-permute-done((f32[8,16,128]{2,1,0:T(8,128)}, f32[8,16,128]{2,1,0:T(8,128)S(1)}, u32[]{:S(2)}, u32[]{:S(2)}) %collective-permute-start.7) | collective-permute-done | bytes 65568 | tf_op jit(solution)/shard_map/ppermute | solution.py:549
  9.8 0.7 %copy-done.9 = f32[4,128]{1,0:T(4,128)S(1)} copy-done((f32[4,128]{1,0:T(4,128)S(1)}, f32[4,128]{1,0:T(4,128)}, u32[]{:S(2)}) %copy-start.9) | copy-done | bytes 2072
  10.5 1.5 %shard_map.212 = (f32[3,6,16,256]{3,2,1,0:T(8,128)S(1)}, f32[3,6,16,256]{3,2,1,0:T(8,128)S(1)}, f32[3,6,16,256]{3,2,1,0:T(8,128)S(1)}, f32[3,6,16,256]{3,2,1,0:T...) custom-call(f32[3,6,16,256]{3,2,1,0:T(8,128)S(1)} %get-tuple-element, ...), custom_call_target="tpu_custom_call", output_to_operand_aliasing={{0}: (0, {}), {1}: (1, {}), {2}: (2, {}), {3}: (3, {}), {4}... | custom-call | flops 4000000 | bytes 8000000 | tf_op jit(solution)/shard_map/pallas_call | solution.py:563
  11.9 2.2 %collective-permute-start.8 = (f32[13,16,128]{2,1,0:T(8,128)S(1)}, f32[13,16,128]{2,1,0:T(8,128)S(1)}, u32[]{:S(2)}, u32[]{:S(2)}) collective-permute-start(f32[13,16,128]{2,1,0:T(8,128)S(1)} %get-tuple-element.170), channel_id=1, source_target_pairs={{0,16},{16,0},{32,48},{48,32},{64,80},{80,64},{96,112},{112,96},{1... | collective-permute-start | bytes 319496 | tf_op jit(solution)/shard_map/ppermute | solution.py:603
  14.1 6.7 %collective-permute-start.9 = (f32[13,16,128]{2,1,0:T(8,128)S(1)}, f32[13,16,128]{2,1,0:T(8,128)S(1)}, u32[]{:S(2)}, u32[]{:S(2)}) collective-permute-start(f32[13,16,128]{2,1,0:T(8,128)S(1)} %get-tuple-element.171), channel_id=1, source_target_pairs={{16,32},{32,16},{48,64},{64,48},{80,96},{96,80},{112,128},{128,112... | collective-permute-start | bytes 319496 | tf_op jit(solution)/shard_map/ppermute | solution.py:603
  20.8 1.5 %shard_map.209 = (f32[3,6,16,256]{3,2,1,0:T(8,128)S(1)}, f32[3,6,16,256]{3,2,1,0:T(8,128)S(1)}, f32[3,6,16,256]{3,2,1,0:T(8,128)S(1)}, f32[3,6,16,256]{3,2,1,0:T...) custom-call(f32[3,6,16,256]{3,2,1,0:T(8,128)S(1)} %get-tuple-element, ...), custom_call_target="tpu_custom_call", output_to_operand_aliasing={{0}: (0, {}), {1}: (1, {}), {2}: (2, {}), {3}: (3, {}), {4}... | custom-call | flops 4000000 | bytes 8000000 | tf_op jit(solution)/shard_map/pallas_call | solution.py:563
  22.3 0.1 collective-permute-start.1
  22.4 4.0 %collective-permute-start.2 = (f32[13,16,128]{2,1,0:T(8,128)S(1)}, f32[13,16,128]{2,1,0:T(8,128)S(1)}, u32[]{:S(2)}, u32[]{:S(2)}) collective-permute-start(f32[13,16,128]{2,1,0:T(8,128)S(1)} %get-tuple-element.130), channel_id=1, source_target_pairs={{16,32},{32,16},{48,64},{64,48},{80,96},{96,80},{112,128},{128,112... | collective-permute-start | bytes 319496 | tf_op jit(solution)/shard_map/ppermute | solution.py:603
  26.4 2.4 %shard_map.213 = (f32[3,6,16,256]{3,2,1,0:T(8,128)S(1)}, f32[3,6,16,256]{3,2,1,0:T(8,128)S(1)}, f32[3,6,16,256]{3,2,1,0:T(8,128)S(1)}, f32[3,6,16,256]{3,2,1,0:T...) custom-call(f32[3,6,16,256]{3,2,1,0:T(8,128)S(1)} %get-tuple-element, ...), custom_call_target="tpu_custom_call" | custom-call | flops 4000000 | bytes 8000000 | tf_op jit(solution)/shard_map/pallas_call | solution.py:563
  28.7 0.1 collective-permute-start.10
  28.9 4.5 %collective-permute-start.11 = (f32[11,16,128]{2,1,0:T(8,128)S(1)}, f32[11,16,128]{2,1,0:T(8,128)S(1)}, u32[]{:S(2)}, u32[]{:S(2)}) collective-permute-start(f32[11,16,128]{2,1,0:T(8,128)S(1)} %get-tuple-element.182), channel_id=1, source_target_pairs={{16,32},{32,16},{48,64},{64,48},{80,96},{96,80},{112,128},{128,112... | collective-permute-start | bytes 270344 | tf_op jit(solution)/shard_map/ppermute | solution.py:603
  33.3 2.3 %shard_map.210 = (f32[3,6,16,256]{3,2,1,0:T(8,128)S(1)}, f32[3,6,16,256]{3,2,1,0:T(8,128)S(1)}, f32[3,6,16,256]{3,2,1,0:T(8,128)S(1)}, f32[3,6,16,256]{3,2,1,0:T...) custom-call(f32[3,6,16,256]{3,2,1,0:T(8,128)S(1)} %get-tuple-element, ...), custom_call_target="tpu_custom_call" | custom-call | flops 4000000 | bytes 8000000 | tf_op jit(solution)/shard_map/pallas_call | solution.py:563
  35.7 0.3 collective-permute-start.3
  36.0 3.5 %collective-permute-start.4 = (f32[11,16,128]{2,1,0:T(8,128)S(1)}, f32[11,16,128]{2,1,0:T(8,128)S(1)}, u32[]{:S(2)}, u32[]{:S(2)}) collective-permute-start(f32[11,16,128]{2,1,0:T(8,128)S(1)} %get-tuple-element.141), channel_id=1, source_target_pairs={{16,32},{32,16},{48,64},{64,48},{80,96},{96,80},{112,128},{128,112... | collective-permute-start | bytes 270344 | tf_op jit(solution)/shard_map/ppermute | solution.py:603
  39.4 2.1 %shard_map.214 = (f32[3,6,16,256]{3,2,1,0:T(8,128)S(1)}, f32[3,6,16,256]{3,2,1,0:T(8,128)S(1)}, f32[3,6,16,256]{3,2,1,0:T(8,128)S(1)}, f32[3,6,16,256]{3,2,1,0:T...) custom-call(f32[3,6,16,256]{3,2,1,0:T(8,128)S(1)} %get-tuple-element, ...), custom_call_target="tpu_custom_call" | custom-call | flops 4000000 | bytes 8000000 | tf_op jit(solution)/shard_map/pallas_call | solution.py:563
  41.5 2.2 %collective-permute-start.12 = (f32[11,16,128]{2,1,0:T(8,128)S(1)}, f32[11,16,128]{2,1,0:T(8,128)S(1)}, u32[]{:S(2)}, u32[]{:S(2)}) collective-permute-start(f32[11,16,128]{2,1,0:T(8,128)S(1)} %get-tuple-element.191), channel_id=1, source_target_pairs={{0,16},{16,0},{32,48},{48,32},{64,80},{80,64},{96,112},{112,96},{1... | collective-permute-start | bytes 270344 | tf_op jit(solution)/shard_map/ppermute | solution.py:603
  43.8 1.6 %collective-permute-start.13 = (f32[11,16,128]{2,1,0:T(8,128)S(1)}, f32[11,16,128]{2,1,0:T(8,128)S(1)}, u32[]{:S(2)}, u32[]{:S(2)}) collective-permute-start(f32[11,16,128]{2,1,0:T(8,128)S(1)} %get-tuple-element.192), channel_id=1, source_target_pairs={{16,32},{32,16},{48,64},{64,48},{80,96},{96,80},{112,128},{128,112... | collective-permute-start | bytes 270344 | tf_op jit(solution)/shard_map/ppermute | solution.py:603
  45.3 2.1 %shard_map.211 = (f32[3,6,16,256]{3,2,1,0:T(8,128)S(1)}, f32[3,6,16,256]{3,2,1,0:T(8,128)S(1)}, f32[3,6,16,256]{3,2,1,0:T(8,128)S(1)}, f32[3,6,16,256]{3,2,1,0:T...) custom-call(f32[3,6,16,256]{3,2,1,0:T(8,128)S(1)} %get-tuple-element, ...), custom_call_target="tpu_custom_call" | custom-call | flops 4000000 | bytes 8000000 | tf_op jit(solution)/shard_map/pallas_call | solution.py:563
  47.4 2.5 %collective-permute-start.5 = (f32[11,16,128]{2,1,0:T(8,128)S(1)}, f32[11,16,128]{2,1,0:T(8,128)S(1)}, u32[]{:S(2)}, u32[]{:S(2)}) collective-permute-start(f32[11,16,128]{2,1,0:T(8,128)S(1)} %get-tuple-element.150), channel_id=1, source_target_pairs={{0,16},{16,0},{32,48},{48,32},{64,80},{80,64},{96,112},{112,96},{1... | collective-permute-start | bytes 270344 | tf_op jit(solution)/shard_map/ppermute | solution.py:603
  50.0 2.8 %collective-permute-start.6 = (f32[11,16,128]{2,1,0:T(8,128)S(1)}, f32[11,16,128]{2,1,0:T(8,128)S(1)}, u32[]{:S(2)}, u32[]{:S(2)}) collective-permute-start(f32[11,16,128]{2,1,0:T(8,128)S(1)} %get-tuple-element.151), channel_id=1, source_target_pairs={{16,32},{32,16},{48,64},{64,48},{80,96},{96,80},{112,128},{128,112... | collective-permute-start | bytes 270344 | tf_op jit(solution)/shard_map/ppermute | solution.py:603
  52.8 1.7 %shard_map.215 = (f32[3,6,16,256]{3,2,1,0:T(8,128)S(1)}, f32[3,6,16,256]{3,2,1,0:T(8,128)S(1)}, f32[3,6,16,256]{3,2,1,0:T(8,128)S(1)}, f32[3,6,16,256]{3,2,1,0:T...) custom-call(f32[3,6,16,256]{3,2,1,0:T(8,128)S(1)} %get-tuple-element.183.re, ...), custom_call_target="tpu_custom_call" | custom-call | flops 4000000 | bytes 8000000 | tf_op jit(solution)/shard_map/pallas_call | solution.py:563
  54.5 3.6 %collective-permute-done.6.refs_12_ = f32[11,16,128]{2,1,0:T(8,128)S(1)} collective-permute-done((f32[11,16,128]{2,1,0:T(8,128)S(1)}, f32[11,16,128]{2,1,0:T(8,128)S(1)}, u32[]{:S(2)}, u32[]{:S(2)}) %collective-permute-start.6) | collective-permute-done | bytes 90144 | tf_op jit(solution)/shard_map/ppermute | solution.py:603
  58.1 3.1 %shard_map.216 = (f32[3,6,16,384]{3,2,1,0:T(8,128)}, f32[3,6,16,384]{3,2,1,0:T(8,128)}, f32[3,6,16,384]{3,2,1,0:T(8,128)}, f32[3,6,16,384]{3,2,1,0:T(8,128)}, f3...) custom-call(f32[3,6,16,256]{3,2,1,0:T(8,128)S(1)} %get-tuple-element.142.refs_0_, ...), custom_call_target="tpu_custom_call" | custom-call | flops 4000000 | bytes 8000000 | tf_op jit(solution)/shard_map/pallas_call | solution.py:563
  (42 shorter events, 0.1 us)
Async XLA Ops:
  0.6 7.1 %copy-start = (f32[3,16,6,384]{3,1,2,0:T(8,128)S(1)}, f32[3,16,6,384]{3,1,2,0:T(8,128)}, u32[]{:S(2)}) copy-start(f32[3,16,6,384]{3,1,2,0:T(8,128)} %param.16) | copy-start | bytes 1327108
  0.6 7.1 %copy-start.1 = (f32[3,16,6,384]{3,1,2,0:T(8,128)S(1)}, f32[3,16,6,384]{3,1,2,0:T(8,128)}, u32[]{:S(2)}) copy-start(f32[3,16,6,384]{3,1,2,0:T(8,128)} %param.17) | copy-start | bytes 1327108
  0.7 7.1 %copy-start.2 = (f32[3,16,6,384]{3,1,2,0:T(8,128)S(1)}, f32[3,16,6,384]{3,1,2,0:T(8,128)}, u32[]{:S(2)}) copy-start(f32[3,16,6,384]{3,1,2,0:T(8,128)} %param.18) | copy-start | bytes 1327108
  0.7 7.1 %copy-start.3 = (f32[3,16,6,384]{3,1,2,0:T(8,128)S(1)}, f32[3,16,6,384]{3,1,2,0:T(8,128)}, u32[]{:S(2)}) copy-start(f32[3,16,6,384]{3,1,2,0:T(8,128)} %param.19) | copy-start | bytes 1327108
  0.7 7.1 %copy-start.4 = (f32[3,16,6,384]{3,1,2,0:T(8,128)S(1)}, f32[3,16,6,384]{3,1,2,0:T(8,128)}, u32[]{:S(2)}) copy-start(f32[3,16,6,384]{3,1,2,0:T(8,128)} %param.20) | copy-start | bytes 1327108
  0.7 7.1 %copy-start.5 = (s32[16,6,384]{2,0,1:T(8,128)S(1)}, s32[16,6,384]{2,0,1:T(8,128)}, u32[]{:S(2)}) copy-start(s32[16,6,384]{2,0,1:T(8,128)} %param.21) | copy-start | bytes 442372
  3.6 4.0 %copy-start.13 = (f32[8]{0:T(128)S(1)}, f32[8]{0:T(128)}, u32[]{:S(2)}) copy-start(f32[8]{0:T(128)} %param.24) | copy-start | bytes 100
  3.6 4.0 %copy-start.14 = (f32[8]{0:T(128)S(1)}, f32[8]{0:T(128)}, u32[]{:S(2)}) copy-start(f32[8]{0:T(128)} %param.23) | copy-start | bytes 100
  3.7 4.0 %copy-start.10 = (f32[8]{0:T(128)S(1)}, f32[8]{0:T(128)}, u32[]{:S(2)}) copy-start(f32[8]{0:T(128)} %param.25) | copy-start | bytes 100
  3.7 4.0 %copy-start.11 = (f32[8]{0:T(128)S(1)}, f32[8]{0:T(128)}, u32[]{:S(2)}) copy-start(f32[8]{0:T(128)} %param.27) | copy-start | bytes 100
  3.7 4.0 %copy-start.12 = (f32[8]{0:T(128)S(1)}, f32[8]{0:T(128)}, u32[]{:S(2)}) copy-start(f32[8]{0:T(128)} %param.26) | copy-start | bytes 100
  3.7 6.1 %collective-permute-start.7 = (f32[8,16,128]{2,1,0:T(8,128)}, f32[8,16,128]{2,1,0:T(8,128)S(1)}, u32[]{:S(2)}, u32[]{:S(2)}) collective-permute-start(f32[8,16,128]{2,1,0:T(8,128)} %get-tuple-element.159), channel_id=1, source_target_pairs={{0,1},{1,2},{2,3},{3,4},{4,5},{5,6},{6,7},{7,8},{8,9},{9,10},{10,1... | collective-permute-start | bytes 196616 | tf_op jit(solution)/shard_map/ppermute | solution.py:549
  3.8 3.9 %copy-start.15 = (f32[8]{0:T(128)S(1)}, f32[8]{0:T(128)}, u32[]{:S(2)}) copy-start(f32[8]{0:T(128)} %param.22) | copy-start | bytes 100
  3.8 17.0 %collective-permute-start = (f32[8,16,128]{2,1,0:T(8,128)}, f32[8,16,128]{2,1,0:T(8,128)S(1)}, u32[]{:S(2)}, u32[]{:S(2)}) collective-permute-start(f32[8,16,128]{2,1,0:T(8,128)} %get-tuple-element.118), channel_id=1, source_target_pairs={{0,15},{1,0},{2,1},{3,2},{4,3},{5,4},{6,5},{7,6},{8,7},{9,8},{10,9... | collective-permute-start | bytes 196616 | tf_op jit(solution)/shard_map/ppermute | solution.py:549
  7.8 2.0 %copy-start.6 = (f32[3,32,128]{2,1,0:T(8,128)S(1)}, f32[3,32,128]{2,1,0:T(8,128)}, u32[]{:S(2)}) copy-start(f32[3,32,128]{2,1,0:T(8,128)} %get-tuple-element.114.refs_7_) | copy-start | bytes 147460
  7.8 2.0 %copy-start.7 = (f32[3,32,128]{2,1,0:T(8,128)S(1)}, f32[3,32,128]{2,1,0:T(8,128)}, u32[]{:S(2)}) copy-start(f32[3,32,128]{2,1,0:T(8,128)} %get-tuple-element.115.refs_8_) | copy-start | bytes 147460
  8.9 0.9 %copy-start.8 = (s32[32,128]{1,0:T(8,128)S(1)}, s32[32,128]{1,0:T(8,128)}, u32[]{:S(2)}) copy-start(s32[32,128]{1,0:T(8,128)} %get-tuple-element.116.refs_9_) | copy-start | bytes 49156
  9.8 0.7 %copy-start.9 = (f32[4,128]{1,0:T(4,128)S(1)}, f32[4,128]{1,0:T(4,128)}, u32[]{:S(2)}) copy-start(f32[4,128]{1,0:T(4,128)} %get-tuple-element.117.refs_10_) | copy-start | bytes 6148
  11.9 14.5 %collective-permute-start.8 = (f32[13,16,128]{2,1,0:T(8,128)S(1)}, f32[13,16,128]{2,1,0:T(8,128)S(1)}, u32[]{:S(2)}, u32[]{:S(2)}) collective-permute-start(f32[13,16,128]{2,1,0:T(8,128)S(1)} %get-tuple-element.170), channel_id=1, source_target_pairs={{0,16},{16,0},{32,48},{48,32},{64,80},{80,64},{96,112},{112,96},{1... | collective-permute-start | bytes 319496 | tf_op jit(solution)/shard_map/ppermute | solution.py:603
  14.1 12.2 %collective-permute-start.9 = (f32[13,16,128]{2,1,0:T(8,128)S(1)}, f32[13,16,128]{2,1,0:T(8,128)S(1)}, u32[]{:S(2)}, u32[]{:S(2)}) collective-permute-start(f32[13,16,128]{2,1,0:T(8,128)S(1)} %get-tuple-element.171), channel_id=1, source_target_pairs={{16,32},{32,16},{48,64},{64,48},{80,96},{96,80},{112,128},{128,112... | collective-permute-start | bytes 319496 | tf_op jit(solution)/shard_map/ppermute | solution.py:603
  22.3 11.0 %collective-permute-start.1 = (f32[13,16,128]{2,1,0:T(8,128)S(1)}, f32[13,16,128]{2,1,0:T(8,128)S(1)}, u32[]{:S(2)}, u32[]{:S(2)}) collective-permute-start(f32[13,16,128]{2,1,0:T(8,128)S(1)} %get-tuple-element.129), channel_id=1, source_target_pairs={{0,16},{16,0},{32,48},{48,32},{64,80},{80,64},{96,112},{112,96},{1... | collective-permute-start | bytes 319496 | tf_op jit(solution)/shard_map/ppermute | solution.py:603
  22.4 10.9 %collective-permute-start.2 = (f32[13,16,128]{2,1,0:T(8,128)S(1)}, f32[13,16,128]{2,1,0:T(8,128)S(1)}, u32[]{:S(2)}, u32[]{:S(2)}) collective-permute-start(f32[13,16,128]{2,1,0:T(8,128)S(1)} %get-tuple-element.130), channel_id=1, source_target_pairs={{16,32},{32,16},{48,64},{64,48},{80,96},{96,80},{112,128},{128,112... | collective-permute-start | bytes 319496 | tf_op jit(solution)/shard_map/ppermute | solution.py:603
  28.7 10.7 %collective-permute-start.10 = (f32[11,16,128]{2,1,0:T(8,128)S(1)}, f32[11,16,128]{2,1,0:T(8,128)S(1)}, u32[]{:S(2)}, u32[]{:S(2)}) collective-permute-start(f32[11,16,128]{2,1,0:T(8,128)S(1)} %get-tuple-element.181), channel_id=1, source_target_pairs={{0,16},{16,0},{32,48},{48,32},{64,80},{80,64},{96,112},{112,96},{1... | collective-permute-start | bytes 270344 | tf_op jit(solution)/shard_map/ppermute | solution.py:603
  28.9 10.6 %collective-permute-start.11 = (f32[11,16,128]{2,1,0:T(8,128)S(1)}, f32[11,16,128]{2,1,0:T(8,128)S(1)}, u32[]{:S(2)}, u32[]{:S(2)}) collective-permute-start(f32[11,16,128]{2,1,0:T(8,128)S(1)} %get-tuple-element.182), channel_id=1, source_target_pairs={{16,32},{32,16},{48,64},{64,48},{80,96},{96,80},{112,128},{128,112... | collective-permute-start | bytes 270344 | tf_op jit(solution)/shard_map/ppermute | solution.py:603
  35.7 9.6 %collective-permute-start.3 = (f32[11,16,128]{2,1,0:T(8,128)S(1)}, f32[11,16,128]{2,1,0:T(8,128)S(1)}, u32[]{:S(2)}, u32[]{:S(2)}) collective-permute-start(f32[11,16,128]{2,1,0:T(8,128)S(1)} %get-tuple-element.140), channel_id=1, source_target_pairs={{0,16},{16,0},{32,48},{48,32},{64,80},{80,64},{96,112},{112,96},{1... | collective-permute-start | bytes 270344 | tf_op jit(solution)/shard_map/ppermute | solution.py:603
  36.0 9.4 %collective-permute-start.4 = (f32[11,16,128]{2,1,0:T(8,128)S(1)}, f32[11,16,128]{2,1,0:T(8,128)S(1)}, u32[]{:S(2)}, u32[]{:S(2)}) collective-permute-start(f32[11,16,128]{2,1,0:T(8,128)S(1)} %get-tuple-element.141), channel_id=1, source_target_pairs={{16,32},{32,16},{48,64},{64,48},{80,96},{96,80},{112,128},{128,112... | collective-permute-start | bytes 270344 | tf_op jit(solution)/shard_map/ppermute | solution.py:603
  41.5 11.3 %collective-permute-start.12 = (f32[11,16,128]{2,1,0:T(8,128)S(1)}, f32[11,16,128]{2,1,0:T(8,128)S(1)}, u32[]{:S(2)}, u32[]{:S(2)}) collective-permute-start(f32[11,16,128]{2,1,0:T(8,128)S(1)} %get-tuple-element.191), channel_id=1, source_target_pairs={{0,16},{16,0},{32,48},{48,32},{64,80},{80,64},{96,112},{112,96},{1... | collective-permute-start | bytes 270344 | tf_op jit(solution)/shard_map/ppermute | solution.py:603
  43.8 9.0 %collective-permute-start.13 = (f32[11,16,128]{2,1,0:T(8,128)S(1)}, f32[11,16,128]{2,1,0:T(8,128)S(1)}, u32[]{:S(2)}, u32[]{:S(2)}) collective-permute-start(f32[11,16,128]{2,1,0:T(8,128)S(1)} %get-tuple-element.192), channel_id=1, source_target_pairs={{16,32},{32,16},{48,64},{64,48},{80,96},{96,80},{112,128},{128,112... | collective-permute-start | bytes 270344 | tf_op jit(solution)/shard_map/ppermute | solution.py:603
  47.4 7.0 %collective-permute-start.5 = (f32[11,16,128]{2,1,0:T(8,128)S(1)}, f32[11,16,128]{2,1,0:T(8,128)S(1)}, u32[]{:S(2)}, u32[]{:S(2)}) collective-permute-start(f32[11,16,128]{2,1,0:T(8,128)S(1)} %get-tuple-element.150), channel_id=1, source_target_pairs={{0,16},{16,0},{32,48},{48,32},{64,80},{80,64},{96,112},{112,96},{1... | collective-permute-start | bytes 270344 | tf_op jit(solution)/shard_map/ppermute | solution.py:603
  50.0 8.1 %collective-permute-start.6 = (f32[11,16,128]{2,1,0:T(8,128)S(1)}, f32[11,16,128]{2,1,0:T(8,128)S(1)}, u32[]{:S(2)}, u32[]{:S(2)}) collective-permute-start(f32[11,16,128]{2,1,0:T(8,128)S(1)} %get-tuple-element.151), channel_id=1, source_target_pairs={{16,32},{32,16},{48,64},{64,48},{80,96},{96,80},{112,128},{128,112... | collective-permute-start | bytes 270344 | tf_op jit(solution)/shard_map/ppermute | solution.py:603
where the time goes:
time: 61.4 us; the launch traced here: 61.2 us
  starting transfers between devices  34.3 us (56%)
  Pallas kernels  20.6 us (34%)
  waiting for transfers between devices  4.54 us (7%)
  between operations  0.96 us (2%)
  local copies, waits for them, and re-layouts  0.79 us (1%)
    ppermute x12, starting transfers between devices, exchanged(): swapped.append(lax.ppermute(message, 'gx', pairs))  30.4 us
    pallas_call x10, Pallas kernels, call(): pl.pallas_call(kernel, out_shape=outs, in_specs=specs or [FULL] * len(arg...  20.6 us
    ppermute x2, starting transfers between devices, shifted(): lax.ppermute(value, axis, [(source, (source + steps) % count) for source...  3.92 us
    ppermute x12, waiting for transfers between devices, exchanged(): swapped.append(lax.ppermute(message, 'gx', pairs))  3.65 us
  transfers between devices with their start and end apart: 14, of which 2 were waited for; matrix products, arithmetic and copies ran while one was open for 0% of the time, Pallas kernels for 24%

commit v1 on v0

--- a/solution.py
+++ b/solution.py
@@ -118,8 +118,8 @@
 
 def pack_y_kernel(*refs):
     fields, (material, ce_in, ch_in, cmat_in, prior_in) = refs[0:5], refs[5:10]
-    to_left, to_right, ce, ch, cmat, prior = refs[10:16]
-    firsts, lasts, mats, sems = refs[16:20]
+    to_first, to_second, firsts, lasts, mats, ce, ch, cmat, prior, sems = refs[10:20]
+    even = lax.rem(lax.axis_index("gy"), 2) == 0
     pairs = []
     for a in range(5):
         pairs.append((fields[a].at[:, :, :, 0:128], firsts.at[a]))
@@ -152,8 +152,8 @@
             pair = tuple(jnp.where(keep, old, new) for old, new in zip(built[plane], pair))
         built[plane] = pair
     for plane, (one, other) in built.items():
-        to_left[plane] = one
-        to_right[plane] = other
+        to_first[plane] = jnp.where(even, other, one)
+        to_second[plane] = jnp.where(even, one, other)
 
 
 def with_ghosts(half, message, key, tile):
@@ -165,10 +165,10 @@
 
 
 def load_kernel(*refs):
-    own, material_in, tab = refs[0:5], refs[5], refs[6]
-    states = (refs[7:12], refs[12:17])
-    c_halves, mat_halves = refs[17:19], refs[19:21]
-    material, sems = refs[21:23]
+    own, material_in, coarse_in, tab = refs[0:5], refs[5], refs[6:10], refs[10]
+    states = (refs[11:16], refs[16:21])
+    c_halves, mat_halves, coarse = refs[21:23], refs[23:25], refs[25:29]
+    material, sems = refs[29:31]
     first = pltpu.make_async_copy(material_in, material, sems.at[10])
     first.start()
     copies = []
@@ -177,6 +177,9 @@
             source = own[a].at[:, :, :, 128 * half : 128 * half + W]
             copies.append(pltpu.make_async_copy(source, states[half][a], sems.at[5 * half + a]))
             copies[-1].start()
+    for i, (source, target) in enumerate(zip(coarse_in, coarse)):
+        copies.append(pltpu.make_async_copy(source, target, sems.at[11 + i]))
+        copies[-1].start()
     first.wait()
     for x in range(ROWS):
         for half in range(2):
@@ -377,8 +380,13 @@
 
 
 def start_kernel(half, *refs):
-    fields_in, (c_in, mat_in, ce_in, ch_in, cmat, prior, tab, message) = refs[0:5], refs[5:13]
-    fields, (c, ce, ch, inv, pl_ref, to_first, to_second, mat) = refs[13:18], refs[18:26]
+    fields_in, (c_in, mat_in, ce_in, ch_in, cmat, prior, tab) = refs[0:5], refs[5:12]
+    received, fields = refs[12:14], refs[14:19]
+    c, ce, ch, inv, pl_ref, to_first, to_second, mat, message = refs[19:28]
+    even = lax.rem(lax.axis_index("gy"), 2) == 0
+    swap = even if half == 0 else jnp.logical_not(even)
+    for plane in range(Y_PLANES):
+        message[plane] = jnp.where(swap, received[1][plane], received[0][plane])
     outer = slice(128, 256) if half == 0 else slice(0, 128)
     inner = slice(0, 128) if half == 0 else slice(128, 256)
     for x in range(ROWS):
@@ -411,7 +419,7 @@
     send_edges(half, True, fields, c, ce, ch, pl_ref, mat, to_first, to_second)
 
 
-def coarse_step(half, first, olds, news, c, ghost, olds_c, news_c, inv, pl_ref, from_left, from_right):
+def coarse_step(half, first, olds, news, c, ghost, olds_c, news_c, inv, pl_ref, from_left, from_right, finished=None):
     e_items, h_items = x_items(first)
     zero = jnp.zeros((Z, W), F32)
     flat = (0.0, 0.0)
@@ -426,6 +434,8 @@
         coarse_h.append(h_row(row_of(ch0, r), coarse_e0[r], following, flat))
         for k in range(3):
             ch[k, r] = coarse_h[r][k]
+    if finished:
+        finished(-2)
 
     ge = gh = he = hh = None
     summed = [[None] * CROWS for _ in range(2)]
@@ -464,6 +474,8 @@
                 summed[k][x // RATIO] = part if have is None else have + part
             preceding = h[1:]
             current = upper
+            if finished and t == RATIO - 1:
+                finished(x)
         if t == 0:
             (a, b), (a2, b2) = [[ghost[k, side] for k in range(2)] for side in range(2)]
             ge = [
@@ -488,6 +500,8 @@
         for k in range(3):
             ce[k, r] = coarse_e0[r][k] + inv[r] * curl[k]
         preceding = coarse_h[r][1:]
+    if finished:
+        finished(-1)
 
 
 def ghost_coefficients(half, ghost, tab, from_left, from_right):
@@ -519,34 +533,52 @@
 def final_kernel(half, *refs):
     olds, rest = refs[0:5], refs[5:]
     c, ce0, ch0, inv, pl0, ghost = rest[0:6]
-    from_left, from_right = sort_messages(rest[6:8], rest[-2:])
+    received, rest = rest[6:8], rest[8:]
     if half == 0:
-        news, (ce, ch) = rest[8:13], rest[13:15]
+        outs, news, ce, ch = rest[0:5], rest[5:10], rest[10], rest[11]
+        rest = rest[12:]
     else:
-        others, others_c = rest[8:13], rest[13:15]
-        outs, outs_c = rest[15:20], rest[20:22]
-        news, (ce, ch) = rest[22:27], rest[27:29]
-    coarse_step(half, False, olds, news, c, ghost, (ce0, ch0), (ce, ch), inv, pl0, from_left, from_right)
-    if half == 0:
-        return
+        others, others_c = rest[5:10], rest[10:12]
+        outs, outs_c, news, ce, ch = rest[12:17], rest[17:19], rest[19:24], rest[24], rest[25]
+        coarse_parts = rest[26:28]
+        rest = rest[28:]
+    sorted_refs, sems = rest[0:2], rest[2]
+    from_left, from_right = sort_messages(received, sorted_refs)
     first = lanes((Z, 128)) < 64
-    for a in range(5):
-        for k in range(3):
-            for x in range(ROWS):
-                outs[a][k, x, :, 0:128] = others[a][k, x, :, 0:128]
-                outs[a][k, x, :, 128:256] = jnp.where(
-                    first, others[a][k, x, :, 128:256], news[a][k, x, :, 0:128]
-                )
-                outs[a][k, x, :, 256:384] = news[a][k, x, :, 128:256]
-    for other, source, target in zip(others_c, (ce, ch), outs_c):
+    copies = []
+
+    def coarse_finished(a):
+        if half == 0:
+            return
         for k in range(3):
             for r in range(CROWS):
-                target[k, pl.ds(r, Z, stride=CROWS), :] = jnp.where(first, other[k, r], source[k, r])
-
-
-def shifted(value, axis, steps):
-    count = lax.axis_size(axis)
-    return lax.ppermute(value, axis, [(source, (source + steps) % count) for source in range(count)])
+                value = jnp.where(first, others_c[a][k, r], (ce, ch)[a][k, r])
+                coarse_parts[a][k, pl.ds(r, Z, stride=CROWS), :] = value
+        copies.append(pltpu.make_async_copy(coarse_parts[a], outs_c[a], sems.at[ROWS, a]))
+        copies[-1].start()
+
+    def finished(x):
+        if x < 0:
+            return coarse_finished(-x - 1)
+        for a in range(5):
+            if half == 0:
+                source = news[a].at[:, x, :, 0:128]
+                target = outs[a].at[:, x, :, 0:128]
+            else:
+                for k in range(3):
+                    news[a][k, x, :, 0:128] = jnp.where(
+                        first, others[a][k, x, :, 128:256], news[a][k, x, :, 0:128]
+                    )
+                source = news[a].at[:, x]
+                target = outs[a].at[:, x, :, 128:384]
+            copies.append(pltpu.make_async_copy(source, target, sems.at[x, a]))
+            copies[-1].start()
+
+    coarse_step(
+        half, False, olds, news, c, ghost, (ce0, ch0), (ce, ch), inv, pl0, from_left, from_right, finished
+    )
+    for copy in copies:
+        copy.wait()
 
 
 FULL = pl.BlockSpec(memory_space=pltpu.VMEM)
@@ -558,13 +590,13 @@
 PLANES = (8, W)
 
 
-def call(kernel, outs, args, specs=None, scratch=(), aliases=None, vmem=16):
+def call(kernel, outs, args, specs=None, scratch=(), aliases=None, vmem=16, out_specs=None):
     outs = [dims if isinstance(dims, jax.ShapeDtypeStruct) else jax.ShapeDtypeStruct(dims, F32) for dims in outs]
     return pl.pallas_call(
         kernel,
         out_shape=outs,
         in_specs=specs or [FULL] * len(args),
-        out_specs=[FULL] * len(outs),
+        out_specs=out_specs or [FULL] * len(outs),
         scratch_shapes=list(scratch),
         input_output_aliases=aliases or {},
         compiler_params=pltpu.CompilerParams(vmem_limit_bytes=vmem * 1024 * 1024),
@@ -595,12 +627,12 @@
     return [(x_places(half, items)[1], Z, 128) for items in x_items(first)]
 
 
-def exchanged(messages):
-    count = lax.axis_size("gx")
+def exchanged(messages, axis):
+    count = lax.axis_size(axis)
     swapped = []
     for message, first in zip(messages, (0, 1)):
         pairs = [((first + i) % count, (first + (i ^ 1)) % count) for i in range(count)]
-        swapped.append(lax.ppermute(message, "gx", pairs))
+        swapped.append(lax.ppermute(message, axis, pairs))
     return swapped
 
 
@@ -631,31 +663,39 @@
     ch = coarse_h.reshape(3, Z * CROWS, 128)
     cmat = coarse_material.reshape(Z * CROWS, 128)
     prior = coarse_prior.reshape(2 * CROWS, 128)
+    in_hbm = lambda values: [pltpu.with_memory_space_constraint(value, pltpu.HBM) for value in values]
+    fields, coarse = in_hbm(fields), in_hbm([ce, ch, cmat, prior])
+    (mat,) = in_hbm([mat])
     tab = table(permittivity, plasma, damping, strength, resonance, linewidth)
 
     vmem = lambda *dims: pltpu.VMEM(dims, F32)
-    ints = lambda *dims: jax.ShapeDtypeStruct(dims, jnp.int32)
-    to_left, to_right, ce, ch, cmat, prior = call(
+    packed = call(
         pack_y_kernel,
-        [(Y_PLANES, Z, 128)] * 2 + [ce.shape, ch.shape, ints(*cmat.shape), prior.shape],
-        [*fields, mat, ce, ch, cmat, prior],
+        [(Y_PLANES, Z, 128)] * 2,
+        [*fields, mat, *coarse],
         [RAW] * 10,
         [
             vmem(5, 3, ROWS, Z, 128),
             vmem(5, 3, ROWS, Z, 128),
             pltpu.VMEM((2, ROWS, Z, 128), jnp.int32),
+            vmem(*ce.shape),
+            vmem(*ch.shape),
+            pltpu.VMEM(cmat.shape, jnp.int32),
+            vmem(*prior.shape),
             pltpu.SemaphoreType.DMA((16,)),
         ],
-        vmem=61,
+        vmem=16,
     )
-    from_right = shifted(to_left, "gy", -1)
-    from_left = shifted(to_right, "gy", 1)
+    received = exchanged(packed, "gy")
     loaded = call(
         load_kernel,
-        [FIELD] * 10 + [COEF] * 2 + [(ROWS, Z, W)] * 2,
-        [*fields, mat, tab],
-        [RAW] * 6 + [FULL],
-        [pltpu.VMEM((ROWS, Z, OWN), jnp.int32), pltpu.SemaphoreType.DMA((11,))],
+        [FIELD] * 10
+        + [COEF] * 2
+        + [(ROWS, Z, W)] * 2
+        + [jax.ShapeDtypeStruct(value.shape, value.dtype) for value in coarse],
+        [*fields, mat, *coarse, tab],
+        [RAW] * 10 + [FULL],
+        [pltpu.VMEM((ROWS, Z, OWN), jnp.int32), pltpu.SemaphoreType.DMA((15,))],
     )
     parts, waiting = [None, None], [None, None]
     for half in range(2):
@@ -663,12 +703,12 @@
         out = call(
             functools.partial(start_kernel, half),
             [FIELD] * 5 + [COEF, COARSE, COARSE, (CROWS, Z, CW), PLANES] + message_shapes(half, True),
-            [*state, loaded[10 + half], loaded[12 + half], ce, ch, cmat, prior, tab, (from_left, from_right)[half]],
-            scratch=[vmem(ROWS, Z, W)],
+            [*state, loaded[10 + half], loaded[12 + half], *loaded[14:18], tab, *received],
+            scratch=[vmem(ROWS, Z, W), vmem(Y_PLANES, Z, 128)],
             aliases={index: index for index in range(6)},
         )
         parts[half] = (out[0:5], out[5:10], tab)
-        waiting[half] = exchanged(out[10:12])
+        waiting[half] = exchanged(out[10:12], "gx")
     for step in range(STEPS - 1):
         for half in range(2):
             state, (c, ce, ch, inv, planes), ghost = parts[half]
@@ -684,16 +724,22 @@
             if step == 0:
                 ghost = out[10]
             parts[half] = (out[0:5], (c, out[5], out[6], inv, out[7]), ghost)
-            waiting[half] = exchanged(out[8:10])
+            waiting[half] = exchanged(out[8:10], "gx")
+    whole = [(3, ROWS, Z, OWN)] * 5
     done = []
     for half in range(2):
         state, coarse, ghost = parts[half]
+        args = [*state, *coarse, ghost, *waiting[half], *done]
         done = call(
             functools.partial(final_kernel, half),
-            [FIELD] * 5 + [COARSE] * 2 if half == 0 else [(3, ROWS, Z, OWN)] * 5 + [(3, Z * CROWS, 128)] * 2,
-            [*state, *coarse, ghost, *waiting[half], *done],
-            scratch=([vmem(*FIELD)] * 5 + [vmem(*COARSE)] * 2 if half else [])
-            + [vmem(*message.shape) for message in waiting[half]],
+            whole + ([(3, Z * CROWS, 128)] * 2 if half else [FIELD] * 5 + [COARSE] * 2),
+            args,
+            specs=[RAW if 13 <= i < 18 else FULL for i in range(len(args))],
+            out_specs=[RAW] * 7 if half else [RAW] * 5 + [FULL] * 7,
+            scratch=([vmem(*FIELD)] * 5 + [vmem(*COARSE)] * 2 + [vmem(3, Z * CROWS, 128)] * 2 if half else [])
+            + [vmem(*message.shape) for message in waiting[half]]
+            + [pltpu.SemaphoreType.DMA((ROWS + 1, 5))],
+            aliases={13 + i: i for i in range(5)} if half else None,
         )
     fine = [jnp.transpose(value, (0, 2, 1, 3)) for value in done[0:5]]
     coarse = [value.reshape(3, Z, CROWS, 128) for value in done[5:7]]

time: 61.4 us -> 59 us (0.961)
  waiting for transfers between devices: 4.54 us -> 3.64 us
  starting transfers between devices: 34.3 us -> 33.4 us
  local copies, waits for them, and re-layouts: 0.79 us -> 0.07 us
    ppermute x14, waiting for transfers between devices: 4.54 us -> 3.64 us  [exchanged(): swapped.append(lax.ppermute(message, axis, pairs))]
    ppermute x14, starting transfers between devices: 34.3 us -> 33.4 us  [exchanged(): swapped.append(lax.ppermute(message, axis, pairs))]
    unnamed x32 -> x12, local copies, waits for them, and re-layouts: 0.75 us -> 0.04 us
  transfers between devices with their start and end apart: 14 -> 14, of which waited for: 2 -> 2; matrix products, arithmetic and copies ran while one was open for 0% -> 0% of each run, Pallas kernels for 24% -> 25%
where the time goes in v1:
time: 59 us; the launch traced here: 58.9 us
  starting transfers between devices  33.4 us (57%)
  Pallas kernels  20.8 us (35%)
  waiting for transfers between devices  3.64 us (6%)
  between operations  1 us (2%)
    ppermute x14, starting transfers between devices, exchanged(): swapped.append(lax.ppermute(message, axis, pairs))  33.4 us
    pallas_call x10, Pallas kernels, call(): pl.pallas_call(kernel, out_shape=outs, in_specs=specs or [FULL] * len(arg...  20.8 us
    ppermute x14, waiting for transfers between devices, exchanged(): swapped.append(lax.ppermute(message, axis, pairs))  3.64 us
  transfers between devices with their start and end apart: 14, of which 2 were waited for; matrix products, arithmetic and copies ran while one was open for 0% of the time, Pallas kernels for 25%

profile of v1, /device:TPU:2, one launch (start us, length us, event | category | flops | bytes accessed | tf_op | source)
XLA Modules:
  0.0 58.9 jit_solution(6177833310520766998)
XLA Ops:
  0.6 2.1 %shard_map.208 = (f32[8,16,128]{2,1,0:T(8,128)S(1)}, f32[8,16,128]{2,1,0:T(8,128)S(1)}) custom-call(f32[3,6,16,384]{3,2,1,0:T(8,128)} %bitcast.28, f32[3,6,16,384]{3,2,1,0:T(8,128)} %bitcast.30, f32[3,6,16,384]{3,2,1,0:T(8,128)} %bitcast.32, f32[3,6,16,384]{3,2,1,0:T(8,128)} %bitcast.34, f32[3,6,16,384]{3,2,1,0:T(8,128)} %bitcast.36, ...), custom_call_target="tpu_custom_call" | custom-call | flops 4000000 | bytes 8000000 | tf_op jit(solution)/shard_map/pallas_call | solution.py:595
  2.8 0.0 copy-start.3
  2.8 0.0 copy-start.4
  2.8 0.0 copy-start
  2.8 0.0 copy-start.1
  2.8 0.0 copy-start.2
  2.8 0.1 collective-permute-start
  2.9 0.0 copy-start.5
  2.9 3.1 %collective-permute-start.1 = (f32[8,16,128]{2,1,0:T(8,128)S(1)}, f32[8,16,128]{2,1,0:T(8,128)S(1)}, u32[]{:S(2)}, u32[]{:S(2)}) collective-permute-start(f32[8,16,128]{2,1,0:T(8,128)S(1)} %get-tuple-element.124), channel_id=1, source_target_pairs={{1,2},{2,1},{3,4},{4,3},{5,6},{6,5},{7,8},{8,7},{9,10},{10,9},{11,... | collective-permute-start | bytes 196616 | tf_op jit(solution)/shard_map/ppermute | solution.py:635
  6.1 2.0 %shard_map.207 = (f32[3,6,16,256]{3,2,1,0:T(8,128)S(1)}, f32[3,6,16,256]{3,2,1,0:T(8,128)S(1)}, f32[3,6,16,256]{3,2,1,0:T(8,128)S(1)}, f32[3,6,16,256]{3,2,1,0:T...) custom-call(f32[3,6,16,384]{3,2,1,0:T(8,128)} %bitcast.29, ...), custom_call_target="tpu_custom_call" | custom-call | flops 4000000 | bytes 8000000 | tf_op jit(solution)/shard_map/pallas_call | solution.py:595
  8.1 0.7 %collective-permute-done.1.refs_13_ = f32[8,16,128]{2,1,0:T(8,128)S(1)} collective-permute-done((f32[8,16,128]{2,1,0:T(8,128)S(1)}, f32[8,16,128]{2,1,0:T(8,128)S(1)}, u32[]{:S(2)}, u32[]{:S(2)}) %collective-permute-start.1) | collective-permute-done | bytes 65568 | tf_op jit(solution)/shard_map/ppermute | solution.py:635
  8.8 1.5 %shard_map.212 = (f32[3,6,16,256]{3,2,1,0:T(8,128)S(1)}, f32[3,6,16,256]{3,2,1,0:T(8,128)S(1)}, f32[3,6,16,256]{3,2,1,0:T(8,128)S(1)}, f32[3,6,16,256]{3,2,1,0:T...) custom-call(f32[3,6,16,256]{3,2,1,0:T(8,128)S(1)} %get-tuple-element, ...), custom_call_target="tpu_custom_call", output_to_operand_aliasing={{0}: (0, {}), {1}: (1, {}), {2}: (2, {}), {3}: (3, {}), {4}... | custom-call | flops 4000000 | bytes 8000000 | tf_op jit(solution)/shard_map/pallas_call | solution.py:595
  10.3 2.2 %collective-permute-start.8 = (f32[13,16,128]{2,1,0:T(8,128)S(1)}, f32[13,16,128]{2,1,0:T(8,128)S(1)}, u32[]{:S(2)}, u32[]{:S(2)}) collective-permute-start(f32[13,16,128]{2,1,0:T(8,128)S(1)} %get-tuple-element.175), channel_id=1, source_target_pairs={{0,16},{16,0},{32,48},{48,32},{64,80},{80,64},{96,112},{112,96},{1... | collective-permute-start | bytes 319496 | tf_op jit(solution)/shard_map/ppermute | solution.py:635
  12.5 6.7 %collective-permute-start.9 = (f32[13,16,128]{2,1,0:T(8,128)S(1)}, f32[13,16,128]{2,1,0:T(8,128)S(1)}, u32[]{:S(2)}, u32[]{:S(2)}) collective-permute-start(f32[13,16,128]{2,1,0:T(8,128)S(1)} %get-tuple-element.176), channel_id=1, source_target_pairs={{16,32},{32,16},{48,64},{64,48},{80,96},{96,80},{112,128},{128,112... | collective-permute-start | bytes 319496 | tf_op jit(solution)/shard_map/ppermute | solution.py:635
  19.2 1.5 %shard_map.209 = (f32[3,6,16,256]{3,2,1,0:T(8,128)S(1)}, f32[3,6,16,256]{3,2,1,0:T(8,128)S(1)}, f32[3,6,16,256]{3,2,1,0:T(8,128)S(1)}, f32[3,6,16,256]{3,2,1,0:T...) custom-call(f32[3,6,16,256]{3,2,1,0:T(8,128)S(1)} %get-tuple-element, ...), custom_call_target="tpu_custom_call", output_to_operand_aliasing={{0}: (0, {}), {1}: (1, {}), {2}: (2, {}), {3}: (3, {}), {4}... | custom-call | flops 4000000 | bytes 8000000 | tf_op jit(solution)/shard_map/pallas_call | solution.py:595
  20.7 0.1 collective-permute-start.2
  20.8 4.0 %collective-permute-start.3 = (f32[13,16,128]{2,1,0:T(8,128)S(1)}, f32[13,16,128]{2,1,0:T(8,128)S(1)}, u32[]{:S(2)}, u32[]{:S(2)}) collective-permute-start(f32[13,16,128]{2,1,0:T(8,128)S(1)} %get-tuple-element.136), channel_id=1, source_target_pairs={{16,32},{32,16},{48,64},{64,48},{80,96},{96,80},{112,128},{128,112... | collective-permute-start | bytes 319496 | tf_op jit(solution)/shard_map/ppermute | solution.py:635
  24.7 2.4 %shard_map.213 = (f32[3,6,16,256]{3,2,1,0:T(8,128)S(1)}, f32[3,6,16,256]{3,2,1,0:T(8,128)S(1)}, f32[3,6,16,256]{3,2,1,0:T(8,128)S(1)}, f32[3,6,16,256]{3,2,1,0:T...) custom-call(f32[3,6,16,256]{3,2,1,0:T(8,128)S(1)} %get-tuple-element, ...), custom_call_target="tpu_custom_call" | custom-call | flops 4000000 | bytes 8000000 | tf_op jit(solution)/shard_map/pallas_call | solution.py:595
  27.1 0.1 collective-permute-start.10
  27.2 4.7 %collective-permute-start.11 = (f32[11,16,128]{2,1,0:T(8,128)S(1)}, f32[11,16,128]{2,1,0:T(8,128)S(1)}, u32[]{:S(2)}, u32[]{:S(2)}) collective-permute-start(f32[11,16,128]{2,1,0:T(8,128)S(1)} %get-tuple-element.187), channel_id=1, source_target_pairs={{16,32},{32,16},{48,64},{64,48},{80,96},{96,80},{112,128},{128,112... | collective-permute-start | bytes 270344 | tf_op jit(solution)/shard_map/ppermute | solution.py:635
  31.9 2.3 %shard_map.210 = (f32[3,6,16,256]{3,2,1,0:T(8,128)S(1)}, f32[3,6,16,256]{3,2,1,0:T(8,128)S(1)}, f32[3,6,16,256]{3,2,1,0:T(8,128)S(1)}, f32[3,6,16,256]{3,2,1,0:T...) custom-call(f32[3,6,16,256]{3,2,1,0:T(8,128)S(1)} %get-tuple-element, ...), custom_call_target="tpu_custom_call" | custom-call | flops 4000000 | bytes 8000000 | tf_op jit(solution)/shard_map/pallas_call | solution.py:595
  34.3 0.1 collective-permute-start.4
  34.4 3.2 %collective-permute-start.5 = (f32[11,16,128]{2,1,0:T(8,128)S(1)}, f32[11,16,128]{2,1,0:T(8,128)S(1)}, u32[]{:S(2)}, u32[]{:S(2)}) collective-permute-start(f32[11,16,128]{2,1,0:T(8,128)S(1)} %get-tuple-element.147), channel_id=1, source_target_pairs={{16,32},{32,16},{48,64},{64,48},{80,96},{96,80},{112,128},{128,112... | collective-permute-start | bytes 270344 | tf_op jit(solution)/shard_map/ppermute | solution.py:635
  37.6 2.1 %shard_map.214 = (f32[3,6,16,256]{3,2,1,0:T(8,128)S(1)}, f32[3,6,16,256]{3,2,1,0:T(8,128)S(1)}, f32[3,6,16,256]{3,2,1,0:T(8,128)S(1)}, f32[3,6,16,256]{3,2,1,0:T...) custom-call(f32[3,6,16,256]{3,2,1,0:T(8,128)S(1)} %get-tuple-element, ...), custom_call_target="tpu_custom_call" | custom-call | flops 4000000 | bytes 8000000 | tf_op jit(solution)/shard_map/pallas_call | solution.py:595
  39.8 2.2 %collective-permute-start.12 = (f32[11,16,128]{2,1,0:T(8,128)S(1)}, f32[11,16,128]{2,1,0:T(8,128)S(1)}, u32[]{:S(2)}, u32[]{:S(2)}) collective-permute-start(f32[11,16,128]{2,1,0:T(8,128)S(1)} %get-tuple-element.196), channel_id=1, source_target_pairs={{0,16},{16,0},{32,48},{48,32},{64,80},{80,64},{96,112},{112,96},{1... | collective-permute-start | bytes 270344 | tf_op jit(solution)/shard_map/ppermute | solution.py:635
  42.0 1.7 %collective-permute-start.13 = (f32[11,16,128]{2,1,0:T(8,128)S(1)}, f32[11,16,128]{2,1,0:T(8,128)S(1)}, u32[]{:S(2)}, u32[]{:S(2)}) collective-permute-start(f32[11,16,128]{2,1,0:T(8,128)S(1)} %get-tuple-element.197), channel_id=1, source_target_pairs={{16,32},{32,16},{48,64},{64,48},{80,96},{96,80},{112,128},{128,112... | collective-permute-start | bytes 270344 | tf_op jit(solution)/shard_map/ppermute | solution.py:635
  43.7 2.1 %shard_map.211 = (f32[3,6,16,256]{3,2,1,0:T(8,128)S(1)}, f32[3,6,16,256]{3,2,1,0:T(8,128)S(1)}, f32[3,6,16,256]{3,2,1,0:T(8,128)S(1)}, f32[3,6,16,256]{3,2,1,0:T...) custom-call(f32[3,6,16,256]{3,2,1,0:T(8,128)S(1)} %get-tuple-element, ...), custom_call_target="tpu_custom_call" | custom-call | flops 4000000 | bytes 8000000 | tf_op jit(solution)/shard_map/pallas_call | solution.py:595
  45.8 2.4 %collective-permute-start.6 = (f32[11,16,128]{2,1,0:T(8,128)S(1)}, f32[11,16,128]{2,1,0:T(8,128)S(1)}, u32[]{:S(2)}, u32[]{:S(2)}) collective-permute-start(f32[11,16,128]{2,1,0:T(8,128)S(1)} %get-tuple-element.156), channel_id=1, source_target_pairs={{0,16},{16,0},{32,48},{48,32},{64,80},{80,64},{96,112},{112,96},{1... | collective-permute-start | bytes 270344 | tf_op jit(solution)/shard_map/ppermute | solution.py:635
  48.2 2.9 %collective-permute-start.7 = (f32[11,16,128]{2,1,0:T(8,128)S(1)}, f32[11,16,128]{2,1,0:T(8,128)S(1)}, u32[]{:S(2)}, u32[]{:S(2)}) collective-permute-start(f32[11,16,128]{2,1,0:T(8,128)S(1)} %get-tuple-element.157), channel_id=1, source_target_pairs={{16,32},{32,16},{48,64},{64,48},{80,96},{96,80},{112,128},{128,112... | collective-permute-start | bytes 270344 | tf_op jit(solution)/shard_map/ppermute | solution.py:635
  51.1 2.3 %shard_map.215 = (f32[3,6,16,384]{3,2,1,0:T(8,128)}, f32[3,6,16,384]{3,2,1,0:T(8,128)}, f32[3,6,16,384]{3,2,1,0:T(8,128)}, f32[3,6,16,384]{3,2,1,0:T(8,128)}, f3...) custom-call(f32[3,6,16,256]{3,2,1,0:T(8,128)S(1)} %get-tuple-element, ...), custom_call_target="tpu_custom_call" | custom-call | flops 4000000 | bytes 8000000 | tf_op jit(solution)/shard_map/pallas_call | solution.py:595
  53.4 2.9 %collective-permute-done.7.refs_12_ = f32[11,16,128]{2,1,0:T(8,128)S(1)} collective-permute-done((f32[11,16,128]{2,1,0:T(8,128)S(1)}, f32[11,16,128]{2,1,0:T(8,128)S(1)}, u32[]{:S(2)}, u32[]{:S(2)}) %collective-permute-start.7) | collective-permute-done | bytes 90144 | tf_op jit(solution)/shard_map/ppermute | solution.py:635
  56.4 2.4 %shard_map.216 = (f32[3,6,16,384]{3,2,1,0:T(8,128)}, f32[3,6,16,384]{3,2,1,0:T(8,128)}, f32[3,6,16,384]{3,2,1,0:T(8,128)}, f32[3,6,16,384]{3,2,1,0:T(8,128)}, f3...) custom-call(f32[3,6,16,256]{3,2,1,0:T(8,128)S(1)} %get-tuple-element, ...), custom_call_target="tpu_custom_call", output_to_operand_aliasing={{0}: (13, {}), {1}: (14, {}), {2}: (15, {}), {3}: (16, {}),... | custom-call | flops 4000000 | bytes 8000000 | tf_op jit(solution)/shard_map/pallas_call | solution.py:595
  (22 shorter events, 0.1 us)
Async XLA Ops:
  2.8 3.3 %copy-start.3 = (f32[8]{0:T(128)S(1)}, f32[8]{0:T(128)}, u32[]{:S(2)}) copy-start(f32[8]{0:T(128)} %param.24) | copy-start | bytes 100
  2.8 3.2 %copy-start.4 = (f32[8]{0:T(128)S(1)}, f32[8]{0:T(128)}, u32[]{:S(2)}) copy-start(f32[8]{0:T(128)} %param.23) | copy-start | bytes 100
  2.8 3.2 %copy-start = (f32[8]{0:T(128)S(1)}, f32[8]{0:T(128)}, u32[]{:S(2)}) copy-start(f32[8]{0:T(128)} %param.25) | copy-start | bytes 100
  2.8 3.2 %copy-start.1 = (f32[8]{0:T(128)S(1)}, f32[8]{0:T(128)}, u32[]{:S(2)}) copy-start(f32[8]{0:T(128)} %param.27) | copy-start | bytes 100
  2.8 3.2 %copy-start.2 = (f32[8]{0:T(128)S(1)}, f32[8]{0:T(128)}, u32[]{:S(2)}) copy-start(f32[8]{0:T(128)} %param.26) | copy-start | bytes 100
  2.8 5.3 %collective-permute-start = (f32[8,16,128]{2,1,0:T(8,128)S(1)}, f32[8,16,128]{2,1,0:T(8,128)S(1)}, u32[]{:S(2)}, u32[]{:S(2)}) collective-permute-start(f32[8,16,128]{2,1,0:T(8,128)S(1)} %get-tuple-element.123), channel_id=1, source_target_pairs={{0,1},{1,0},{2,3},{3,2},{4,5},{5,4},{6,7},{7,6},{8,9},{9,8},{10,11... | collective-permute-start | bytes 196616 | tf_op jit(solution)/shard_map/ppermute | solution.py:635
  2.9 3.1 %copy-start.5 = (f32[8]{0:T(128)S(1)}, f32[8]{0:T(128)}, u32[]{:S(2)}) copy-start(f32[8]{0:T(128)} %param.22) | copy-start | bytes 100
  2.9 5.9 %collective-permute-start.1 = (f32[8,16,128]{2,1,0:T(8,128)S(1)}, f32[8,16,128]{2,1,0:T(8,128)S(1)}, u32[]{:S(2)}, u32[]{:S(2)}) collective-permute-start(f32[8,16,128]{2,1,0:T(8,128)S(1)} %get-tuple-element.124), channel_id=1, source_target_pairs={{1,2},{2,1},{3,4},{4,3},{5,6},{6,5},{7,8},{8,7},{9,10},{10,9},{11,... | collective-permute-start | bytes 196616 | tf_op jit(solution)/shard_map/ppermute | solution.py:635
  10.3 14.4 %collective-permute-start.8 = (f32[13,16,128]{2,1,0:T(8,128)S(1)}, f32[13,16,128]{2,1,0:T(8,128)S(1)}, u32[]{:S(2)}, u32[]{:S(2)}) collective-permute-start(f32[13,16,128]{2,1,0:T(8,128)S(1)} %get-tuple-element.175), channel_id=1, source_target_pairs={{0,16},{16,0},{32,48},{48,32},{64,80},{80,64},{96,112},{112,96},{1... | collective-permute-start | bytes 319496 | tf_op jit(solution)/shard_map/ppermute | solution.py:635
  12.5 12.2 %collective-permute-start.9 = (f32[13,16,128]{2,1,0:T(8,128)S(1)}, f32[13,16,128]{2,1,0:T(8,128)S(1)}, u32[]{:S(2)}, u32[]{:S(2)}) collective-permute-start(f32[13,16,128]{2,1,0:T(8,128)S(1)} %get-tuple-element.176), channel_id=1, source_target_pairs={{16,32},{32,16},{48,64},{64,48},{80,96},{96,80},{112,128},{128,112... | collective-permute-start | bytes 319496 | tf_op jit(solution)/shard_map/ppermute | solution.py:635
  20.7 11.3 %collective-permute-start.2 = (f32[13,16,128]{2,1,0:T(8,128)S(1)}, f32[13,16,128]{2,1,0:T(8,128)S(1)}, u32[]{:S(2)}, u32[]{:S(2)}) collective-permute-start(f32[13,16,128]{2,1,0:T(8,128)S(1)} %get-tuple-element.135), channel_id=1, source_target_pairs={{0,16},{16,0},{32,48},{48,32},{64,80},{80,64},{96,112},{112,96},{1... | collective-permute-start | bytes 319496 | tf_op jit(solution)/shard_map/ppermute | solution.py:635
  20.8 11.2 %collective-permute-start.3 = (f32[13,16,128]{2,1,0:T(8,128)S(1)}, f32[13,16,128]{2,1,0:T(8,128)S(1)}, u32[]{:S(2)}, u32[]{:S(2)}) collective-permute-start(f32[13,16,128]{2,1,0:T(8,128)S(1)} %get-tuple-element.136), channel_id=1, source_target_pairs={{16,32},{32,16},{48,64},{64,48},{80,96},{96,80},{112,128},{128,112... | collective-permute-start | bytes 319496 | tf_op jit(solution)/shard_map/ppermute | solution.py:635
  27.1 10.5 %collective-permute-start.10 = (f32[11,16,128]{2,1,0:T(8,128)S(1)}, f32[11,16,128]{2,1,0:T(8,128)S(1)}, u32[]{:S(2)}, u32[]{:S(2)}) collective-permute-start(f32[11,16,128]{2,1,0:T(8,128)S(1)} %get-tuple-element.186), channel_id=1, source_target_pairs={{0,16},{16,0},{32,48},{48,32},{64,80},{80,64},{96,112},{112,96},{1... | collective-permute-start | bytes 270344 | tf_op jit(solution)/shard_map/ppermute | solution.py:635
  27.2 10.4 %collective-permute-start.11 = (f32[11,16,128]{2,1,0:T(8,128)S(1)}, f32[11,16,128]{2,1,0:T(8,128)S(1)}, u32[]{:S(2)}, u32[]{:S(2)}) collective-permute-start(f32[11,16,128]{2,1,0:T(8,128)S(1)} %get-tuple-element.187), channel_id=1, source_target_pairs={{16,32},{32,16},{48,64},{64,48},{80,96},{96,80},{112,128},{128,112... | collective-permute-start | bytes 270344 | tf_op jit(solution)/shard_map/ppermute | solution.py:635
  34.3 9.4 %collective-permute-start.4 = (f32[11,16,128]{2,1,0:T(8,128)S(1)}, f32[11,16,128]{2,1,0:T(8,128)S(1)}, u32[]{:S(2)}, u32[]{:S(2)}) collective-permute-start(f32[11,16,128]{2,1,0:T(8,128)S(1)} %get-tuple-element.146), channel_id=1, source_target_pairs={{0,16},{16,0},{32,48},{48,32},{64,80},{80,64},{96,112},{112,96},{1... | collective-permute-start | bytes 270344 | tf_op jit(solution)/shard_map/ppermute | solution.py:635
  34.4 9.3 %collective-permute-start.5 = (f32[11,16,128]{2,1,0:T(8,128)S(1)}, f32[11,16,128]{2,1,0:T(8,128)S(1)}, u32[]{:S(2)}, u32[]{:S(2)}) collective-permute-start(f32[11,16,128]{2,1,0:T(8,128)S(1)} %get-tuple-element.147), channel_id=1, source_target_pairs={{16,32},{32,16},{48,64},{64,48},{80,96},{96,80},{112,128},{128,112... | collective-permute-start | bytes 270344 | tf_op jit(solution)/shard_map/ppermute | solution.py:635
  39.8 11.3 %collective-permute-start.12 = (f32[11,16,128]{2,1,0:T(8,128)S(1)}, f32[11,16,128]{2,1,0:T(8,128)S(1)}, u32[]{:S(2)}, u32[]{:S(2)}) collective-permute-start(f32[11,16,128]{2,1,0:T(8,128)S(1)} %get-tuple-element.196), channel_id=1, source_target_pairs={{0,16},{16,0},{32,48},{48,32},{64,80},{80,64},{96,112},{112,96},{1... | collective-permute-start | bytes 270344 | tf_op jit(solution)/shard_map/ppermute | solution.py:635
  42.0 9.1 %collective-permute-start.13 = (f32[11,16,128]{2,1,0:T(8,128)S(1)}, f32[11,16,128]{2,1,0:T(8,128)S(1)}, u32[]{:S(2)}, u32[]{:S(2)}) collective-permute-start(f32[11,16,128]{2,1,0:T(8,128)S(1)} %get-tuple-element.197), channel_id=1, source_target_pairs={{16,32},{32,16},{48,64},{64,48},{80,96},{96,80},{112,128},{128,112... | collective-permute-start | bytes 270344 | tf_op jit(solution)/shard_map/ppermute | solution.py:635
  45.8 7.6 %collective-permute-start.6 = (f32[11,16,128]{2,1,0:T(8,128)S(1)}, f32[11,16,128]{2,1,0:T(8,128)S(1)}, u32[]{:S(2)}, u32[]{:S(2)}) collective-permute-start(f32[11,16,128]{2,1,0:T(8,128)S(1)} %get-tuple-element.156), channel_id=1, source_target_pairs={{0,16},{16,0},{32,48},{48,32},{64,80},{80,64},{96,112},{112,96},{1... | collective-permute-start | bytes 270344 | tf_op jit(solution)/shard_map/ppermute | solution.py:635
  48.2 8.1 %collective-permute-start.7 = (f32[11,16,128]{2,1,0:T(8,128)S(1)}, f32[11,16,128]{2,1,0:T(8,128)S(1)}, u32[]{:S(2)}, u32[]{:S(2)}) collective-permute-start(f32[11,16,128]{2,1,0:T(8,128)S(1)} %get-tuple-element.157), channel_id=1, source_target_pairs={{16,32},{32,16},{48,64},{64,48},{80,96},{96,80},{112,128},{128,112... | collective-permute-start | bytes 270344 | tf_op jit(solution)/shard_map/ppermute | solution.py:635

commit v2 on v1

--- a/solution.py
+++ b/solution.py
@@ -130,12 +130,14 @@
     copies = [pltpu.make_async_copy(src, dst, sems.at[i]) for i, (src, dst) in enumerate(pairs)]
     for copy in copies:
         copy.start()
-    for copy in copies:
-        copy.wait()
+    needs = {("f", a): [2 * a, 2 * a + 1] for a in range(5)}
+    needs.update({("m", 0): [10, 11], ("c", 0): [12], ("c", 1): [13], ("cm", 0): [14], ("prior", 0): [15]})
     lane = lanes((Z, 128))
     built = {}
     for key, (plane, offset, width) in Y_SLOTS.items():
         kind, a, k, x = key
+        for needed in needs.pop((kind, a), []):
+            copies[needed].wait()
         if kind == "f":
             first, last = firsts[a, k, x], lasts[a, k, x]
         elif kind == "m":
@@ -457,23 +459,25 @@
         for x in range(ROWS):
             upper = row_of(fe, x + 1) if x + 1 < ROWS else None
             h = h_row(
-                row_of(fh, x), current, upper[1:] if upper else following, top_plane(pl_ref, x, t)
-            )
-            e2, j2, p2, v2 = e_row(
-                current, h, preceding, row_of(fj, x), row_of(fp, x), row_of(fv, x), [c[k, x] for k in range(6)]
+                row_of(fh, x), row_of(fe, x), upper[1:] if upper else following, top_plane(pl_ref, x, t)
             )
             for k in range(3):
-                news[0][k, x] = e2[k]
                 news[1][k, x] = h[k]
-                news[2][k, x] = j2[k]
-                news[3][k, x] = p2[k]
-                news[4][k, x] = v2[k]
             for k in range(2):
                 part = h[k][8:Z]
                 have = summed[k][x // RATIO]
                 summed[k][x // RATIO] = part if have is None else have + part
+        for x in range(ROWS):
+            h = row_of(news[1], x)
+            e2, j2, p2, v2 = e_row(
+                row_of(fe, x), h, preceding, row_of(fj, x), row_of(fp, x), row_of(fv, x), [c[k, x] for k in range(6)]
+            )
+            for k in range(3):
+                news[0][k, x] = e2[k]
+                news[2][k, x] = j2[k]
+                news[3][k, x] = p2[k]
+                news[4][k, x] = v2[k]
             preceding = h[1:]
-            current = upper
             if finished and t == RATIO - 1:
                 finished(x)
         if t == 0:

time: 59 us -> 57.2 us (0.969)
  Pallas kernels: 20.8 us -> 18.8 us
    pallas_call x10, Pallas kernels: 20.8 us -> 18.8 us  [call(): pl.pallas_call(kernel, out_shape=outs, in_specs=specs or [FULL] * len(arg...]
  transfers between devices with their start and end apart: 14 -> 14, of which waited for: 2 -> 3; matrix products, arithmetic and copies ran while one was open for 0% -> 0% of each run, Pallas kernels for 25% -> 22%
where the time goes in v2:
time: 57.2 us; the launch traced here: 57.1 us
  starting transfers between devices  33.4 us (58%)
  Pallas kernels  18.8 us (33%)
  waiting for transfers between devices  3.74 us (7%)
  between operations  1 us (2%)
    ppermute x14, starting transfers between devices, exchanged(): swapped.append(lax.ppermute(message, axis, pairs))  33.4 us
    pallas_call x10, Pallas kernels, call(): pl.pallas_call(kernel, out_shape=outs, in_specs=specs or [FULL] * len(arg...  18.8 us
    ppermute x14, waiting for transfers between devices, exchanged(): swapped.append(lax.ppermute(message, axis, pairs))  3.74 us
  transfers between devices with their start and end apart: 14, of which 3 were waited for; matrix products, arithmetic and copies ran while one was open for 0% of the time, Pallas kernels for 22%

profile of v2, /device:TPU:2, one launch (start us, length us, event | category | flops | bytes accessed | tf_op | source)
XLA Modules:
  0.0 57.1 jit_solution(811514632329001826)
XLA Ops:
  0.6 2.3 %shard_map.208 = (f32[8,16,128]{2,1,0:T(8,128)S(1)}, f32[8,16,128]{2,1,0:T(8,128)S(1)}) custom-call(f32[3,6,16,384]{3,2,1,0:T(8,128)} %bitcast.28, f32[3,6,16,384]{3,2,1,0:T(8,128)} %bitcast.30, f32[3,6,16,384]{3,2,1,0:T(8,128)} %bitcast.32, f32[3,6,16,384]{3,2,1,0:T(8,128)} %bitcast.34, f32[3,6,16,384]{3,2,1,0:T(8,128)} %bitcast.36, ...), custom_call_target="tpu_custom_call" | custom-call | flops 4000000 | bytes 8000000 | tf_op jit(solution)/shard_map/pallas_call | solution.py:599
  2.9 0.0 copy-start.3
  2.9 0.0 copy-start.4
  2.9 0.0 copy-start
  3.0 0.0 copy-start.1
  3.0 0.1 collective-permute-start
  3.1 0.0 copy-start.5
  3.1 3.1 %collective-permute-start.1 = (f32[8,16,128]{2,1,0:T(8,128)S(1)}, f32[8,16,128]{2,1,0:T(8,128)S(1)}, u32[]{:S(2)}, u32[]{:S(2)}) collective-permute-start(f32[8,16,128]{2,1,0:T(8,128)S(1)} %get-tuple-element.124), channel_id=1, source_target_pairs={{1,2},{2,1},{3,4},{4,3},{5,6},{6,5},{7,8},{8,7},{9,10},{10,9},{11,... | collective-permute-start | bytes 196616 | tf_op jit(solution)/shard_map/ppermute | solution.py:639
  6.3 2.0 %shard_map.207 = (f32[3,6,16,256]{3,2,1,0:T(8,128)S(1)}, f32[3,6,16,256]{3,2,1,0:T(8,128)S(1)}, f32[3,6,16,256]{3,2,1,0:T(8,128)S(1)}, f32[3,6,16,256]{3,2,1,0:T...) custom-call(f32[3,6,16,384]{3,2,1,0:T(8,128)} %bitcast.29, ...), custom_call_target="tpu_custom_call" | custom-call | flops 4000000 | bytes 8000000 | tf_op jit(solution)/shard_map/pallas_call | solution.py:599
  8.3 0.7 %collective-permute-done.1.refs_13_ = f32[8,16,128]{2,1,0:T(8,128)S(1)} collective-permute-done((f32[8,16,128]{2,1,0:T(8,128)S(1)}, f32[8,16,128]{2,1,0:T(8,128)S(1)}, u32[]{:S(2)}, u32[]{:S(2)}) %collective-permute-start.1) | collective-permute-done | bytes 65568 | tf_op jit(solution)/shard_map/ppermute | solution.py:639
  9.0 1.5 %shard_map.212 = (f32[3,6,16,256]{3,2,1,0:T(8,128)S(1)}, f32[3,6,16,256]{3,2,1,0:T(8,128)S(1)}, f32[3,6,16,256]{3,2,1,0:T(8,128)S(1)}, f32[3,6,16,256]{3,2,1,0:T...) custom-call(f32[3,6,16,256]{3,2,1,0:T(8,128)S(1)} %get-tuple-element, ...), custom_call_target="tpu_custom_call", output_to_operand_aliasing={{0}: (0, {}), {1}: (1, {}), {2}: (2, {}), {3}: (3, {}), {4}... | custom-call | flops 4000000 | bytes 8000000 | tf_op jit(solution)/shard_map/pallas_call | solution.py:599
  10.4 2.2 %collective-permute-start.8 = (f32[13,16,128]{2,1,0:T(8,128)S(1)}, f32[13,16,128]{2,1,0:T(8,128)S(1)}, u32[]{:S(2)}, u32[]{:S(2)}) collective-permute-start(f32[13,16,128]{2,1,0:T(8,128)S(1)} %get-tuple-element.175), channel_id=1, source_target_pairs={{0,16},{16,0},{32,48},{48,32},{64,80},{80,64},{96,112},{112,96},{1... | collective-permute-start | bytes 319496 | tf_op jit(solution)/shard_map/ppermute | solution.py:639
  12.7 6.7 %collective-permute-start.9 = (f32[13,16,128]{2,1,0:T(8,128)S(1)}, f32[13,16,128]{2,1,0:T(8,128)S(1)}, u32[]{:S(2)}, u32[]{:S(2)}) collective-permute-start(f32[13,16,128]{2,1,0:T(8,128)S(1)} %get-tuple-element.176), channel_id=1, source_target_pairs={{16,32},{32,16},{48,64},{64,48},{80,96},{96,80},{112,128},{128,112... | collective-permute-start | bytes 319496 | tf_op jit(solution)/shard_map/ppermute | solution.py:639
  19.4 1.5 %shard_map.209 = (f32[3,6,16,256]{3,2,1,0:T(8,128)S(1)}, f32[3,6,16,256]{3,2,1,0:T(8,128)S(1)}, f32[3,6,16,256]{3,2,1,0:T(8,128)S(1)}, f32[3,6,16,256]{3,2,1,0:T...) custom-call(f32[3,6,16,256]{3,2,1,0:T(8,128)S(1)} %get-tuple-element, ...), custom_call_target="tpu_custom_call", output_to_operand_aliasing={{0}: (0, {}), {1}: (1, {}), {2}: (2, {}), {3}: (3, {}), {4}... | custom-call | flops 4000000 | bytes 8000000 | tf_op jit(solution)/shard_map/pallas_call | solution.py:599
  20.8 0.1 collective-permute-start.2
  20.9 4.0 %collective-permute-start.3 = (f32[13,16,128]{2,1,0:T(8,128)S(1)}, f32[13,16,128]{2,1,0:T(8,128)S(1)}, u32[]{:S(2)}, u32[]{:S(2)}) collective-permute-start(f32[13,16,128]{2,1,0:T(8,128)S(1)} %get-tuple-element.136), channel_id=1, source_target_pairs={{16,32},{32,16},{48,64},{64,48},{80,96},{96,80},{112,128},{128,112... | collective-permute-start | bytes 319496 | tf_op jit(solution)/shard_map/ppermute | solution.py:639
  24.9 1.7 %shard_map.213 = (f32[3,6,16,256]{3,2,1,0:T(8,128)S(1)}, f32[3,6,16,256]{3,2,1,0:T(8,128)S(1)}, f32[3,6,16,256]{3,2,1,0:T(8,128)S(1)}, f32[3,6,16,256]{3,2,1,0:T...) custom-call(f32[3,6,16,256]{3,2,1,0:T(8,128)S(1)} %get-tuple-element, ...), custom_call_target="tpu_custom_call" | custom-call | flops 4000000 | bytes 8000000 | tf_op jit(solution)/shard_map/pallas_call | solution.py:599
  26.6 0.1 collective-permute-start.10
  26.7 4.7 %collective-permute-start.11 = (f32[11,16,128]{2,1,0:T(8,128)S(1)}, f32[11,16,128]{2,1,0:T(8,128)S(1)}, u32[]{:S(2)}, u32[]{:S(2)}) collective-permute-start(f32[11,16,128]{2,1,0:T(8,128)S(1)} %get-tuple-element.187), channel_id=1, source_target_pairs={{16,32},{32,16},{48,64},{64,48},{80,96},{96,80},{112,128},{128,112... | collective-permute-start | bytes 270344 | tf_op jit(solution)/shard_map/ppermute | solution.py:639
  31.4 1.7 %shard_map.210 = (f32[3,6,16,256]{3,2,1,0:T(8,128)S(1)}, f32[3,6,16,256]{3,2,1,0:T(8,128)S(1)}, f32[3,6,16,256]{3,2,1,0:T(8,128)S(1)}, f32[3,6,16,256]{3,2,1,0:T...) custom-call(f32[3,6,16,256]{3,2,1,0:T(8,128)S(1)} %get-tuple-element, ...), custom_call_target="tpu_custom_call" | custom-call | flops 4000000 | bytes 8000000 | tf_op jit(solution)/shard_map/pallas_call | solution.py:599
  33.2 0.2 collective-permute-start.4
  33.4 3.1 %collective-permute-start.5 = (f32[11,16,128]{2,1,0:T(8,128)S(1)}, f32[11,16,128]{2,1,0:T(8,128)S(1)}, u32[]{:S(2)}, u32[]{:S(2)}) collective-permute-start(f32[11,16,128]{2,1,0:T(8,128)S(1)} %get-tuple-element.147), channel_id=1, source_target_pairs={{16,32},{32,16},{48,64},{64,48},{80,96},{96,80},{112,128},{128,112... | collective-permute-start | bytes 270344 | tf_op jit(solution)/shard_map/ppermute | solution.py:639
  36.5 1.7 %shard_map.214 = (f32[3,6,16,256]{3,2,1,0:T(8,128)S(1)}, f32[3,6,16,256]{3,2,1,0:T(8,128)S(1)}, f32[3,6,16,256]{3,2,1,0:T(8,128)S(1)}, f32[3,6,16,256]{3,2,1,0:T...) custom-call(f32[3,6,16,256]{3,2,1,0:T(8,128)S(1)} %get-tuple-element, ...), custom_call_target="tpu_custom_call" | custom-call | flops 4000000 | bytes 8000000 | tf_op jit(solution)/shard_map/pallas_call | solution.py:599
  38.2 2.2 %collective-permute-start.12 = (f32[11,16,128]{2,1,0:T(8,128)S(1)}, f32[11,16,128]{2,1,0:T(8,128)S(1)}, u32[]{:S(2)}, u32[]{:S(2)}) collective-permute-start(f32[11,16,128]{2,1,0:T(8,128)S(1)} %get-tuple-element.196), channel_id=1, source_target_pairs={{0,16},{16,0},{32,48},{48,32},{64,80},{80,64},{96,112},{112,96},{1... | collective-permute-start | bytes 270344 | tf_op jit(solution)/shard_map/ppermute | solution.py:639
  40.4 2.0 %collective-permute-start.13 = (f32[11,16,128]{2,1,0:T(8,128)S(1)}, f32[11,16,128]{2,1,0:T(8,128)S(1)}, u32[]{:S(2)}, u32[]{:S(2)}) collective-permute-start(f32[11,16,128]{2,1,0:T(8,128)S(1)} %get-tuple-element.197), channel_id=1, source_target_pairs={{16,32},{32,16},{48,64},{64,48},{80,96},{96,80},{112,128},{128,112... | collective-permute-start | bytes 270344 | tf_op jit(solution)/shard_map/ppermute | solution.py:639
  42.4 1.7 %shard_map.211 = (f32[3,6,16,256]{3,2,1,0:T(8,128)S(1)}, f32[3,6,16,256]{3,2,1,0:T(8,128)S(1)}, f32[3,6,16,256]{3,2,1,0:T(8,128)S(1)}, f32[3,6,16,256]{3,2,1,0:T...) custom-call(f32[3,6,16,256]{3,2,1,0:T(8,128)S(1)} %get-tuple-element, ...), custom_call_target="tpu_custom_call" | custom-call | flops 4000000 | bytes 8000000 | tf_op jit(solution)/shard_map/pallas_call | solution.py:599
  44.1 2.2 %collective-permute-start.6 = (f32[11,16,128]{2,1,0:T(8,128)S(1)}, f32[11,16,128]{2,1,0:T(8,128)S(1)}, u32[]{:S(2)}, u32[]{:S(2)}) collective-permute-start(f32[11,16,128]{2,1,0:T(8,128)S(1)} %get-tuple-element.156), channel_id=1, source_target_pairs={{0,16},{16,0},{32,48},{48,32},{64,80},{80,64},{96,112},{112,96},{1... | collective-permute-start | bytes 270344 | tf_op jit(solution)/shard_map/ppermute | solution.py:639
  46.3 2.8 %collective-permute-start.7 = (f32[11,16,128]{2,1,0:T(8,128)S(1)}, f32[11,16,128]{2,1,0:T(8,128)S(1)}, u32[]{:S(2)}, u32[]{:S(2)}) collective-permute-start(f32[11,16,128]{2,1,0:T(8,128)S(1)} %get-tuple-element.157), channel_id=1, source_target_pairs={{16,32},{32,16},{48,64},{64,48},{80,96},{96,80},{112,128},{128,112... | collective-permute-start | bytes 270344 | tf_op jit(solution)/shard_map/ppermute | solution.py:639
  49.1 0.5 collective-permute-done.13.refs_12_
  49.5 2.3 %shard_map.215 = (f32[3,6,16,384]{3,2,1,0:T(8,128)}, f32[3,6,16,384]{3,2,1,0:T(8,128)}, f32[3,6,16,384]{3,2,1,0:T(8,128)}, f32[3,6,16,384]{3,2,1,0:T(8,128)}, f3...) custom-call(f32[3,6,16,256]{3,2,1,0:T(8,128)S(1)} %get-tuple-element, ...), custom_call_target="tpu_custom_call" | custom-call | flops 4000000 | bytes 8000000 | tf_op jit(solution)/shard_map/pallas_call | solution.py:599
  51.9 2.6 %collective-permute-done.7.refs_12_ = f32[11,16,128]{2,1,0:T(8,128)S(1)} collective-permute-done((f32[11,16,128]{2,1,0:T(8,128)S(1)}, f32[11,16,128]{2,1,0:T(8,128)S(1)}, u32[]{:S(2)}, u32[]{:S(2)}) %collective-permute-start.7) | collective-permute-done | bytes 90144 | tf_op jit(solution)/shard_map/ppermute | solution.py:639
  54.4 2.4 %shard_map.216 = (f32[3,6,16,384]{3,2,1,0:T(8,128)}, f32[3,6,16,384]{3,2,1,0:T(8,128)}, f32[3,6,16,384]{3,2,1,0:T(8,128)}, f32[3,6,16,384]{3,2,1,0:T(8,128)}, f3...) custom-call(f32[3,6,16,256]{3,2,1,0:T(8,128)S(1)} %get-tuple-element, ...), custom_call_target="tpu_custom_call", output_to_operand_aliasing={{0}: (13, {}), {1}: (14, {}), {2}: (15, {}), {3}: (16, {}),... | custom-call | flops 4000000 | bytes 8000000 | tf_op jit(solution)/shard_map/pallas_call | solution.py:599
  (22 shorter events, 0.1 us)
Async XLA Ops:
  2.9 3.3 %copy-start.3 = (f32[8]{0:T(128)S(1)}, f32[8]{0:T(128)}, u32[]{:S(2)}) copy-start(f32[8]{0:T(128)} %param.24) | copy-start | bytes 100
  2.9 3.2 %copy-start.4 = (f32[8]{0:T(128)S(1)}, f32[8]{0:T(128)}, u32[]{:S(2)}) copy-start(f32[8]{0:T(128)} %param.23) | copy-start | bytes 100
  2.9 3.2 %copy-start = (f32[8]{0:T(128)S(1)}, f32[8]{0:T(128)}, u32[]{:S(2)}) copy-start(f32[8]{0:T(128)} %param.25) | copy-start | bytes 100
  3.0 3.2 %copy-start.1 = (f32[8]{0:T(128)S(1)}, f32[8]{0:T(128)}, u32[]{:S(2)}) copy-start(f32[8]{0:T(128)} %param.27) | copy-start | bytes 100
  3.0 3.2 %copy-start.2 = (f32[8]{0:T(128)S(1)}, f32[8]{0:T(128)}, u32[]{:S(2)}) copy-start(f32[8]{0:T(128)} %param.26) | copy-start | bytes 100
  3.0 5.3 %collective-permute-start = (f32[8,16,128]{2,1,0:T(8,128)S(1)}, f32[8,16,128]{2,1,0:T(8,128)S(1)}, u32[]{:S(2)}, u32[]{:S(2)}) collective-permute-start(f32[8,16,128]{2,1,0:T(8,128)S(1)} %get-tuple-element.123), channel_id=1, source_target_pairs={{0,1},{1,0},{2,3},{3,2},{4,5},{5,4},{6,7},{7,6},{8,9},{9,8},{10,11... | collective-permute-start | bytes 196616 | tf_op jit(solution)/shard_map/ppermute | solution.py:639
  3.1 3.1 %copy-start.5 = (f32[8]{0:T(128)S(1)}, f32[8]{0:T(128)}, u32[]{:S(2)}) copy-start(f32[8]{0:T(128)} %param.22) | copy-start | bytes 100
  3.1 5.9 %collective-permute-start.1 = (f32[8,16,128]{2,1,0:T(8,128)S(1)}, f32[8,16,128]{2,1,0:T(8,128)S(1)}, u32[]{:S(2)}, u32[]{:S(2)}) collective-permute-start(f32[8,16,128]{2,1,0:T(8,128)S(1)} %get-tuple-element.124), channel_id=1, source_target_pairs={{1,2},{2,1},{3,4},{4,3},{5,6},{6,5},{7,8},{8,7},{9,10},{10,9},{11,... | collective-permute-start | bytes 196616 | tf_op jit(solution)/shard_map/ppermute | solution.py:639
  10.4 14.4 %collective-permute-start.8 = (f32[13,16,128]{2,1,0:T(8,128)S(1)}, f32[13,16,128]{2,1,0:T(8,128)S(1)}, u32[]{:S(2)}, u32[]{:S(2)}) collective-permute-start(f32[13,16,128]{2,1,0:T(8,128)S(1)} %get-tuple-element.175), channel_id=1, source_target_pairs={{0,16},{16,0},{32,48},{48,32},{64,80},{80,64},{96,112},{112,96},{1... | collective-permute-start | bytes 319496 | tf_op jit(solution)/shard_map/ppermute | solution.py:639
  12.7 12.2 %collective-permute-start.9 = (f32[13,16,128]{2,1,0:T(8,128)S(1)}, f32[13,16,128]{2,1,0:T(8,128)S(1)}, u32[]{:S(2)}, u32[]{:S(2)}) collective-permute-start(f32[13,16,128]{2,1,0:T(8,128)S(1)} %get-tuple-element.176), channel_id=1, source_target_pairs={{16,32},{32,16},{48,64},{64,48},{80,96},{96,80},{112,128},{128,112... | collective-permute-start | bytes 319496 | tf_op jit(solution)/shard_map/ppermute | solution.py:639
  20.8 10.6 %collective-permute-start.2 = (f32[13,16,128]{2,1,0:T(8,128)S(1)}, f32[13,16,128]{2,1,0:T(8,128)S(1)}, u32[]{:S(2)}, u32[]{:S(2)}) collective-permute-start(f32[13,16,128]{2,1,0:T(8,128)S(1)} %get-tuple-element.135), channel_id=1, source_target_pairs={{0,16},{16,0},{32,48},{48,32},{64,80},{80,64},{96,112},{112,96},{1... | collective-permute-start | bytes 319496 | tf_op jit(solution)/shard_map/ppermute | solution.py:639
  20.9 10.5 %collective-permute-start.3 = (f32[13,16,128]{2,1,0:T(8,128)S(1)}, f32[13,16,128]{2,1,0:T(8,128)S(1)}, u32[]{:S(2)}, u32[]{:S(2)}) collective-permute-start(f32[13,16,128]{2,1,0:T(8,128)S(1)} %get-tuple-element.136), channel_id=1, source_target_pairs={{16,32},{32,16},{48,64},{64,48},{80,96},{96,80},{112,128},{128,112... | collective-permute-start | bytes 319496 | tf_op jit(solution)/shard_map/ppermute | solution.py:639
  26.6 9.9 %collective-permute-start.10 = (f32[11,16,128]{2,1,0:T(8,128)S(1)}, f32[11,16,128]{2,1,0:T(8,128)S(1)}, u32[]{:S(2)}, u32[]{:S(2)}) collective-permute-start(f32[11,16,128]{2,1,0:T(8,128)S(1)} %get-tuple-element.186), channel_id=1, source_target_pairs={{0,16},{16,0},{32,48},{48,32},{64,80},{80,64},{96,112},{112,96},{1... | collective-permute-start | bytes 270344 | tf_op jit(solution)/shard_map/ppermute | solution.py:639
  26.7 9.8 %collective-permute-start.11 = (f32[11,16,128]{2,1,0:T(8,128)S(1)}, f32[11,16,128]{2,1,0:T(8,128)S(1)}, u32[]{:S(2)}, u32[]{:S(2)}) collective-permute-start(f32[11,16,128]{2,1,0:T(8,128)S(1)} %get-tuple-element.187), channel_id=1, source_target_pairs={{16,32},{32,16},{48,64},{64,48},{80,96},{96,80},{112,128},{128,112... | collective-permute-start | bytes 270344 | tf_op jit(solution)/shard_map/ppermute | solution.py:639
  33.2 9.3 %collective-permute-start.4 = (f32[11,16,128]{2,1,0:T(8,128)S(1)}, f32[11,16,128]{2,1,0:T(8,128)S(1)}, u32[]{:S(2)}, u32[]{:S(2)}) collective-permute-start(f32[11,16,128]{2,1,0:T(8,128)S(1)} %get-tuple-element.146), channel_id=1, source_target_pairs={{0,16},{16,0},{32,48},{48,32},{64,80},{80,64},{96,112},{112,96},{1... | collective-permute-start | bytes 270344 | tf_op jit(solution)/shard_map/ppermute | solution.py:639
  33.4 9.1 %collective-permute-start.5 = (f32[11,16,128]{2,1,0:T(8,128)S(1)}, f32[11,16,128]{2,1,0:T(8,128)S(1)}, u32[]{:S(2)}, u32[]{:S(2)}) collective-permute-start(f32[11,16,128]{2,1,0:T(8,128)S(1)} %get-tuple-element.147), channel_id=1, source_target_pairs={{16,32},{32,16},{48,64},{64,48},{80,96},{96,80},{112,128},{128,112... | collective-permute-start | bytes 270344 | tf_op jit(solution)/shard_map/ppermute | solution.py:639
  38.2 10.9 %collective-permute-start.12 = (f32[11,16,128]{2,1,0:T(8,128)S(1)}, f32[11,16,128]{2,1,0:T(8,128)S(1)}, u32[]{:S(2)}, u32[]{:S(2)}) collective-permute-start(f32[11,16,128]{2,1,0:T(8,128)S(1)} %get-tuple-element.196), channel_id=1, source_target_pairs={{0,16},{16,0},{32,48},{48,32},{64,80},{80,64},{96,112},{112,96},{1... | collective-permute-start | bytes 270344 | tf_op jit(solution)/shard_map/ppermute | solution.py:639
  40.4 9.1 %collective-permute-start.13 = (f32[11,16,128]{2,1,0:T(8,128)S(1)}, f32[11,16,128]{2,1,0:T(8,128)S(1)}, u32[]{:S(2)}, u32[]{:S(2)}) collective-permute-start(f32[11,16,128]{2,1,0:T(8,128)S(1)} %get-tuple-element.197), channel_id=1, source_target_pairs={{16,32},{32,16},{48,64},{64,48},{80,96},{96,80},{112,128},{128,112... | collective-permute-start | bytes 270344 | tf_op jit(solution)/shard_map/ppermute | solution.py:639
  44.1 7.7 %collective-permute-start.6 = (f32[11,16,128]{2,1,0:T(8,128)S(1)}, f32[11,16,128]{2,1,0:T(8,128)S(1)}, u32[]{:S(2)}, u32[]{:S(2)}) collective-permute-start(f32[11,16,128]{2,1,0:T(8,128)S(1)} %get-tuple-element.156), channel_id=1, source_target_pairs={{0,16},{16,0},{32,48},{48,32},{64,80},{80,64},{96,112},{112,96},{1... | collective-permute-start | bytes 270344 | tf_op jit(solution)/shard_map/ppermute | solution.py:639
  46.3 8.1 %collective-permute-start.7 = (f32[11,16,128]{2,1,0:T(8,128)S(1)}, f32[11,16,128]{2,1,0:T(8,128)S(1)}, u32[]{:S(2)}, u32[]{:S(2)}) collective-permute-start(f32[11,16,128]{2,1,0:T(8,128)S(1)} %get-tuple-element.157), channel_id=1, source_target_pairs={{16,32},{32,16},{48,64},{64,48},{80,96},{96,80},{112,128},{128,112... | collective-permute-start | bytes 270344 | tf_op jit(solution)/shard_map/ppermute | solution.py:639

commit v3 on v2

--- a/solution.py
+++ b/solution.py
@@ -130,14 +130,12 @@
     copies = [pltpu.make_async_copy(src, dst, sems.at[i]) for i, (src, dst) in enumerate(pairs)]
     for copy in copies:
         copy.start()
-    needs = {("f", a): [2 * a, 2 * a + 1] for a in range(5)}
-    needs.update({("m", 0): [10, 11], ("c", 0): [12], ("c", 1): [13], ("cm", 0): [14], ("prior", 0): [15]})
+    for copy in copies:
+        copy.wait()
     lane = lanes((Z, 128))
     built = {}
     for key, (plane, offset, width) in Y_SLOTS.items():
         kind, a, k, x = key
-        for needed in needs.pop((kind, a), []):
-            copies[needed].wait()
         if kind == "f":
             first, last = firsts[a, k, x], lasts[a, k, x]
         elif kind == "m":
@@ -391,14 +389,15 @@
         message[plane] = jnp.where(swap, received[1][plane], received[0][plane])
     outer = slice(128, 256) if half == 0 else slice(0, 128)
     inner = slice(0, 128) if half == 0 else slice(128, 256)
-    for x in range(ROWS):
-        value = with_ghosts(half, message, ("m", 0, 0, x), mat_in[x, :, outer])
-        index = jnp.clip(value.astype(jnp.int32), 0, 127)
-        if x in (0, ROWS - 1):
-            mat[x, :, outer] = value
-            mat[x, :, inner] = mat_in[x, :, inner]
-        for k in range(6):
-            c[k, x, :, outer] = lookup(tab, k, index)
+    for x in (0, ROWS - 1):
+        mat[x, :, outer] = with_ghosts(half, message, ("m", 0, 0, x), mat_in[x, :, outer])
+        mat[x, :, inner] = mat_in[x, :, inner]
+    (packed_plane,) = {Y_SLOTS["m", 0, 0, x][0] for x in range(ROWS)}
+    index = jnp.clip(message[packed_plane].astype(jnp.int32), 0, 127)
+    for k in range(6):
+        packed = {packed_plane: lookup(tab, k, index)}
+        for x in range(ROWS):
+            c[k, x, :, outer] = with_ghosts(half, packed, ("m", 0, 0, x), c_in[k, x, :, outer])
     for a in range(5):
         for k in range(3):
             for x in range(ROWS):
@@ -437,7 +436,7 @@
         for k in range(3):
             ch[k, r] = coarse_h[r][k]
     if finished:
-        finished(-2)
+        finished((6,))
 
     ge = gh = he = hh = None
     summed = [[None] * CROWS for _ in range(2)]
@@ -456,6 +455,15 @@
             gh = h_row(old, ge, e_first[1:], flat, (0, 1, 2) if t < RATIO - 1 else (1, 2))
         preceding = [read_x(from_left, half, h_items, ("h", t, k)) + gh[k] for k in (1, 2)]
         current = e_first
+        last = finished is not None and t == RATIO - 1
+        if last:
+            for x in range(ROWS):
+                for k in range(3):
+                    v2 = c[3, x] * fv[k, x] + c[4, x] * (c[5, x] * fe[k, x] - fp[k, x])
+                    news[2][k, x] = c[1, x] * fj[k, x] + c[2, x] * fe[k, x]
+                    news[3][k, x] = fp[k, x] + TIMESTEP * v2
+                    news[4][k, x] = v2
+            finished((2, 3, 4))
         for x in range(ROWS):
             upper = row_of(fe, x + 1) if x + 1 < ROWS else None
             h = h_row(
@@ -467,8 +475,16 @@
                 part = h[k][8:Z]
                 have = summed[k][x // RATIO]
                 summed[k][x // RATIO] = part if have is None else have + part
+        if last:
+            finished((1,))
         for x in range(ROWS):
             h = row_of(news[1], x)
+            if last:
+                curl = curl_h(h, preceding, flat)
+                for k in range(3):
+                    news[0][k, x] = fe[k, x] + c[0, x] * (curl[k] - fj[k, x] - fv[k, x])
+                preceding = h[1:]
+                continue
             e2, j2, p2, v2 = e_row(
                 row_of(fe, x), h, preceding, row_of(fj, x), row_of(fp, x), row_of(fv, x), [c[k, x] for k in range(6)]
             )
@@ -478,8 +494,8 @@
                 news[3][k, x] = p2[k]
                 news[4][k, x] = v2[k]
             preceding = h[1:]
-            if finished and t == RATIO - 1:
-                finished(x)
+        if last:
+            finished((0,))
         if t == 0:
             (a, b), (a2, b2) = [[ghost[k, side] for k in range(2)] for side in range(2)]
             ge = [
@@ -505,7 +521,7 @@
             ce[k, r] = coarse_e0[r][k] + inv[r] * curl[k]
         preceding = coarse_h[r][1:]
     if finished:
-        finished(-1)
+        finished((5,))
 
 
 def ghost_coefficients(half, ghost, tab, from_left, from_right):
@@ -558,24 +574,24 @@
             for r in range(CROWS):
                 value = jnp.where(first, others_c[a][k, r], (ce, ch)[a][k, r])
                 coarse_parts[a][k, pl.ds(r, Z, stride=CROWS), :] = value
-        copies.append(pltpu.make_async_copy(coarse_parts[a], outs_c[a], sems.at[ROWS, a]))
+        copies.append(pltpu.make_async_copy(coarse_parts[a], outs_c[a], sems.at[5 + a]))
         copies[-1].start()
 
-    def finished(x):
-        if x < 0:
-            return coarse_finished(-x - 1)
-        for a in range(5):
+    def finished(arrays):
+        for a in arrays:
+            if a >= 5:
+                coarse_finished(a - 5)
+                continue
             if half == 0:
-                source = news[a].at[:, x, :, 0:128]
-                target = outs[a].at[:, x, :, 0:128]
+                source, target = news[a].at[:, :, :, 0:128], outs[a].at[:, :, :, 0:128]
             else:
-                for k in range(3):
-                    news[a][k, x, :, 0:128] = jnp.where(
-                        first, others[a][k, x, :, 128:256], news[a][k, x, :, 0:128]
-                    )
-                source = news[a].at[:, x]
-                target = outs[a].at[:, x, :, 128:384]
-            copies.append(pltpu.make_async_copy(source, target, sems.at[x, a]))
+                for x in range(ROWS):
+                    for k in range(3):
+                        news[a][k, x, :, 0:128] = jnp.where(
+                            first, others[a][k, x, :, 128:256], news[a][k, x, :, 0:128]
+                        )
+                source, target = news[a], outs[a].at[:, :, :, 128:384]
+            copies.append(pltpu.make_async_copy(source, target, sems.at[a]))
             copies[-1].start()
 
     coarse_step(
@@ -742,7 +758,7 @@
             out_specs=[RAW] * 7 if half else [RAW] * 5 + [FULL] * 7,
             scratch=([vmem(*FIELD)] * 5 + [vmem(*COARSE)] * 2 + [vmem(3, Z * CROWS, 128)] * 2 if half else [])
             + [vmem(*message.shape) for message in waiting[half]]
-            + [pltpu.SemaphoreType.DMA((ROWS + 1, 5))],
+            + [pltpu.SemaphoreType.DMA((7,))],
             aliases={13 + i: i for i in range(5)} if half else None,
         )
     fine = [jnp.transpose(value, (0, 2, 1, 3)) for value in done[0:5]]

time: 57.2 us -> 56.6 us (0.990)
  Pallas kernels: 18.8 us -> 17.9 us
    pallas_call x10, Pallas kernels: 18.8 us -> 17.9 us  [call(): pl.pallas_call(kernel, out_shape=outs, in_specs=specs or [FULL] * len(arg...]
  transfers between devices with their start and end apart: 14 -> 14, of which waited for: 3 -> 3; matrix products, arithmetic and copies ran while one was open for 0% -> 0% of each run, Pallas kernels for 22% -> 21%
where the time goes in v3:
time: 56.6 us; the launch traced here: 56.5 us
  starting transfers between devices  33.5 us (59%)
  Pallas kernels  17.9 us (32%)
  waiting for transfers between devices  4.03 us (7%)
  between operations  1 us (2%)
    ppermute x14, starting transfers between devices, exchanged(): swapped.append(lax.ppermute(message, axis, pairs))  33.5 us
    pallas_call x10, Pallas kernels, call(): pl.pallas_call(kernel, out_shape=outs, in_specs=specs or [FULL] * len(arg...  17.9 us
    ppermute x14, waiting for transfers between devices, exchanged(): swapped.append(lax.ppermute(message, axis, pairs))  4.03 us
  transfers between devices with their start and end apart: 14, of which 3 were waited for; matrix products, arithmetic and copies ran while one was open for 0% of the time, Pallas kernels for 21%

profile of v3, /device:TPU:2, one launch (start us, length us, event | category | flops | bytes accessed | tf_op | source)
XLA Modules:
  0.0 56.5 jit_solution(3875812457816409160)
XLA Ops:
  0.6 2.1 %shard_map.208 = (f32[8,16,128]{2,1,0:T(8,128)S(1)}, f32[8,16,128]{2,1,0:T(8,128)S(1)}) custom-call(f32[3,6,16,384]{3,2,1,0:T(8,128)} %bitcast.28, f32[3,6,16,384]{3,2,1,0:T(8,128)} %bitcast.30, f32[3,6,16,384]{3,2,1,0:T(8,128)} %bitcast.32, f32[3,6,16,384]{3,2,1,0:T(8,128)} %bitcast.34, f32[3,6,16,384]{3,2,1,0:T(8,128)} %bitcast.36, ...), custom_call_target="tpu_custom_call" | custom-call | flops 4000000 | bytes 8000000 | tf_op jit(solution)/shard_map/pallas_call | solution.py:615
  2.8 0.0 copy-start.3
  2.8 0.0 copy-start.4
  2.8 0.0 copy-start
  2.8 0.0 copy-start.1
  2.8 0.1 collective-permute-start
  2.9 0.0 copy-start.5
  2.9 3.1 %collective-permute-start.1 = (f32[8,16,128]{2,1,0:T(8,128)S(1)}, f32[8,16,128]{2,1,0:T(8,128)S(1)}, u32[]{:S(2)}, u32[]{:S(2)}) collective-permute-start(f32[8,16,128]{2,1,0:T(8,128)S(1)} %get-tuple-element.124), channel_id=1, source_target_pairs={{1,2},{2,1},{3,4},{4,3},{5,6},{6,5},{7,8},{8,7},{9,10},{10,9},{11,... | collective-permute-start | bytes 196616 | tf_op jit(solution)/shard_map/ppermute | solution.py:655
  6.1 2.0 %shard_map.207 = (f32[3,6,16,256]{3,2,1,0:T(8,128)S(1)}, f32[3,6,16,256]{3,2,1,0:T(8,128)S(1)}, f32[3,6,16,256]{3,2,1,0:T(8,128)S(1)}, f32[3,6,16,256]{3,2,1,0:T...) custom-call(f32[3,6,16,384]{3,2,1,0:T(8,128)} %bitcast.29, ...), custom_call_target="tpu_custom_call" | custom-call | flops 4000000 | bytes 8000000 | tf_op jit(solution)/shard_map/pallas_call | solution.py:615
  8.1 0.7 %collective-permute-done.1.refs_13_ = f32[8,16,128]{2,1,0:T(8,128)S(1)} collective-permute-done((f32[8,16,128]{2,1,0:T(8,128)S(1)}, f32[8,16,128]{2,1,0:T(8,128)S(1)}, u32[]{:S(2)}, u32[]{:S(2)}) %collective-permute-start.1) | collective-permute-done | bytes 65568 | tf_op jit(solution)/shard_map/ppermute | solution.py:655
  8.8 1.4 %shard_map.212 = (f32[3,6,16,256]{3,2,1,0:T(8,128)S(1)}, f32[3,6,16,256]{3,2,1,0:T(8,128)S(1)}, f32[3,6,16,256]{3,2,1,0:T(8,128)S(1)}, f32[3,6,16,256]{3,2,1,0:T...) custom-call(f32[3,6,16,256]{3,2,1,0:T(8,128)S(1)} %get-tuple-element, ...), custom_call_target="tpu_custom_call", output_to_operand_aliasing={{0}: (0, {}), {1}: (1, {}), {2}: (2, {}), {3}: (3, {}), {4}... | custom-call | flops 4000000 | bytes 8000000 | tf_op jit(solution)/shard_map/pallas_call | solution.py:615
  10.2 2.2 %collective-permute-start.8 = (f32[13,16,128]{2,1,0:T(8,128)S(1)}, f32[13,16,128]{2,1,0:T(8,128)S(1)}, u32[]{:S(2)}, u32[]{:S(2)}) collective-permute-start(f32[13,16,128]{2,1,0:T(8,128)S(1)} %get-tuple-element.175), channel_id=1, source_target_pairs={{0,16},{16,0},{32,48},{48,32},{64,80},{80,64},{96,112},{112,96},{1... | collective-permute-start | bytes 319496 | tf_op jit(solution)/shard_map/ppermute | solution.py:655
  12.4 6.7 %collective-permute-start.9 = (f32[13,16,128]{2,1,0:T(8,128)S(1)}, f32[13,16,128]{2,1,0:T(8,128)S(1)}, u32[]{:S(2)}, u32[]{:S(2)}) collective-permute-start(f32[13,16,128]{2,1,0:T(8,128)S(1)} %get-tuple-element.176), channel_id=1, source_target_pairs={{16,32},{32,16},{48,64},{64,48},{80,96},{96,80},{112,128},{128,112... | collective-permute-start | bytes 319496 | tf_op jit(solution)/shard_map/ppermute | solution.py:655
  19.1 1.3 %shard_map.209 = (f32[3,6,16,256]{3,2,1,0:T(8,128)S(1)}, f32[3,6,16,256]{3,2,1,0:T(8,128)S(1)}, f32[3,6,16,256]{3,2,1,0:T(8,128)S(1)}, f32[3,6,16,256]{3,2,1,0:T...) custom-call(f32[3,6,16,256]{3,2,1,0:T(8,128)S(1)} %get-tuple-element, ...), custom_call_target="tpu_custom_call", output_to_operand_aliasing={{0}: (0, {}), {1}: (1, {}), {2}: (2, {}), {3}: (3, {}), {4}... | custom-call | flops 4000000 | bytes 8000000 | tf_op jit(solution)/shard_map/pallas_call | solution.py:615
  20.4 0.1 collective-permute-start.2
  20.5 4.0 %collective-permute-start.3 = (f32[13,16,128]{2,1,0:T(8,128)S(1)}, f32[13,16,128]{2,1,0:T(8,128)S(1)}, u32[]{:S(2)}, u32[]{:S(2)}) collective-permute-start(f32[13,16,128]{2,1,0:T(8,128)S(1)} %get-tuple-element.136), channel_id=1, source_target_pairs={{16,32},{32,16},{48,64},{64,48},{80,96},{96,80},{112,128},{128,112... | collective-permute-start | bytes 319496 | tf_op jit(solution)/shard_map/ppermute | solution.py:655
  24.5 1.7 %shard_map.213 = (f32[3,6,16,256]{3,2,1,0:T(8,128)S(1)}, f32[3,6,16,256]{3,2,1,0:T(8,128)S(1)}, f32[3,6,16,256]{3,2,1,0:T(8,128)S(1)}, f32[3,6,16,256]{3,2,1,0:T...) custom-call(f32[3,6,16,256]{3,2,1,0:T(8,128)S(1)} %get-tuple-element, ...), custom_call_target="tpu_custom_call" | custom-call | flops 4000000 | bytes 8000000 | tf_op jit(solution)/shard_map/pallas_call | solution.py:615
  26.3 0.1 collective-permute-start.10
  26.4 4.9 %collective-permute-start.11 = (f32[11,16,128]{2,1,0:T(8,128)S(1)}, f32[11,16,128]{2,1,0:T(8,128)S(1)}, u32[]{:S(2)}, u32[]{:S(2)}) collective-permute-start(f32[11,16,128]{2,1,0:T(8,128)S(1)} %get-tuple-element.187), channel_id=1, source_target_pairs={{16,32},{32,16},{48,64},{64,48},{80,96},{96,80},{112,128},{128,112... | collective-permute-start | bytes 270344 | tf_op jit(solution)/shard_map/ppermute | solution.py:655
  31.3 1.7 %shard_map.210 = (f32[3,6,16,256]{3,2,1,0:T(8,128)S(1)}, f32[3,6,16,256]{3,2,1,0:T(8,128)S(1)}, f32[3,6,16,256]{3,2,1,0:T(8,128)S(1)}, f32[3,6,16,256]{3,2,1,0:T...) custom-call(f32[3,6,16,256]{3,2,1,0:T(8,128)S(1)} %get-tuple-element, ...), custom_call_target="tpu_custom_call" | custom-call | flops 4000000 | bytes 8000000 | tf_op jit(solution)/shard_map/pallas_call | solution.py:615
  33.0 0.1 collective-permute-start.4
  33.1 3.0 %collective-permute-start.5 = (f32[11,16,128]{2,1,0:T(8,128)S(1)}, f32[11,16,128]{2,1,0:T(8,128)S(1)}, u32[]{:S(2)}, u32[]{:S(2)}) collective-permute-start(f32[11,16,128]{2,1,0:T(8,128)S(1)} %get-tuple-element.147), channel_id=1, source_target_pairs={{16,32},{32,16},{48,64},{64,48},{80,96},{96,80},{112,128},{128,112... | collective-permute-start | bytes 270344 | tf_op jit(solution)/shard_map/ppermute | solution.py:655
  36.1 1.7 %shard_map.214 = (f32[3,6,16,256]{3,2,1,0:T(8,128)S(1)}, f32[3,6,16,256]{3,2,1,0:T(8,128)S(1)}, f32[3,6,16,256]{3,2,1,0:T(8,128)S(1)}, f32[3,6,16,256]{3,2,1,0:T...) custom-call(f32[3,6,16,256]{3,2,1,0:T(8,128)S(1)} %get-tuple-element, ...), custom_call_target="tpu_custom_call" | custom-call | flops 4000000 | bytes 8000000 | tf_op jit(solution)/shard_map/pallas_call | solution.py:615
  37.8 2.2 %collective-permute-start.12 = (f32[11,16,128]{2,1,0:T(8,128)S(1)}, f32[11,16,128]{2,1,0:T(8,128)S(1)}, u32[]{:S(2)}, u32[]{:S(2)}) collective-permute-start(f32[11,16,128]{2,1,0:T(8,128)S(1)} %get-tuple-element.196), channel_id=1, source_target_pairs={{0,16},{16,0},{32,48},{48,32},{64,80},{80,64},{96,112},{112,96},{1... | collective-permute-start | bytes 270344 | tf_op jit(solution)/shard_map/ppermute | solution.py:655
  40.1 2.1 %collective-permute-start.13 = (f32[11,16,128]{2,1,0:T(8,128)S(1)}, f32[11,16,128]{2,1,0:T(8,128)S(1)}, u32[]{:S(2)}, u32[]{:S(2)}) collective-permute-start(f32[11,16,128]{2,1,0:T(8,128)S(1)} %get-tuple-element.197), channel_id=1, source_target_pairs={{16,32},{32,16},{48,64},{64,48},{80,96},{96,80},{112,128},{128,112... | collective-permute-start | bytes 270344 | tf_op jit(solution)/shard_map/ppermute | solution.py:655
  42.2 1.7 %shard_map.211 = (f32[3,6,16,256]{3,2,1,0:T(8,128)S(1)}, f32[3,6,16,256]{3,2,1,0:T(8,128)S(1)}, f32[3,6,16,256]{3,2,1,0:T(8,128)S(1)}, f32[3,6,16,256]{3,2,1,0:T...) custom-call(f32[3,6,16,256]{3,2,1,0:T(8,128)S(1)} %get-tuple-element, ...), custom_call_target="tpu_custom_call" | custom-call | flops 4000000 | bytes 8000000 | tf_op jit(solution)/shard_map/pallas_call | solution.py:615
  43.9 2.1 %collective-permute-start.6 = (f32[11,16,128]{2,1,0:T(8,128)S(1)}, f32[11,16,128]{2,1,0:T(8,128)S(1)}, u32[]{:S(2)}, u32[]{:S(2)}) collective-permute-start(f32[11,16,128]{2,1,0:T(8,128)S(1)} %get-tuple-element.156), channel_id=1, source_target_pairs={{0,16},{16,0},{32,48},{48,32},{64,80},{80,64},{96,112},{112,96},{1... | collective-permute-start | bytes 270344 | tf_op jit(solution)/shard_map/ppermute | solution.py:655
  45.9 2.9 %collective-permute-start.7 = (f32[11,16,128]{2,1,0:T(8,128)S(1)}, f32[11,16,128]{2,1,0:T(8,128)S(1)}, u32[]{:S(2)}, u32[]{:S(2)}) collective-permute-start(f32[11,16,128]{2,1,0:T(8,128)S(1)} %get-tuple-element.157), channel_id=1, source_target_pairs={{16,32},{32,16},{48,64},{64,48},{80,96},{96,80},{112,128},{128,112... | collective-permute-start | bytes 270344 | tf_op jit(solution)/shard_map/ppermute | solution.py:655
  48.8 0.3 collective-permute-done.13.refs_12_
  49.1 1.9 %shard_map.215 = (f32[3,6,16,384]{3,2,1,0:T(8,128)}, f32[3,6,16,384]{3,2,1,0:T(8,128)}, f32[3,6,16,384]{3,2,1,0:T(8,128)}, f32[3,6,16,384]{3,2,1,0:T(8,128)}, f3...) custom-call(f32[3,6,16,256]{3,2,1,0:T(8,128)S(1)} %get-tuple-element, ...), custom_call_target="tpu_custom_call" | custom-call | flops 4000000 | bytes 8000000 | tf_op jit(solution)/shard_map/pallas_call | solution.py:615
  51.1 3.0 %collective-permute-done.7.refs_12_ = f32[11,16,128]{2,1,0:T(8,128)S(1)} collective-permute-done((f32[11,16,128]{2,1,0:T(8,128)S(1)}, f32[11,16,128]{2,1,0:T(8,128)S(1)}, u32[]{:S(2)}, u32[]{:S(2)}) %collective-permute-start.7) | collective-permute-done | bytes 90144 | tf_op jit(solution)/shard_map/ppermute | solution.py:655
  54.1 2.3 %shard_map.216 = (f32[3,6,16,384]{3,2,1,0:T(8,128)}, f32[3,6,16,384]{3,2,1,0:T(8,128)}, f32[3,6,16,384]{3,2,1,0:T(8,128)}, f32[3,6,16,384]{3,2,1,0:T(8,128)}, f3...) custom-call(f32[3,6,16,256]{3,2,1,0:T(8,128)S(1)} %get-tuple-element, ...), custom_call_target="tpu_custom_call", output_to_operand_aliasing={{0}: (13, {}), {1}: (14, {}), {2}: (15, {}), {3}: (16, {}),... | custom-call | flops 4000000 | bytes 8000000 | tf_op jit(solution)/shard_map/pallas_call | solution.py:615
  (22 shorter events, 0.1 us)
Async XLA Ops:
  2.8 3.3 %copy-start.3 = (f32[8]{0:T(128)S(1)}, f32[8]{0:T(128)}, u32[]{:S(2)}) copy-start(f32[8]{0:T(128)} %param.24) | copy-start | bytes 100
  2.8 3.2 %copy-start.4 = (f32[8]{0:T(128)S(1)}, f32[8]{0:T(128)}, u32[]{:S(2)}) copy-start(f32[8]{0:T(128)} %param.23) | copy-start | bytes 100
  2.8 3.2 %copy-start = (f32[8]{0:T(128)S(1)}, f32[8]{0:T(128)}, u32[]{:S(2)}) copy-start(f32[8]{0:T(128)} %param.25) | copy-start | bytes 100
  2.8 3.2 %copy-start.1 = (f32[8]{0:T(128)S(1)}, f32[8]{0:T(128)}, u32[]{:S(2)}) copy-start(f32[8]{0:T(128)} %param.27) | copy-start | bytes 100
  2.8 3.2 %copy-start.2 = (f32[8]{0:T(128)S(1)}, f32[8]{0:T(128)}, u32[]{:S(2)}) copy-start(f32[8]{0:T(128)} %param.26) | copy-start | bytes 100
  2.8 5.3 %collective-permute-start = (f32[8,16,128]{2,1,0:T(8,128)S(1)}, f32[8,16,128]{2,1,0:T(8,128)S(1)}, u32[]{:S(2)}, u32[]{:S(2)}) collective-permute-start(f32[8,16,128]{2,1,0:T(8,128)S(1)} %get-tuple-element.123), channel_id=1, source_target_pairs={{0,1},{1,0},{2,3},{3,2},{4,5},{5,4},{6,7},{7,6},{8,9},{9,8},{10,11... | collective-permute-start | bytes 196616 | tf_op jit(solution)/shard_map/ppermute | solution.py:655
  2.9 3.1 %copy-start.5 = (f32[8]{0:T(128)S(1)}, f32[8]{0:T(128)}, u32[]{:S(2)}) copy-start(f32[8]{0:T(128)} %param.22) | copy-start | bytes 100
  2.9 5.9 %collective-permute-start.1 = (f32[8,16,128]{2,1,0:T(8,128)S(1)}, f32[8,16,128]{2,1,0:T(8,128)S(1)}, u32[]{:S(2)}, u32[]{:S(2)}) collective-permute-start(f32[8,16,128]{2,1,0:T(8,128)S(1)} %get-tuple-element.124), channel_id=1, source_target_pairs={{1,2},{2,1},{3,4},{4,3},{5,6},{6,5},{7,8},{8,7},{9,10},{10,9},{11,... | collective-permute-start | bytes 196616 | tf_op jit(solution)/shard_map/ppermute | solution.py:655
  10.2 14.3 %collective-permute-start.8 = (f32[13,16,128]{2,1,0:T(8,128)S(1)}, f32[13,16,128]{2,1,0:T(8,128)S(1)}, u32[]{:S(2)}, u32[]{:S(2)}) collective-permute-start(f32[13,16,128]{2,1,0:T(8,128)S(1)} %get-tuple-element.175), channel_id=1, source_target_pairs={{0,16},{16,0},{32,48},{48,32},{64,80},{80,64},{96,112},{112,96},{1... | collective-permute-start | bytes 319496 | tf_op jit(solution)/shard_map/ppermute | solution.py:655
  12.4 12.1 %collective-permute-start.9 = (f32[13,16,128]{2,1,0:T(8,128)S(1)}, f32[13,16,128]{2,1,0:T(8,128)S(1)}, u32[]{:S(2)}, u32[]{:S(2)}) collective-permute-start(f32[13,16,128]{2,1,0:T(8,128)S(1)} %get-tuple-element.176), channel_id=1, source_target_pairs={{16,32},{32,16},{48,64},{64,48},{80,96},{96,80},{112,128},{128,112... | collective-permute-start | bytes 319496 | tf_op jit(solution)/shard_map/ppermute | solution.py:655
  20.4 10.8 %collective-permute-start.2 = (f32[13,16,128]{2,1,0:T(8,128)S(1)}, f32[13,16,128]{2,1,0:T(8,128)S(1)}, u32[]{:S(2)}, u32[]{:S(2)}) collective-permute-start(f32[13,16,128]{2,1,0:T(8,128)S(1)} %get-tuple-element.135), channel_id=1, source_target_pairs={{0,16},{16,0},{32,48},{48,32},{64,80},{80,64},{96,112},{112,96},{1... | collective-permute-start | bytes 319496 | tf_op jit(solution)/shard_map/ppermute | solution.py:655
  20.5 10.7 %collective-permute-start.3 = (f32[13,16,128]{2,1,0:T(8,128)S(1)}, f32[13,16,128]{2,1,0:T(8,128)S(1)}, u32[]{:S(2)}, u32[]{:S(2)}) collective-permute-start(f32[13,16,128]{2,1,0:T(8,128)S(1)} %get-tuple-element.136), channel_id=1, source_target_pairs={{16,32},{32,16},{48,64},{64,48},{80,96},{96,80},{112,128},{128,112... | collective-permute-start | bytes 319496 | tf_op jit(solution)/shard_map/ppermute | solution.py:655
  26.3 9.9 %collective-permute-start.10 = (f32[11,16,128]{2,1,0:T(8,128)S(1)}, f32[11,16,128]{2,1,0:T(8,128)S(1)}, u32[]{:S(2)}, u32[]{:S(2)}) collective-permute-start(f32[11,16,128]{2,1,0:T(8,128)S(1)} %get-tuple-element.186), channel_id=1, source_target_pairs={{0,16},{16,0},{32,48},{48,32},{64,80},{80,64},{96,112},{112,96},{1... | collective-permute-start | bytes 270344 | tf_op jit(solution)/shard_map/ppermute | solution.py:655
  26.4 9.8 %collective-permute-start.11 = (f32[11,16,128]{2,1,0:T(8,128)S(1)}, f32[11,16,128]{2,1,0:T(8,128)S(1)}, u32[]{:S(2)}, u32[]{:S(2)}) collective-permute-start(f32[11,16,128]{2,1,0:T(8,128)S(1)} %get-tuple-element.187), channel_id=1, source_target_pairs={{16,32},{32,16},{48,64},{64,48},{80,96},{96,80},{112,128},{128,112... | collective-permute-start | bytes 270344 | tf_op jit(solution)/shard_map/ppermute | solution.py:655
  33.0 9.2 %collective-permute-start.4 = (f32[11,16,128]{2,1,0:T(8,128)S(1)}, f32[11,16,128]{2,1,0:T(8,128)S(1)}, u32[]{:S(2)}, u32[]{:S(2)}) collective-permute-start(f32[11,16,128]{2,1,0:T(8,128)S(1)} %get-tuple-element.146), channel_id=1, source_target_pairs={{0,16},{16,0},{32,48},{48,32},{64,80},{80,64},{96,112},{112,96},{1... | collective-permute-start | bytes 270344 | tf_op jit(solution)/shard_map/ppermute | solution.py:655
  33.1 9.1 %collective-permute-start.5 = (f32[11,16,128]{2,1,0:T(8,128)S(1)}, f32[11,16,128]{2,1,0:T(8,128)S(1)}, u32[]{:S(2)}, u32[]{:S(2)}) collective-permute-start(f32[11,16,128]{2,1,0:T(8,128)S(1)} %get-tuple-element.147), channel_id=1, source_target_pairs={{16,32},{32,16},{48,64},{64,48},{80,96},{96,80},{112,128},{128,112... | collective-permute-start | bytes 270344 | tf_op jit(solution)/shard_map/ppermute | solution.py:655
  37.8 11.0 %collective-permute-start.12 = (f32[11,16,128]{2,1,0:T(8,128)S(1)}, f32[11,16,128]{2,1,0:T(8,128)S(1)}, u32[]{:S(2)}, u32[]{:S(2)}) collective-permute-start(f32[11,16,128]{2,1,0:T(8,128)S(1)} %get-tuple-element.196), channel_id=1, source_target_pairs={{0,16},{16,0},{32,48},{48,32},{64,80},{80,64},{96,112},{112,96},{1... | collective-permute-start | bytes 270344 | tf_op jit(solution)/shard_map/ppermute | solution.py:655
  40.1 9.1 %collective-permute-start.13 = (f32[11,16,128]{2,1,0:T(8,128)S(1)}, f32[11,16,128]{2,1,0:T(8,128)S(1)}, u32[]{:S(2)}, u32[]{:S(2)}) collective-permute-start(f32[11,16,128]{2,1,0:T(8,128)S(1)} %get-tuple-element.197), channel_id=1, source_target_pairs={{16,32},{32,16},{48,64},{64,48},{80,96},{96,80},{112,128},{128,112... | collective-permute-start | bytes 270344 | tf_op jit(solution)/shard_map/ppermute | solution.py:655
  43.9 7.2 %collective-permute-start.6 = (f32[11,16,128]{2,1,0:T(8,128)S(1)}, f32[11,16,128]{2,1,0:T(8,128)S(1)}, u32[]{:S(2)}, u32[]{:S(2)}) collective-permute-start(f32[11,16,128]{2,1,0:T(8,128)S(1)} %get-tuple-element.156), channel_id=1, source_target_pairs={{0,16},{16,0},{32,48},{48,32},{64,80},{80,64},{96,112},{112,96},{1... | collective-permute-start | bytes 270344 | tf_op jit(solution)/shard_map/ppermute | solution.py:655
  45.9 8.1 %collective-permute-start.7 = (f32[11,16,128]{2,1,0:T(8,128)S(1)}, f32[11,16,128]{2,1,0:T(8,128)S(1)}, u32[]{:S(2)}, u32[]{:S(2)}) collective-permute-start(f32[11,16,128]{2,1,0:T(8,128)S(1)} %get-tuple-element.157), channel_id=1, source_target_pairs={{16,32},{32,16},{48,64},{64,48},{80,96},{96,80},{112,128},{128,112... | collective-permute-start | bytes 270344 | tf_op jit(solution)/shard_map/ppermute | solution.py:655

commit v4 on v3

--- a/solution.py
+++ b/solution.py
@@ -95,16 +95,17 @@
 
 
 def y_slots():
-    entries = [("f", a, k, x, GHOST) for a in range(5) for k in range(3) for x in range(ROWS)]
-    entries += [("m", 0, 0, x, GHOST) for x in range(ROWS)]
-    entries += [("c", a, k, r, CGHOST) for a in range(2) for k in range(3) for r in range(CROWS)]
-    entries += [("cm", 0, 0, r, CGHOST) for r in range(CROWS)]
-    entries += [("prior", 0, 0, 0, CGHOST)]
+    fine = [("m", 0, 0, x) for x in range(ROWS)]
+    fine += [("f", a, k, x) for a in range(5) for k in range(3) for x in range(ROWS)]
+    coarse = [("c", a, k, r) for a in range(2) for k in range(3) for r in range(CROWS)]
+    coarse += [("cm", 0, 0, r) for r in range(CROWS)] + [("prior", 0, 0, 0)]
     slots, plane, offset = {}, 0, 0
-    for *key, width in entries:
-        if offset + width > 128:
-            plane, offset = plane + 1, 0
-        slots[tuple(key)] = (plane, offset, width)
+    for keys, width in ((fine, GHOST), (coarse, CGHOST)):
+        for key in keys:
+            if offset + 2 * width > 128:
+                plane, offset = plane + 1, 0
+            slots[key] = (plane, offset, width)
+            offset += width
         offset += width
     return slots, plane + 1
 
@@ -146,10 +147,11 @@
             first = last = cmat[pl.ds(x, Z, stride=CROWS), :].astype(F32)
         else:
             first = last = jnp.concatenate([prior[...]] * (Z // 4), 0)
-        pair = (rolled(first, offset, 1), rolled(last, offset + width, 1))
+        both = rolled(first if first is last else jnp.where(lane < 64, first, last), offset + width, 1)
+        pair = (both, both)
         if plane in built:
-            keep = lane < offset
-            pair = tuple(jnp.where(keep, old, new) for old, new in zip(built[plane], pair))
+            starts = (offset + width, offset)
+            pair = tuple(jnp.where(lane < start, old, both) for old, start in zip(built[plane], starts))
         built[plane] = pair
     for plane, (one, other) in built.items():
         to_first[plane] = jnp.where(even, other, one)
@@ -161,7 +163,7 @@
     lane = lanes((Z, 128))
     if half == 0:
         return jnp.where(lane < 96, tile, rolled(message[plane], -offset - width, 1))
-    return jnp.where(lane < 32, rolled(message[plane], -offset, 1), tile)
+    return jnp.where(lane < 32, rolled(message[plane], -offset - width, 1), tile)
 
 
 def load_kernel(*refs):

time: 56.6 us -> 56.5 us (level)
  transfers between devices with their start and end apart: 14 -> 14, of which waited for: 3 -> 3; matrix products, arithmetic and copies ran while one was open for 0% -> 0% of each run, Pallas kernels for 21% -> 22%
where the time goes in v4:
time: 56.5 us; the launch traced here: 56.4 us
  starting transfers between devices  33.4 us (59%)
  Pallas kernels  17.7 us (31%)
  waiting for transfers between devices  4.11 us (7%)
  between operations  1 us (2%)
    ppermute x14, starting transfers between devices, exchanged(): swapped.append(lax.ppermute(message, axis, pairs))  33.4 us
    pallas_call x10, Pallas kernels, call(): pl.pallas_call(kernel, out_shape=outs, in_specs=specs or [FULL] * len(arg...  17.7 us
    ppermute x14, waiting for transfers between devices, exchanged(): swapped.append(lax.ppermute(message, axis, pairs))  4.11 us
  transfers between devices with their start and end apart: 14, of which 3 were waited for; matrix products, arithmetic and copies ran while one was open for 0% of the time, Pallas kernels for 22%

profile of v4, /device:TPU:2, one launch (start us, length us, event | category | flops | bytes accessed | tf_op | source)
XLA Modules:
  0.0 56.4 jit_solution(16560532290367848617)
XLA Ops:
  0.6 1.9 %shard_map.208 = (f32[8,16,128]{2,1,0:T(8,128)S(1)}, f32[8,16,128]{2,1,0:T(8,128)S(1)}) custom-call(f32[3,6,16,384]{3,2,1,0:T(8,128)} %bitcast.28, f32[3,6,16,384]{3,2,1,0:T(8,128)} %bitcast.30, f32[3,6,16,384]{3,2,1,0:T(8,128)} %bitcast.32, f32[3,6,16,384]{3,2,1,0:T(8,128)} %bitcast.34, f32[3,6,16,384]{3,2,1,0:T(8,128)} %bitcast.36, ...), custom_call_target="tpu_custom_call" | custom-call | flops 4000000 | bytes 8000000 | tf_op jit(solution)/shard_map/pallas_call | solution.py:617
  2.5 0.0 copy-start.3
  2.6 0.0 copy-start.4
  2.6 0.0 copy-start
  2.6 0.0 copy-start.1
  2.6 0.1 collective-permute-start
  2.7 0.0 copy-start.5
  2.7 3.1 %collective-permute-start.1 = (f32[8,16,128]{2,1,0:T(8,128)S(1)}, f32[8,16,128]{2,1,0:T(8,128)S(1)}, u32[]{:S(2)}, u32[]{:S(2)}) collective-permute-start(f32[8,16,128]{2,1,0:T(8,128)S(1)} %get-tuple-element.124), channel_id=1, source_target_pairs={{1,2},{2,1},{3,4},{4,3},{5,6},{6,5},{7,8},{8,7},{9,10},{10,9},{11,... | collective-permute-start | bytes 196616 | tf_op jit(solution)/shard_map/ppermute | solution.py:657
  5.9 2.0 %shard_map.207 = (f32[3,6,16,256]{3,2,1,0:T(8,128)S(1)}, f32[3,6,16,256]{3,2,1,0:T(8,128)S(1)}, f32[3,6,16,256]{3,2,1,0:T(8,128)S(1)}, f32[3,6,16,256]{3,2,1,0:T...) custom-call(f32[3,6,16,384]{3,2,1,0:T(8,128)} %bitcast.29, ...), custom_call_target="tpu_custom_call" | custom-call | flops 4000000 | bytes 8000000 | tf_op jit(solution)/shard_map/pallas_call | solution.py:617
  7.9 0.7 %collective-permute-done.1.refs_13_ = f32[8,16,128]{2,1,0:T(8,128)S(1)} collective-permute-done((f32[8,16,128]{2,1,0:T(8,128)S(1)}, f32[8,16,128]{2,1,0:T(8,128)S(1)}, u32[]{:S(2)}, u32[]{:S(2)}) %collective-permute-start.1) | collective-permute-done | bytes 65568 | tf_op jit(solution)/shard_map/ppermute | solution.py:657
  8.6 1.4 %shard_map.212 = (f32[3,6,16,256]{3,2,1,0:T(8,128)S(1)}, f32[3,6,16,256]{3,2,1,0:T(8,128)S(1)}, f32[3,6,16,256]{3,2,1,0:T(8,128)S(1)}, f32[3,6,16,256]{3,2,1,0:T...) custom-call(f32[3,6,16,256]{3,2,1,0:T(8,128)S(1)} %get-tuple-element, ...), custom_call_target="tpu_custom_call", output_to_operand_aliasing={{0}: (0, {}), {1}: (1, {}), {2}: (2, {}), {3}: (3, {}), {4}... | custom-call | flops 4000000 | bytes 8000000 | tf_op jit(solution)/shard_map/pallas_call | solution.py:617
  10.0 2.2 %collective-permute-start.8 = (f32[13,16,128]{2,1,0:T(8,128)S(1)}, f32[13,16,128]{2,1,0:T(8,128)S(1)}, u32[]{:S(2)}, u32[]{:S(2)}) collective-permute-start(f32[13,16,128]{2,1,0:T(8,128)S(1)} %get-tuple-element.175), channel_id=1, source_target_pairs={{0,16},{16,0},{32,48},{48,32},{64,80},{80,64},{96,112},{112,96},{1... | collective-permute-start | bytes 319496 | tf_op jit(solution)/shard_map/ppermute | solution.py:657
  12.2 6.7 %collective-permute-start.9 = (f32[13,16,128]{2,1,0:T(8,128)S(1)}, f32[13,16,128]{2,1,0:T(8,128)S(1)}, u32[]{:S(2)}, u32[]{:S(2)}) collective-permute-start(f32[13,16,128]{2,1,0:T(8,128)S(1)} %get-tuple-element.176), channel_id=1, source_target_pairs={{16,32},{32,16},{48,64},{64,48},{80,96},{96,80},{112,128},{128,112... | collective-permute-start | bytes 319496 | tf_op jit(solution)/shard_map/ppermute | solution.py:657
  18.9 1.4 %shard_map.209 = (f32[3,6,16,256]{3,2,1,0:T(8,128)S(1)}, f32[3,6,16,256]{3,2,1,0:T(8,128)S(1)}, f32[3,6,16,256]{3,2,1,0:T(8,128)S(1)}, f32[3,6,16,256]{3,2,1,0:T...) custom-call(f32[3,6,16,256]{3,2,1,0:T(8,128)S(1)} %get-tuple-element, ...), custom_call_target="tpu_custom_call", output_to_operand_aliasing={{0}: (0, {}), {1}: (1, {}), {2}: (2, {}), {3}: (3, {}), {4}... | custom-call | flops 4000000 | bytes 8000000 | tf_op jit(solution)/shard_map/pallas_call | solution.py:617
  20.3 0.1 collective-permute-start.2
  20.4 4.0 %collective-permute-start.3 = (f32[13,16,128]{2,1,0:T(8,128)S(1)}, f32[13,16,128]{2,1,0:T(8,128)S(1)}, u32[]{:S(2)}, u32[]{:S(2)}) collective-permute-start(f32[13,16,128]{2,1,0:T(8,128)S(1)} %get-tuple-element.136), channel_id=1, source_target_pairs={{16,32},{32,16},{48,64},{64,48},{80,96},{96,80},{112,128},{128,112... | collective-permute-start | bytes 319496 | tf_op jit(solution)/shard_map/ppermute | solution.py:657
  24.4 1.7 %shard_map.213 = (f32[3,6,16,256]{3,2,1,0:T(8,128)S(1)}, f32[3,6,16,256]{3,2,1,0:T(8,128)S(1)}, f32[3,6,16,256]{3,2,1,0:T(8,128)S(1)}, f32[3,6,16,256]{3,2,1,0:T...) custom-call(f32[3,6,16,256]{3,2,1,0:T(8,128)S(1)} %get-tuple-element, ...), custom_call_target="tpu_custom_call" | custom-call | flops 4000000 | bytes 8000000 | tf_op jit(solution)/shard_map/pallas_call | solution.py:617
  26.1 0.1 collective-permute-start.10
  26.2 4.8 %collective-permute-start.11 = (f32[11,16,128]{2,1,0:T(8,128)S(1)}, f32[11,16,128]{2,1,0:T(8,128)S(1)}, u32[]{:S(2)}, u32[]{:S(2)}) collective-permute-start(f32[11,16,128]{2,1,0:T(8,128)S(1)} %get-tuple-element.187), channel_id=1, source_target_pairs={{16,32},{32,16},{48,64},{64,48},{80,96},{96,80},{112,128},{128,112... | collective-permute-start | bytes 270344 | tf_op jit(solution)/shard_map/ppermute | solution.py:657
  31.0 1.7 %shard_map.210 = (f32[3,6,16,256]{3,2,1,0:T(8,128)S(1)}, f32[3,6,16,256]{3,2,1,0:T(8,128)S(1)}, f32[3,6,16,256]{3,2,1,0:T(8,128)S(1)}, f32[3,6,16,256]{3,2,1,0:T...) custom-call(f32[3,6,16,256]{3,2,1,0:T(8,128)S(1)} %get-tuple-element, ...), custom_call_target="tpu_custom_call" | custom-call | flops 4000000 | bytes 8000000 | tf_op jit(solution)/shard_map/pallas_call | solution.py:617
  32.7 0.1 collective-permute-start.4
  32.9 3.1 %collective-permute-start.5 = (f32[11,16,128]{2,1,0:T(8,128)S(1)}, f32[11,16,128]{2,1,0:T(8,128)S(1)}, u32[]{:S(2)}, u32[]{:S(2)}) collective-permute-start(f32[11,16,128]{2,1,0:T(8,128)S(1)} %get-tuple-element.147), channel_id=1, source_target_pairs={{16,32},{32,16},{48,64},{64,48},{80,96},{96,80},{112,128},{128,112... | collective-permute-start | bytes 270344 | tf_op jit(solution)/shard_map/ppermute | solution.py:657
  36.0 1.7 %shard_map.214 = (f32[3,6,16,256]{3,2,1,0:T(8,128)S(1)}, f32[3,6,16,256]{3,2,1,0:T(8,128)S(1)}, f32[3,6,16,256]{3,2,1,0:T(8,128)S(1)}, f32[3,6,16,256]{3,2,1,0:T...) custom-call(f32[3,6,16,256]{3,2,1,0:T(8,128)S(1)} %get-tuple-element, ...), custom_call_target="tpu_custom_call" | custom-call | flops 4000000 | bytes 8000000 | tf_op jit(solution)/shard_map/pallas_call | solution.py:617
  37.7 2.2 %collective-permute-start.12 = (f32[11,16,128]{2,1,0:T(8,128)S(1)}, f32[11,16,128]{2,1,0:T(8,128)S(1)}, u32[]{:S(2)}, u32[]{:S(2)}) collective-permute-start(f32[11,16,128]{2,1,0:T(8,128)S(1)} %get-tuple-element.196), channel_id=1, source_target_pairs={{0,16},{16,0},{32,48},{48,32},{64,80},{80,64},{96,112},{112,96},{1... | collective-permute-start | bytes 270344 | tf_op jit(solution)/shard_map/ppermute | solution.py:657
  39.9 2.0 %collective-permute-start.13 = (f32[11,16,128]{2,1,0:T(8,128)S(1)}, f32[11,16,128]{2,1,0:T(8,128)S(1)}, u32[]{:S(2)}, u32[]{:S(2)}) collective-permute-start(f32[11,16,128]{2,1,0:T(8,128)S(1)} %get-tuple-element.197), channel_id=1, source_target_pairs={{16,32},{32,16},{48,64},{64,48},{80,96},{96,80},{112,128},{128,112... | collective-permute-start | bytes 270344 | tf_op jit(solution)/shard_map/ppermute | solution.py:657
  41.9 1.7 %shard_map.211 = (f32[3,6,16,256]{3,2,1,0:T(8,128)S(1)}, f32[3,6,16,256]{3,2,1,0:T(8,128)S(1)}, f32[3,6,16,256]{3,2,1,0:T(8,128)S(1)}, f32[3,6,16,256]{3,2,1,0:T...) custom-call(f32[3,6,16,256]{3,2,1,0:T(8,128)S(1)} %get-tuple-element, ...), custom_call_target="tpu_custom_call" | custom-call | flops 4000000 | bytes 8000000 | tf_op jit(solution)/shard_map/pallas_call | solution.py:617
  43.6 2.2 %collective-permute-start.6 = (f32[11,16,128]{2,1,0:T(8,128)S(1)}, f32[11,16,128]{2,1,0:T(8,128)S(1)}, u32[]{:S(2)}, u32[]{:S(2)}) collective-permute-start(f32[11,16,128]{2,1,0:T(8,128)S(1)} %get-tuple-element.156), channel_id=1, source_target_pairs={{0,16},{16,0},{32,48},{48,32},{64,80},{80,64},{96,112},{112,96},{1... | collective-permute-start | bytes 270344 | tf_op jit(solution)/shard_map/ppermute | solution.py:657
  45.8 2.8 %collective-permute-start.7 = (f32[11,16,128]{2,1,0:T(8,128)S(1)}, f32[11,16,128]{2,1,0:T(8,128)S(1)}, u32[]{:S(2)}, u32[]{:S(2)}) collective-permute-start(f32[11,16,128]{2,1,0:T(8,128)S(1)} %get-tuple-element.157), channel_id=1, source_target_pairs={{16,32},{32,16},{48,64},{64,48},{80,96},{96,80},{112,128},{128,112... | collective-permute-start | bytes 270344 | tf_op jit(solution)/shard_map/ppermute | solution.py:657
  48.6 0.4 collective-permute-done.13.refs_12_
  49.0 1.9 %shard_map.215 = (f32[3,6,16,384]{3,2,1,0:T(8,128)}, f32[3,6,16,384]{3,2,1,0:T(8,128)}, f32[3,6,16,384]{3,2,1,0:T(8,128)}, f32[3,6,16,384]{3,2,1,0:T(8,128)}, f3...) custom-call(f32[3,6,16,256]{3,2,1,0:T(8,128)S(1)} %get-tuple-element, ...), custom_call_target="tpu_custom_call" | custom-call | flops 4000000 | bytes 8000000 | tf_op jit(solution)/shard_map/pallas_call | solution.py:617
  51.0 3.0 %collective-permute-done.7.refs_12_ = f32[11,16,128]{2,1,0:T(8,128)S(1)} collective-permute-done((f32[11,16,128]{2,1,0:T(8,128)S(1)}, f32[11,16,128]{2,1,0:T(8,128)S(1)}, u32[]{:S(2)}, u32[]{:S(2)}) %collective-permute-start.7) | collective-permute-done | bytes 90144 | tf_op jit(solution)/shard_map/ppermute | solution.py:657
  53.9 2.3 %shard_map.216 = (f32[3,6,16,384]{3,2,1,0:T(8,128)}, f32[3,6,16,384]{3,2,1,0:T(8,128)}, f32[3,6,16,384]{3,2,1,0:T(8,128)}, f32[3,6,16,384]{3,2,1,0:T(8,128)}, f3...) custom-call(f32[3,6,16,256]{3,2,1,0:T(8,128)S(1)} %get-tuple-element, ...), custom_call_target="tpu_custom_call", output_to_operand_aliasing={{0}: (13, {}), {1}: (14, {}), {2}: (15, {}), {3}: (16, {}),... | custom-call | flops 4000000 | bytes 8000000 | tf_op jit(solution)/shard_map/pallas_call | solution.py:617
  (22 shorter events, 0.1 us)
Async XLA Ops:
  2.5 3.3 %copy-start.3 = (f32[8]{0:T(128)S(1)}, f32[8]{0:T(128)}, u32[]{:S(2)}) copy-start(f32[8]{0:T(128)} %param.24) | copy-start | bytes 100
  2.6 3.2 %copy-start.4 = (f32[8]{0:T(128)S(1)}, f32[8]{0:T(128)}, u32[]{:S(2)}) copy-start(f32[8]{0:T(128)} %param.23) | copy-start | bytes 100
  2.6 3.2 %copy-start = (f32[8]{0:T(128)S(1)}, f32[8]{0:T(128)}, u32[]{:S(2)}) copy-start(f32[8]{0:T(128)} %param.25) | copy-start | bytes 100
  2.6 3.2 %copy-start.1 = (f32[8]{0:T(128)S(1)}, f32[8]{0:T(128)}, u32[]{:S(2)}) copy-start(f32[8]{0:T(128)} %param.27) | copy-start | bytes 100
  2.6 3.2 %copy-start.2 = (f32[8]{0:T(128)S(1)}, f32[8]{0:T(128)}, u32[]{:S(2)}) copy-start(f32[8]{0:T(128)} %param.26) | copy-start | bytes 100
  2.6 5.3 %collective-permute-start = (f32[8,16,128]{2,1,0:T(8,128)S(1)}, f32[8,16,128]{2,1,0:T(8,128)S(1)}, u32[]{:S(2)}, u32[]{:S(2)}) collective-permute-start(f32[8,16,128]{2,1,0:T(8,128)S(1)} %get-tuple-element.123), channel_id=1, source_target_pairs={{0,1},{1,0},{2,3},{3,2},{4,5},{5,4},{6,7},{7,6},{8,9},{9,8},{10,11... | collective-permute-start | bytes 196616 | tf_op jit(solution)/shard_map/ppermute | solution.py:657
  2.7 3.1 %copy-start.5 = (f32[8]{0:T(128)S(1)}, f32[8]{0:T(128)}, u32[]{:S(2)}) copy-start(f32[8]{0:T(128)} %param.22) | copy-start | bytes 100
  2.7 5.9 %collective-permute-start.1 = (f32[8,16,128]{2,1,0:T(8,128)S(1)}, f32[8,16,128]{2,1,0:T(8,128)S(1)}, u32[]{:S(2)}, u32[]{:S(2)}) collective-permute-start(f32[8,16,128]{2,1,0:T(8,128)S(1)} %get-tuple-element.124), channel_id=1, source_target_pairs={{1,2},{2,1},{3,4},{4,3},{5,6},{6,5},{7,8},{8,7},{9,10},{10,9},{11,... | collective-permute-start | bytes 196616 | tf_op jit(solution)/shard_map/ppermute | solution.py:657
  10.0 14.4 %collective-permute-start.8 = (f32[13,16,128]{2,1,0:T(8,128)S(1)}, f32[13,16,128]{2,1,0:T(8,128)S(1)}, u32[]{:S(2)}, u32[]{:S(2)}) collective-permute-start(f32[13,16,128]{2,1,0:T(8,128)S(1)} %get-tuple-element.175), channel_id=1, source_target_pairs={{0,16},{16,0},{32,48},{48,32},{64,80},{80,64},{96,112},{112,96},{1... | collective-permute-start | bytes 319496 | tf_op jit(solution)/shard_map/ppermute | solution.py:657
  12.2 12.2 %collective-permute-start.9 = (f32[13,16,128]{2,1,0:T(8,128)S(1)}, f32[13,16,128]{2,1,0:T(8,128)S(1)}, u32[]{:S(2)}, u32[]{:S(2)}) collective-permute-start(f32[13,16,128]{2,1,0:T(8,128)S(1)} %get-tuple-element.176), channel_id=1, source_target_pairs={{16,32},{32,16},{48,64},{64,48},{80,96},{96,80},{112,128},{128,112... | collective-permute-start | bytes 319496 | tf_op jit(solution)/shard_map/ppermute | solution.py:657
  20.3 10.7 %collective-permute-start.2 = (f32[13,16,128]{2,1,0:T(8,128)S(1)}, f32[13,16,128]{2,1,0:T(8,128)S(1)}, u32[]{:S(2)}, u32[]{:S(2)}) collective-permute-start(f32[13,16,128]{2,1,0:T(8,128)S(1)} %get-tuple-element.135), channel_id=1, source_target_pairs={{0,16},{16,0},{32,48},{48,32},{64,80},{80,64},{96,112},{112,96},{1... | collective-permute-start | bytes 319496 | tf_op jit(solution)/shard_map/ppermute | solution.py:657
  20.4 10.6 %collective-permute-start.3 = (f32[13,16,128]{2,1,0:T(8,128)S(1)}, f32[13,16,128]{2,1,0:T(8,128)S(1)}, u32[]{:S(2)}, u32[]{:S(2)}) collective-permute-start(f32[13,16,128]{2,1,0:T(8,128)S(1)} %get-tuple-element.136), channel_id=1, source_target_pairs={{16,32},{32,16},{48,64},{64,48},{80,96},{96,80},{112,128},{128,112... | collective-permute-start | bytes 319496 | tf_op jit(solution)/shard_map/ppermute | solution.py:657
  26.1 9.9 %collective-permute-start.10 = (f32[11,16,128]{2,1,0:T(8,128)S(1)}, f32[11,16,128]{2,1,0:T(8,128)S(1)}, u32[]{:S(2)}, u32[]{:S(2)}) collective-permute-start(f32[11,16,128]{2,1,0:T(8,128)S(1)} %get-tuple-element.186), channel_id=1, source_target_pairs={{0,16},{16,0},{32,48},{48,32},{64,80},{80,64},{96,112},{112,96},{1... | collective-permute-start | bytes 270344 | tf_op jit(solution)/shard_map/ppermute | solution.py:657
  26.2 9.8 %collective-permute-start.11 = (f32[11,16,128]{2,1,0:T(8,128)S(1)}, f32[11,16,128]{2,1,0:T(8,128)S(1)}, u32[]{:S(2)}, u32[]{:S(2)}) collective-permute-start(f32[11,16,128]{2,1,0:T(8,128)S(1)} %get-tuple-element.187), channel_id=1, source_target_pairs={{16,32},{32,16},{48,64},{64,48},{80,96},{96,80},{112,128},{128,112... | collective-permute-start | bytes 270344 | tf_op jit(solution)/shard_map/ppermute | solution.py:657
  32.7 9.2 %collective-permute-start.4 = (f32[11,16,128]{2,1,0:T(8,128)S(1)}, f32[11,16,128]{2,1,0:T(8,128)S(1)}, u32[]{:S(2)}, u32[]{:S(2)}) collective-permute-start(f32[11,16,128]{2,1,0:T(8,128)S(1)} %get-tuple-element.146), channel_id=1, source_target_pairs={{0,16},{16,0},{32,48},{48,32},{64,80},{80,64},{96,112},{112,96},{1... | collective-permute-start | bytes 270344 | tf_op jit(solution)/shard_map/ppermute | solution.py:657
  32.9 9.0 %collective-permute-start.5 = (f32[11,16,128]{2,1,0:T(8,128)S(1)}, f32[11,16,128]{2,1,0:T(8,128)S(1)}, u32[]{:S(2)}, u32[]{:S(2)}) collective-permute-start(f32[11,16,128]{2,1,0:T(8,128)S(1)} %get-tuple-element.147), channel_id=1, source_target_pairs={{16,32},{32,16},{48,64},{64,48},{80,96},{96,80},{112,128},{128,112... | collective-permute-start | bytes 270344 | tf_op jit(solution)/shard_map/ppermute | solution.py:657
  37.7 10.9 %collective-permute-start.12 = (f32[11,16,128]{2,1,0:T(8,128)S(1)}, f32[11,16,128]{2,1,0:T(8,128)S(1)}, u32[]{:S(2)}, u32[]{:S(2)}) collective-permute-start(f32[11,16,128]{2,1,0:T(8,128)S(1)} %get-tuple-element.196), channel_id=1, source_target_pairs={{0,16},{16,0},{32,48},{48,32},{64,80},{80,64},{96,112},{112,96},{1... | collective-permute-start | bytes 270344 | tf_op jit(solution)/shard_map/ppermute | solution.py:657
  39.9 9.1 %collective-permute-start.13 = (f32[11,16,128]{2,1,0:T(8,128)S(1)}, f32[11,16,128]{2,1,0:T(8,128)S(1)}, u32[]{:S(2)}, u32[]{:S(2)}) collective-permute-start(f32[11,16,128]{2,1,0:T(8,128)S(1)} %get-tuple-element.197), channel_id=1, source_target_pairs={{16,32},{32,16},{48,64},{64,48},{80,96},{96,80},{112,128},{128,112... | collective-permute-start | bytes 270344 | tf_op jit(solution)/shard_map/ppermute | solution.py:657
  43.6 7.4 %collective-permute-start.6 = (f32[11,16,128]{2,1,0:T(8,128)S(1)}, f32[11,16,128]{2,1,0:T(8,128)S(1)}, u32[]{:S(2)}, u32[]{:S(2)}) collective-permute-start(f32[11,16,128]{2,1,0:T(8,128)S(1)} %get-tuple-element.156), channel_id=1, source_target_pairs={{0,16},{16,0},{32,48},{48,32},{64,80},{80,64},{96,112},{112,96},{1... | collective-permute-start | bytes 270344 | tf_op jit(solution)/shard_map/ppermute | solution.py:657
  45.8 8.1 %collective-permute-start.7 = (f32[11,16,128]{2,1,0:T(8,128)S(1)}, f32[11,16,128]{2,1,0:T(8,128)S(1)}, u32[]{:S(2)}, u32[]{:S(2)}) collective-permute-start(f32[11,16,128]{2,1,0:T(8,128)S(1)} %get-tuple-element.157), channel_id=1, source_target_pairs={{16,32},{32,16},{48,64},{64,48},{80,96},{96,80},{112,128},{128,112... | collective-permute-start | bytes 270344 | tf_op jit(solution)/shard_map/ppermute | solution.py:657

commit v5 on v4

--- a/solution.py
+++ b/solution.py
@@ -129,14 +129,19 @@
     pairs.append((material.at[:, :, OWN - 128 : OWN], mats.at[1]))
     pairs += [(ce_in, ce), (ch_in, ch), (cmat_in, cmat), (prior_in, prior)]
     copies = [pltpu.make_async_copy(src, dst, sems.at[i]) for i, (src, dst) in enumerate(pairs)]
-    for copy in copies:
+    early = copies[10:12] + copies[0:4]
+    late = copies[4:10] + copies[12:]
+    for copy in early + late:
         copy.start()
-    for copy in copies:
+    for copy in early:
         copy.wait()
     lane = lanes((Z, 128))
     built = {}
     for key, (plane, offset, width) in Y_SLOTS.items():
         kind, a, k, x = key
+        if key == ("f", 2, 0, 0):
+            for copy in late:
+                copy.wait()
         if kind == "f":
             first, last = firsts[a, k, x], lasts[a, k, x]
         elif kind == "m":
@@ -422,7 +427,7 @@
     send_edges(half, True, fields, c, ce, ch, pl_ref, mat, to_first, to_second)
 
 
-def coarse_step(half, first, olds, news, c, ghost, olds_c, news_c, inv, pl_ref, from_left, from_right, finished=None):
+def coarse_step(half, first, olds, news, c, ghost, olds_c, news_c, inv, pl_ref, from_left, from_right, finished=None, merged=None):
     e_items, h_items = x_items(first)
     zero = jnp.zeros((Z, W), F32)
     flat = (0.0, 0.0)
@@ -462,9 +467,9 @@
             for x in range(ROWS):
                 for k in range(3):
                     v2 = c[3, x] * fv[k, x] + c[4, x] * (c[5, x] * fe[k, x] - fp[k, x])
-                    news[2][k, x] = c[1, x] * fj[k, x] + c[2, x] * fe[k, x]
-                    news[3][k, x] = fp[k, x] + TIMESTEP * v2
-                    news[4][k, x] = v2
+                    news[2][k, x] = merged(2, k, x, c[1, x] * fj[k, x] + c[2, x] * fe[k, x])
+                    news[3][k, x] = merged(3, k, x, fp[k, x] + TIMESTEP * v2)
+                    news[4][k, x] = merged(4, k, x, v2)
             finished((2, 3, 4))
         for x in range(ROWS):
             upper = row_of(fe, x + 1) if x + 1 < ROWS else None
@@ -472,7 +477,7 @@
                 row_of(fh, x), row_of(fe, x), upper[1:] if upper else following, top_plane(pl_ref, x, t)
             )
             for k in range(3):
-                news[1][k, x] = h[k]
+                news[1][k, x] = merged(1, k, x, h[k]) if last else h[k]
             for k in range(2):
                 part = h[k][8:Z]
                 have = summed[k][x // RATIO]
@@ -484,7 +489,8 @@
             if last:
                 curl = curl_h(h, preceding, flat)
                 for k in range(3):
-                    news[0][k, x] = fe[k, x] + c[0, x] * (curl[k] - fj[k, x] - fv[k, x])
+                    e2 = fe[k, x] + c[0, x] * (curl[k] - fj[k, x] - fv[k, x])
+                    news[0][k, x] = merged(0, k, x, e2)
                 preceding = h[1:]
                 continue
             e2, j2, p2, v2 = e_row(
@@ -579,6 +585,12 @@
         copies.append(pltpu.make_async_copy(coarse_parts[a], outs_c[a], sems.at[5 + a]))
         copies[-1].start()
 
+    def merged(a, k, x, value):
+        if half == 0:
+            return value
+        shared = jnp.where(first, others[a][k, x, :, 128:256], value[:, 0:128])
+        return jnp.concatenate([shared, value[:, 128:256]], 1)
+
     def finished(arrays):
         for a in arrays:
             if a >= 5:
@@ -587,17 +599,12 @@
             if half == 0:
                 source, target = news[a].at[:, :, :, 0:128], outs[a].at[:, :, :, 0:128]
             else:
-                for x in range(ROWS):
-                    for k in range(3):
-                        news[a][k, x, :, 0:128] = jnp.where(
-                            first, others[a][k, x, :, 128:256], news[a][k, x, :, 0:128]
-                        )
                 source, target = news[a], outs[a].at[:, :, :, 128:384]
             copies.append(pltpu.make_async_copy(source, target, sems.at[a]))
             copies[-1].start()
 
     coarse_step(
-        half, False, olds, news, c, ghost, (ce0, ch0), (ce, ch), inv, pl0, from_left, from_right, finished
+        half, False, olds, news, c, ghost, (ce0, ch0), (ce, ch), inv, pl0, from_left, from_right, finished, merged
     )
     for copy in copies:
         copy.wait()

time: 56.5 us -> 56.4 us (level)
  no operation moved by 1% of the time
where the time goes in v5:
time: 56.4 us; the launch traced here: 56.3 us
  starting transfers between devices  33.4 us (59%)
  Pallas kernels  17.7 us (31%)
  waiting for transfers between devices  4.11 us (7%)
  between operations  1 us (2%)
    ppermute x14, starting transfers between devices, exchanged(): swapped.append(lax.ppermute(message, axis, pairs))  33.4 us
    pallas_call x10, Pallas kernels, call(): pl.pallas_call(kernel, out_shape=outs, in_specs=specs or [FULL] * len(arg...  17.7 us
    ppermute x14, waiting for transfers between devices, exchanged(): swapped.append(lax.ppermute(message, axis, pairs))  4.11 us
  transfers between devices with their start and end apart: 14, of which 3 were waited for; matrix products, arithmetic and copies ran while one was open for 0% of the time, Pallas kernels for 22%

profile of v5, /device:TPU:2, one launch (start us, length us, event | category | flops | bytes accessed | tf_op | source)
XLA Modules:
  0.0 56.3 jit_solution(4631284756114477863)
XLA Ops:
  0.6 1.8 %shard_map.208 = (f32[8,16,128]{2,1,0:T(8,128)S(1)}, f32[8,16,128]{2,1,0:T(8,128)S(1)}) custom-call(f32[3,6,16,384]{3,2,1,0:T(8,128)} %bitcast.28, f32[3,6,16,384]{3,2,1,0:T(8,128)} %bitcast.30, f32[3,6,16,384]{3,2,1,0:T(8,128)} %bitcast.32, f32[3,6,16,384]{3,2,1,0:T(8,128)} %bitcast.34, f32[3,6,16,384]{3,2,1,0:T(8,128)} %bitcast.36, ...), custom_call_target="tpu_custom_call" | custom-call | flops 4000000 | bytes 8000000 | tf_op jit(solution)/shard_map/pallas_call | solution.py:624
  2.5 0.0 copy-start.3
  2.5 0.0 copy-start.4
  2.5 0.0 copy-start
  2.5 0.0 copy-start.1
  2.5 0.0 copy-start.2
  2.5 0.1 collective-permute-start
  2.7 3.1 %collective-permute-start.1 = (f32[8,16,128]{2,1,0:T(8,128)S(1)}, f32[8,16,128]{2,1,0:T(8,128)S(1)}, u32[]{:S(2)}, u32[]{:S(2)}) collective-permute-start(f32[8,16,128]{2,1,0:T(8,128)S(1)} %get-tuple-element.124), channel_id=1, source_target_pairs={{1,2},{2,1},{3,4},{4,3},{5,6},{6,5},{7,8},{8,7},{9,10},{10,9},{11,... | collective-permute-start | bytes 196616 | tf_op jit(solution)/shard_map/ppermute | solution.py:664
  5.8 2.0 %shard_map.207 = (f32[3,6,16,256]{3,2,1,0:T(8,128)S(1)}, f32[3,6,16,256]{3,2,1,0:T(8,128)S(1)}, f32[3,6,16,256]{3,2,1,0:T(8,128)S(1)}, f32[3,6,16,256]{3,2,1,0:T...) custom-call(f32[3,6,16,384]{3,2,1,0:T(8,128)} %bitcast.29, ...), custom_call_target="tpu_custom_call" | custom-call | flops 4000000 | bytes 8000000 | tf_op jit(solution)/shard_map/pallas_call | solution.py:624
  7.9 0.7 %collective-permute-done.1.refs_13_ = f32[8,16,128]{2,1,0:T(8,128)S(1)} collective-permute-done((f32[8,16,128]{2,1,0:T(8,128)S(1)}, f32[8,16,128]{2,1,0:T(8,128)S(1)}, u32[]{:S(2)}, u32[]{:S(2)}) %collective-permute-start.1) | collective-permute-done | bytes 65568 | tf_op jit(solution)/shard_map/ppermute | solution.py:664
  8.5 1.4 %shard_map.212 = (f32[3,6,16,256]{3,2,1,0:T(8,128)S(1)}, f32[3,6,16,256]{3,2,1,0:T(8,128)S(1)}, f32[3,6,16,256]{3,2,1,0:T(8,128)S(1)}, f32[3,6,16,256]{3,2,1,0:T...) custom-call(f32[3,6,16,256]{3,2,1,0:T(8,128)S(1)} %get-tuple-element, ...), custom_call_target="tpu_custom_call", output_to_operand_aliasing={{0}: (0, {}), {1}: (1, {}), {2}: (2, {}), {3}: (3, {}), {4}... | custom-call | flops 4000000 | bytes 8000000 | tf_op jit(solution)/shard_map/pallas_call | solution.py:624
  9.9 2.2 %collective-permute-start.8 = (f32[13,16,128]{2,1,0:T(8,128)S(1)}, f32[13,16,128]{2,1,0:T(8,128)S(1)}, u32[]{:S(2)}, u32[]{:S(2)}) collective-permute-start(f32[13,16,128]{2,1,0:T(8,128)S(1)} %get-tuple-element.175), channel_id=1, source_target_pairs={{0,16},{16,0},{32,48},{48,32},{64,80},{80,64},{96,112},{112,96},{1... | collective-permute-start | bytes 319496 | tf_op jit(solution)/shard_map/ppermute | solution.py:664
  12.1 6.7 %collective-permute-start.9 = (f32[13,16,128]{2,1,0:T(8,128)S(1)}, f32[13,16,128]{2,1,0:T(8,128)S(1)}, u32[]{:S(2)}, u32[]{:S(2)}) collective-permute-start(f32[13,16,128]{2,1,0:T(8,128)S(1)} %get-tuple-element.176), channel_id=1, source_target_pairs={{16,32},{32,16},{48,64},{64,48},{80,96},{96,80},{112,128},{128,112... | collective-permute-start | bytes 319496 | tf_op jit(solution)/shard_map/ppermute | solution.py:664
  18.8 1.4 %shard_map.209 = (f32[3,6,16,256]{3,2,1,0:T(8,128)S(1)}, f32[3,6,16,256]{3,2,1,0:T(8,128)S(1)}, f32[3,6,16,256]{3,2,1,0:T(8,128)S(1)}, f32[3,6,16,256]{3,2,1,0:T...) custom-call(f32[3,6,16,256]{3,2,1,0:T(8,128)S(1)} %get-tuple-element, ...), custom_call_target="tpu_custom_call", output_to_operand_aliasing={{0}: (0, {}), {1}: (1, {}), {2}: (2, {}), {3}: (3, {}), {4}... | custom-call | flops 4000000 | bytes 8000000 | tf_op jit(solution)/shard_map/pallas_call | solution.py:624
  20.2 0.1 collective-permute-start.2
  20.3 4.0 %collective-permute-start.3 = (f32[13,16,128]{2,1,0:T(8,128)S(1)}, f32[13,16,128]{2,1,0:T(8,128)S(1)}, u32[]{:S(2)}, u32[]{:S(2)}) collective-permute-start(f32[13,16,128]{2,1,0:T(8,128)S(1)} %get-tuple-element.136), channel_id=1, source_target_pairs={{16,32},{32,16},{48,64},{64,48},{80,96},{96,80},{112,128},{128,112... | collective-permute-start | bytes 319496 | tf_op jit(solution)/shard_map/ppermute | solution.py:664
  24.3 1.7 %shard_map.213 = (f32[3,6,16,256]{3,2,1,0:T(8,128)S(1)}, f32[3,6,16,256]{3,2,1,0:T(8,128)S(1)}, f32[3,6,16,256]{3,2,1,0:T(8,128)S(1)}, f32[3,6,16,256]{3,2,1,0:T...) custom-call(f32[3,6,16,256]{3,2,1,0:T(8,128)S(1)} %get-tuple-element, ...), custom_call_target="tpu_custom_call" | custom-call | flops 4000000 | bytes 8000000 | tf_op jit(solution)/shard_map/pallas_call | solution.py:624
  26.1 0.1 collective-permute-start.10
  26.2 4.8 %collective-permute-start.11 = (f32[11,16,128]{2,1,0:T(8,128)S(1)}, f32[11,16,128]{2,1,0:T(8,128)S(1)}, u32[]{:S(2)}, u32[]{:S(2)}) collective-permute-start(f32[11,16,128]{2,1,0:T(8,128)S(1)} %get-tuple-element.187), channel_id=1, source_target_pairs={{16,32},{32,16},{48,64},{64,48},{80,96},{96,80},{112,128},{128,112... | collective-permute-start | bytes 270344 | tf_op jit(solution)/shard_map/ppermute | solution.py:664
  30.9 1.7 %shard_map.210 = (f32[3,6,16,256]{3,2,1,0:T(8,128)S(1)}, f32[3,6,16,256]{3,2,1,0:T(8,128)S(1)}, f32[3,6,16,256]{3,2,1,0:T(8,128)S(1)}, f32[3,6,16,256]{3,2,1,0:T...) custom-call(f32[3,6,16,256]{3,2,1,0:T(8,128)S(1)} %get-tuple-element, ...), custom_call_target="tpu_custom_call" | custom-call | flops 4000000 | bytes 8000000 | tf_op jit(solution)/shard_map/pallas_call | solution.py:624
  32.7 0.1 collective-permute-start.4
  32.8 3.1 %collective-permute-start.5 = (f32[11,16,128]{2,1,0:T(8,128)S(1)}, f32[11,16,128]{2,1,0:T(8,128)S(1)}, u32[]{:S(2)}, u32[]{:S(2)}) collective-permute-start(f32[11,16,128]{2,1,0:T(8,128)S(1)} %get-tuple-element.147), channel_id=1, source_target_pairs={{16,32},{32,16},{48,64},{64,48},{80,96},{96,80},{112,128},{128,112... | collective-permute-start | bytes 270344 | tf_op jit(solution)/shard_map/ppermute | solution.py:664
  35.9 1.7 %shard_map.214 = (f32[3,6,16,256]{3,2,1,0:T(8,128)S(1)}, f32[3,6,16,256]{3,2,1,0:T(8,128)S(1)}, f32[3,6,16,256]{3,2,1,0:T(8,128)S(1)}, f32[3,6,16,256]{3,2,1,0:T...) custom-call(f32[3,6,16,256]{3,2,1,0:T(8,128)S(1)} %get-tuple-element, ...), custom_call_target="tpu_custom_call" | custom-call | flops 4000000 | bytes 8000000 | tf_op jit(solution)/shard_map/pallas_call | solution.py:624
  37.6 2.2 %collective-permute-start.12 = (f32[11,16,128]{2,1,0:T(8,128)S(1)}, f32[11,16,128]{2,1,0:T(8,128)S(1)}, u32[]{:S(2)}, u32[]{:S(2)}) collective-permute-start(f32[11,16,128]{2,1,0:T(8,128)S(1)} %get-tuple-element.196), channel_id=1, source_target_pairs={{0,16},{16,0},{32,48},{48,32},{64,80},{80,64},{96,112},{112,96},{1... | collective-permute-start | bytes 270344 | tf_op jit(solution)/shard_map/ppermute | solution.py:664
  39.8 2.0 %collective-permute-start.13 = (f32[11,16,128]{2,1,0:T(8,128)S(1)}, f32[11,16,128]{2,1,0:T(8,128)S(1)}, u32[]{:S(2)}, u32[]{:S(2)}) collective-permute-start(f32[11,16,128]{2,1,0:T(8,128)S(1)} %get-tuple-element.197), channel_id=1, source_target_pairs={{16,32},{32,16},{48,64},{64,48},{80,96},{96,80},{112,128},{128,112... | collective-permute-start | bytes 270344 | tf_op jit(solution)/shard_map/ppermute | solution.py:664
  41.8 1.7 %shard_map.211 = (f32[3,6,16,256]{3,2,1,0:T(8,128)S(1)}, f32[3,6,16,256]{3,2,1,0:T(8,128)S(1)}, f32[3,6,16,256]{3,2,1,0:T(8,128)S(1)}, f32[3,6,16,256]{3,2,1,0:T...) custom-call(f32[3,6,16,256]{3,2,1,0:T(8,128)S(1)} %get-tuple-element, ...), custom_call_target="tpu_custom_call" | custom-call | flops 4000000 | bytes 8000000 | tf_op jit(solution)/shard_map/pallas_call | solution.py:624
  43.5 2.2 %collective-permute-start.6 = (f32[11,16,128]{2,1,0:T(8,128)S(1)}, f32[11,16,128]{2,1,0:T(8,128)S(1)}, u32[]{:S(2)}, u32[]{:S(2)}) collective-permute-start(f32[11,16,128]{2,1,0:T(8,128)S(1)} %get-tuple-element.156), channel_id=1, source_target_pairs={{0,16},{16,0},{32,48},{48,32},{64,80},{80,64},{96,112},{112,96},{1... | collective-permute-start | bytes 270344 | tf_op jit(solution)/shard_map/ppermute | solution.py:664
  45.7 2.8 %collective-permute-start.7 = (f32[11,16,128]{2,1,0:T(8,128)S(1)}, f32[11,16,128]{2,1,0:T(8,128)S(1)}, u32[]{:S(2)}, u32[]{:S(2)}) collective-permute-start(f32[11,16,128]{2,1,0:T(8,128)S(1)} %get-tuple-element.157), channel_id=1, source_target_pairs={{16,32},{32,16},{48,64},{64,48},{80,96},{96,80},{112,128},{128,112... | collective-permute-start | bytes 270344 | tf_op jit(solution)/shard_map/ppermute | solution.py:664
  48.5 0.4 collective-permute-done.13.refs_12_
  48.9 1.9 %shard_map.215 = (f32[3,6,16,384]{3,2,1,0:T(8,128)}, f32[3,6,16,384]{3,2,1,0:T(8,128)}, f32[3,6,16,384]{3,2,1,0:T(8,128)}, f32[3,6,16,384]{3,2,1,0:T(8,128)}, f3...) custom-call(f32[3,6,16,256]{3,2,1,0:T(8,128)S(1)} %get-tuple-element, ...), custom_call_target="tpu_custom_call" | custom-call | flops 4000000 | bytes 8000000 | tf_op jit(solution)/shard_map/pallas_call | solution.py:624
  50.9 3.0 %collective-permute-done.7.refs_12_ = f32[11,16,128]{2,1,0:T(8,128)S(1)} collective-permute-done((f32[11,16,128]{2,1,0:T(8,128)S(1)}, f32[11,16,128]{2,1,0:T(8,128)S(1)}, u32[]{:S(2)}, u32[]{:S(2)}) %collective-permute-start.7) | collective-permute-done | bytes 90144 | tf_op jit(solution)/shard_map/ppermute | solution.py:664
  53.9 2.3 %shard_map.216 = (f32[3,6,16,384]{3,2,1,0:T(8,128)}, f32[3,6,16,384]{3,2,1,0:T(8,128)}, f32[3,6,16,384]{3,2,1,0:T(8,128)}, f32[3,6,16,384]{3,2,1,0:T(8,128)}, f3...) custom-call(f32[3,6,16,256]{3,2,1,0:T(8,128)S(1)} %get-tuple-element, ...), custom_call_target="tpu_custom_call", output_to_operand_aliasing={{0}: (13, {}), {1}: (14, {}), {2}: (15, {}), {3}: (16, {}),... | custom-call | flops 4000000 | bytes 8000000 | tf_op jit(solution)/shard_map/pallas_call | solution.py:624
  (22 shorter events, 0.1 us)
Async XLA Ops:
  2.5 3.3 %copy-start.3 = (f32[8]{0:T(128)S(1)}, f32[8]{0:T(128)}, u32[]{:S(2)}) copy-start(f32[8]{0:T(128)} %param.24) | copy-start | bytes 100
  2.5 3.2 %copy-start.4 = (f32[8]{0:T(128)S(1)}, f32[8]{0:T(128)}, u32[]{:S(2)}) copy-start(f32[8]{0:T(128)} %param.23) | copy-start | bytes 100
  2.5 3.2 %copy-start = (f32[8]{0:T(128)S(1)}, f32[8]{0:T(128)}, u32[]{:S(2)}) copy-start(f32[8]{0:T(128)} %param.25) | copy-start | bytes 100
  2.5 3.2 %copy-start.1 = (f32[8]{0:T(128)S(1)}, f32[8]{0:T(128)}, u32[]{:S(2)}) copy-start(f32[8]{0:T(128)} %param.27) | copy-start | bytes 100
  2.5 3.2 %copy-start.2 = (f32[8]{0:T(128)S(1)}, f32[8]{0:T(128)}, u32[]{:S(2)}) copy-start(f32[8]{0:T(128)} %param.26) | copy-start | bytes 100
  2.5 5.3 %collective-permute-start = (f32[8,16,128]{2,1,0:T(8,128)S(1)}, f32[8,16,128]{2,1,0:T(8,128)S(1)}, u32[]{:S(2)}, u32[]{:S(2)}) collective-permute-start(f32[8,16,128]{2,1,0:T(8,128)S(1)} %get-tuple-element.123), channel_id=1, source_target_pairs={{0,1},{1,0},{2,3},{3,2},{4,5},{5,4},{6,7},{7,6},{8,9},{9,8},{10,11... | collective-permute-start | bytes 196616 | tf_op jit(solution)/shard_map/ppermute | solution.py:664
  2.6 3.1 %copy-start.5 = (f32[8]{0:T(128)S(1)}, f32[8]{0:T(128)}, u32[]{:S(2)}) copy-start(f32[8]{0:T(128)} %param.22) | copy-start | bytes 100
  2.7 5.9 %collective-permute-start.1 = (f32[8,16,128]{2,1,0:T(8,128)S(1)}, f32[8,16,128]{2,1,0:T(8,128)S(1)}, u32[]{:S(2)}, u32[]{:S(2)}) collective-permute-start(f32[8,16,128]{2,1,0:T(8,128)S(1)} %get-tuple-element.124), channel_id=1, source_target_pairs={{1,2},{2,1},{3,4},{4,3},{5,6},{6,5},{7,8},{8,7},{9,10},{10,9},{11,... | collective-permute-start | bytes 196616 | tf_op jit(solution)/shard_map/ppermute | solution.py:664
  9.9 14.4 %collective-permute-start.8 = (f32[13,16,128]{2,1,0:T(8,128)S(1)}, f32[13,16,128]{2,1,0:T(8,128)S(1)}, u32[]{:S(2)}, u32[]{:S(2)}) collective-permute-start(f32[13,16,128]{2,1,0:T(8,128)S(1)} %get-tuple-element.175), channel_id=1, source_target_pairs={{0,16},{16,0},{32,48},{48,32},{64,80},{80,64},{96,112},{112,96},{1... | collective-permute-start | bytes 319496 | tf_op jit(solution)/shard_map/ppermute | solution.py:664
  12.1 12.2 %collective-permute-start.9 = (f32[13,16,128]{2,1,0:T(8,128)S(1)}, f32[13,16,128]{2,1,0:T(8,128)S(1)}, u32[]{:S(2)}, u32[]{:S(2)}) collective-permute-start(f32[13,16,128]{2,1,0:T(8,128)S(1)} %get-tuple-element.176), channel_id=1, source_target_pairs={{16,32},{32,16},{48,64},{64,48},{80,96},{96,80},{112,128},{128,112... | collective-permute-start | bytes 319496 | tf_op jit(solution)/shard_map/ppermute | solution.py:664
  20.2 10.7 %collective-permute-start.2 = (f32[13,16,128]{2,1,0:T(8,128)S(1)}, f32[13,16,128]{2,1,0:T(8,128)S(1)}, u32[]{:S(2)}, u32[]{:S(2)}) collective-permute-start(f32[13,16,128]{2,1,0:T(8,128)S(1)} %get-tuple-element.135), channel_id=1, source_target_pairs={{0,16},{16,0},{32,48},{48,32},{64,80},{80,64},{96,112},{112,96},{1... | collective-permute-start | bytes 319496 | tf_op jit(solution)/shard_map/ppermute | solution.py:664
  20.3 10.6 %collective-permute-start.3 = (f32[13,16,128]{2,1,0:T(8,128)S(1)}, f32[13,16,128]{2,1,0:T(8,128)S(1)}, u32[]{:S(2)}, u32[]{:S(2)}) collective-permute-start(f32[13,16,128]{2,1,0:T(8,128)S(1)} %get-tuple-element.136), channel_id=1, source_target_pairs={{16,32},{32,16},{48,64},{64,48},{80,96},{96,80},{112,128},{128,112... | collective-permute-start | bytes 319496 | tf_op jit(solution)/shard_map/ppermute | solution.py:664
  26.1 9.9 %collective-permute-start.10 = (f32[11,16,128]{2,1,0:T(8,128)S(1)}, f32[11,16,128]{2,1,0:T(8,128)S(1)}, u32[]{:S(2)}, u32[]{:S(2)}) collective-permute-start(f32[11,16,128]{2,1,0:T(8,128)S(1)} %get-tuple-element.186), channel_id=1, source_target_pairs={{0,16},{16,0},{32,48},{48,32},{64,80},{80,64},{96,112},{112,96},{1... | collective-permute-start | bytes 270344 | tf_op jit(solution)/shard_map/ppermute | solution.py:664
  26.2 9.8 %collective-permute-start.11 = (f32[11,16,128]{2,1,0:T(8,128)S(1)}, f32[11,16,128]{2,1,0:T(8,128)S(1)}, u32[]{:S(2)}, u32[]{:S(2)}) collective-permute-start(f32[11,16,128]{2,1,0:T(8,128)S(1)} %get-tuple-element.187), channel_id=1, source_target_pairs={{16,32},{32,16},{48,64},{64,48},{80,96},{96,80},{112,128},{128,112... | collective-permute-start | bytes 270344 | tf_op jit(solution)/shard_map/ppermute | solution.py:664
  32.7 9.2 %collective-permute-start.4 = (f32[11,16,128]{2,1,0:T(8,128)S(1)}, f32[11,16,128]{2,1,0:T(8,128)S(1)}, u32[]{:S(2)}, u32[]{:S(2)}) collective-permute-start(f32[11,16,128]{2,1,0:T(8,128)S(1)} %get-tuple-element.146), channel_id=1, source_target_pairs={{0,16},{16,0},{32,48},{48,32},{64,80},{80,64},{96,112},{112,96},{1... | collective-permute-start | bytes 270344 | tf_op jit(solution)/shard_map/ppermute | solution.py:664
  32.8 9.0 %collective-permute-start.5 = (f32[11,16,128]{2,1,0:T(8,128)S(1)}, f32[11,16,128]{2,1,0:T(8,128)S(1)}, u32[]{:S(2)}, u32[]{:S(2)}) collective-permute-start(f32[11,16,128]{2,1,0:T(8,128)S(1)} %get-tuple-element.147), channel_id=1, source_target_pairs={{16,32},{32,16},{48,64},{64,48},{80,96},{96,80},{112,128},{128,112... | collective-permute-start | bytes 270344 | tf_op jit(solution)/shard_map/ppermute | solution.py:664
  37.6 10.9 %collective-permute-start.12 = (f32[11,16,128]{2,1,0:T(8,128)S(1)}, f32[11,16,128]{2,1,0:T(8,128)S(1)}, u32[]{:S(2)}, u32[]{:S(2)}) collective-permute-start(f32[11,16,128]{2,1,0:T(8,128)S(1)} %get-tuple-element.196), channel_id=1, source_target_pairs={{0,16},{16,0},{32,48},{48,32},{64,80},{80,64},{96,112},{112,96},{1... | collective-permute-start | bytes 270344 | tf_op jit(solution)/shard_map/ppermute | solution.py:664
  39.8 9.1 %collective-permute-start.13 = (f32[11,16,128]{2,1,0:T(8,128)S(1)}, f32[11,16,128]{2,1,0:T(8,128)S(1)}, u32[]{:S(2)}, u32[]{:S(2)}) collective-permute-start(f32[11,16,128]{2,1,0:T(8,128)S(1)} %get-tuple-element.197), channel_id=1, source_target_pairs={{16,32},{32,16},{48,64},{64,48},{80,96},{96,80},{112,128},{128,112... | collective-permute-start | bytes 270344 | tf_op jit(solution)/shard_map/ppermute | solution.py:664
  43.5 7.4 %collective-permute-start.6 = (f32[11,16,128]{2,1,0:T(8,128)S(1)}, f32[11,16,128]{2,1,0:T(8,128)S(1)}, u32[]{:S(2)}, u32[]{:S(2)}) collective-permute-start(f32[11,16,128]{2,1,0:T(8,128)S(1)} %get-tuple-element.156), channel_id=1, source_target_pairs={{0,16},{16,0},{32,48},{48,32},{64,80},{80,64},{96,112},{112,96},{1... | collective-permute-start | bytes 270344 | tf_op jit(solution)/shard_map/ppermute | solution.py:664
  45.7 8.1 %collective-permute-start.7 = (f32[11,16,128]{2,1,0:T(8,128)S(1)}, f32[11,16,128]{2,1,0:T(8,128)S(1)}, u32[]{:S(2)}, u32[]{:S(2)}) collective-permute-start(f32[11,16,128]{2,1,0:T(8,128)S(1)} %get-tuple-element.157), channel_id=1, source_target_pairs={{16,32},{32,16},{48,64},{64,48},{80,96},{96,80},{112,128},{128,112... | collective-permute-start | bytes 270344 | tf_op jit(solution)/shard_map/ppermute | solution.py:664
